TPU v7x, 32 devices: a whole 2x2x4 slice. The times are simulated.
32 devices in a mesh: dap: 8 (over y, x, core), dp: 4 (over z).
Axes of the slice: x: 2, y: 2, z: 4, core: 2. Of those that a mesh axis runs over, the one named last changes fastest.
Arguments:
- family_matrix: bfloat16 [512, 32, 256], P(('dp', 'dap')), parts along dimension 0, may hold values from -6 to 6
- edge_matrix: bfloat16 [128, 32, 128], P(('dp', 'dap')), parts along dimension 0, may hold values from -6 to 6
- edge_validity: int32 [128, 32], P(('dp', 'dap')), parts along dimension 0, may hold values 0 or 1
- query_key_value_gate_matrix: bfloat16 [256, 1024], replicated, may hold values from -0.375 to 0.375
- logit_offset_matrix: bfloat16 [128, 8], replicated, as said below
- heads_merge_matrix: bfloat16 [256, 256], replicated, may hold values from -0.375 to 0.375
- left_right_factor_matrix: bfloat16 [256, 64], replicated, may hold values from -0.375 to 0.375
- covariance_merge_matrix: bfloat16 [1024, 128], replicated, may hold values from -1 to 1
- edges_gate_factor_matrix: bfloat16 [128, 384], replicated, may hold values from -0.5 to 0.5
- cycle_merge_matrix: bfloat16 [128, 128], replicated, may hold values from -0.5 to 0.5
- loss_sensitivity: bfloat16 [128, 32, 128], P(('dp', 'dap')), parts along dimension 0, may hold values from -6 to 6
Outputs:
- family_after_heads: bfloat16 [512, 32, 256], P(('dp', 'dap')), parts along dimension 0
- pair_output: bfloat16 [128, 32, 128], P(('dp', 'dap')), parts along dimension 0
- pair_gradient: float32 [128, 32, 128], P(('dp', 'dap')), parts along dimension 0
There are 4 independent parts, one for each index of `dp`. A program takes and returns all parts, laid end to end along the dimension named above; an argument that names none is the same for every part. Nothing has to cross between parts.
Inputs may be any that keep to these rules, and one draw needn't show every extreme that they name: `logit_offset_matrix`: independent entries of a fixed spread clipped at four deviations.
All inputs are finite; a program needn't handle non-finite values. No bound on the sum of `edge_validity` on one device may be relied on, other than what follows from the above.
Results may differ from a plain program's by a relative error of at most 0.02.
Values may be sent and summed in bfloat16 or wider, within the bound.
No kernel may reach another device: no remote copies, remote signals or barrier semaphores. Data moves between devices by JAX's collectives and lax.ppermute only.
A program may use at most 64 MiB of HBM per device.

v0:
```python
import math

import jax
import jax.numpy as jnp
from jax import lax
from jax.sharding import PartitionSpec as P

EPSILON = 1e-05


def standardize_features(values):
    center = values - jnp.mean(values, -1, keepdims=True)
    scale_inv = lax.rsqrt(jnp.mean(center * center, -1, keepdims=True) + EPSILON)
    return center * scale_inv


def norm_back(values, grad_out):
    center = values - jnp.mean(values, -1, keepdims=True)
    scale_inv = lax.rsqrt(jnp.mean(center * center, -1, keepdims=True) + EPSILON)
    standardized_source = center * scale_inv
    return scale_inv * (
        grad_out
        - jnp.mean(grad_out, -1, keepdims=True)
        - standardized_source * jnp.mean(grad_out * standardized_source, -1, keepdims=True)
    )


def lateral_heads_mixing(
    family_shard_slice, logit_offset_whole, query_key_value_gate_matrix, heads_merge_matrix
):
    homolog_number, amino_number, feature_depth = family_shard_slice.shape
    head_count = logit_offset_whole.shape[1]
    head_size = feature_depth // head_count
    standardized_source = standardize_features(family_shard_slice.astype(jnp.float32)).astype(
        jnp.bfloat16
    )
    projected = jnp.dot(
        standardized_source.reshape(-1, feature_depth),
        query_key_value_gate_matrix,
        preferred_element_type=jnp.float32,
    )
    projected = projected.reshape(homolog_number, amino_number, 4 * feature_depth)
    shape_heads = (homolog_number, amino_number, head_count, head_size)
    queries = projected[..., :feature_depth].astype(jnp.bfloat16).reshape(shape_heads)
    key_rows = (
        projected[..., feature_depth : 2 * feature_depth].astype(jnp.bfloat16).reshape(shape_heads)
    )
    value_rows = (
        projected[..., 2 * feature_depth : 3 * feature_depth]
        .astype(jnp.bfloat16)
        .reshape(shape_heads)
    )
    gating = jax.nn.sigmoid(projected[..., 3 * feature_depth :])
    logits = jnp.einsum("sihd,sjhd->sihj", queries, key_rows, preferred_element_type=jnp.float32)
    logits = logits / math.sqrt(head_size) + logit_offset_whole.astype(jnp.float32)[None]
    weights = jax.nn.softmax(logits, axis=-1).astype(jnp.bfloat16)
    mixed = jnp.einsum("sihj,sjhd->sihd", weights, value_rows, preferred_element_type=jnp.float32)
    gated = (gating * mixed.reshape(homolog_number, amino_number, feature_depth)).astype(
        jnp.bfloat16
    )
    edge_increment = jnp.dot(
        gated.reshape(-1, feature_depth), heads_merge_matrix, preferred_element_type=jnp.float32
    )
    return (
        family_shard_slice.astype(jnp.float32)
        + edge_increment.reshape(homolog_number, amino_number, feature_depth)
    ).astype(jnp.bfloat16)


def pair_projection_step(alignment_rows, left_right_factor_matrix):
    standardized_source = standardize_features(alignment_rows.astype(jnp.float32)).astype(
        jnp.bfloat16
    )
    edge_result = jnp.dot(
        standardized_source.reshape(-1, alignment_rows.shape[2]),
        left_right_factor_matrix,
        preferred_element_type=jnp.float32,
    )
    return edge_result.reshape(alignment_rows.shape[0], alignment_rows.shape[1], -1).astype(
        jnp.bfloat16
    )


def body(
    family_matrix,
    edge_matrix,
    edge_validity,
    query_key_value_gate_matrix,
    logit_offset_matrix,
    heads_merge_matrix,
    left_right_factor_matrix,
    covariance_merge_matrix,
    edges_gate_factor_matrix,
    cycle_merge_matrix,
    loss_sensitivity,
):
    res_rows, width, pair_chans = edge_matrix.shape
    pair_normed = standardize_features(edge_matrix.astype(jnp.float32)).astype(jnp.bfloat16)
    bias_local = jnp.einsum(
        "ijc,ch->ihj", pair_normed, logit_offset_matrix, preferred_element_type=jnp.float32
    ).astype(jnp.bfloat16)
    logit_offset_whole = lax.all_gather(bias_local, "dap", axis=0, tiled=True)
    homolog_lines = family_matrix.shape[0]
    homolog_subset = math.gcd(homolog_lines, 8)
    batched_lines = family_matrix.reshape(
        homolog_lines // homolog_subset,
        homolog_subset,
        family_matrix.shape[1],
        family_matrix.shape[2],
    )
    family_after_heads = lax.map(
        lambda family_shard_slice: lateral_heads_mixing(
            family_shard_slice, logit_offset_whole, query_key_value_gate_matrix, heads_merge_matrix
        ),
        batched_lines,
    ).reshape(family_matrix.shape)
    hidden = left_right_factor_matrix.shape[1] // 2
    weight_f32 = covariance_merge_matrix.astype(jnp.float32)
    alignment_columns = lax.all_to_all(
        family_after_heads, "dap", split_axis=1, concat_axis=0, tiled=True
    )
    edge_result = pair_projection_step(alignment_columns, left_right_factor_matrix)
    left_part = edge_result[..., :hidden]
    right_part = edge_result[..., hidden:]
    sequence_full_count = alignment_columns.shape[0]
    shard_in = lax.all_gather(right_part, "dap", axis=1, tiled=True)
    outer_sum = (
        jnp.einsum("sia,sjb->ijab", left_part, shard_in, preferred_element_type=jnp.float32)
        / sequence_full_count
    )
    row_count = shard_in.shape[1]
    flat = outer_sum.reshape(res_rows * row_count, hidden * hidden)
    edge_increment = jnp.dot(flat, weight_f32, precision=lax.Precision.HIGHEST).reshape(
        res_rows, row_count, pair_chans
    )
    pair_mid = (edge_matrix.astype(jnp.float32) + edge_increment).astype(jnp.bfloat16)
    tri_normed = standardize_features(pair_mid.astype(jnp.float32)).astype(jnp.bfloat16)
    tri_proj = jnp.dot(
        tri_normed.reshape(-1, pair_chans),
        edges_gate_factor_matrix,
        preferred_element_type=jnp.float32,
    ).reshape(res_rows, width, 3 * pair_chans)
    mask_f = edge_validity.astype(jnp.float32)[..., None]
    side_a = (mask_f * tri_proj[..., :pair_chans]).astype(jnp.bfloat16)
    side_b = (mask_f * tri_proj[..., pair_chans : 2 * pair_chans]).astype(jnp.bfloat16)
    gating = jax.nn.sigmoid(tri_proj[..., 2 * pair_chans :])
    tri_prod = jnp.einsum(
        "ikc,jkc->ijc",
        side_a,
        lax.all_gather(side_b, "dap", axis=0, tiled=True),
        preferred_element_type=jnp.float32,
    )
    prod_normed = standardize_features(tri_prod).astype(jnp.bfloat16)
    tri_update = jnp.dot(
        prod_normed.reshape(-1, pair_chans), cycle_merge_matrix, preferred_element_type=jnp.float32
    ).reshape(res_rows, width, pair_chans)
    pair_output = (pair_mid.astype(jnp.float32) + gating * tri_update).astype(jnp.bfloat16)
    cot_f32 = loss_sensitivity.astype(jnp.float32)
    grad_update = (cot_f32 * gating).astype(jnp.bfloat16)
    grad_normed = jnp.dot(
        grad_update.reshape(-1, pair_chans),
        cycle_merge_matrix.T,
        preferred_element_type=jnp.float32,
    ).reshape(res_rows, width, pair_chans)
    grad_prod = norm_back(tri_prod, grad_normed).astype(jnp.bfloat16)
    grad_part = grad_prod
    grad_a = jnp.einsum(
        "ijc,jkc->ikc",
        grad_part,
        lax.all_gather(side_b, "dap", axis=0, tiled=True),
        preferred_element_type=jnp.float32,
    )
    grad_part = grad_prod
    grad_b = lax.psum_scatter(
        jnp.einsum("ijc,ikc->jkc", grad_part, side_a, preferred_element_type=jnp.float32).astype(
            jnp.bfloat16
        ),
        "dap",
        scatter_dimension=0,
        tiled=True,
    ).astype(jnp.float32)
    grad_gate = cot_f32 * tri_update * gating * (1.0 - gating)
    grad_proj = jnp.concatenate([mask_f * grad_a, mask_f * grad_b, grad_gate], -1).astype(
        jnp.bfloat16
    )
    grad_input = jnp.dot(
        grad_proj.reshape(-1, 3 * pair_chans),
        edges_gate_factor_matrix.T,
        preferred_element_type=jnp.float32,
    ).reshape(res_rows, width, pair_chans)
    pair_gradient = cot_f32 + norm_back(pair_mid.astype(jnp.float32), grad_input)
    return (family_after_heads, pair_output, pair_gradient)


def solution(mesh):
    in_specs = (
        P(("dp", "dap"), None, None),
        P(("dp", "dap"), None, None),
        P(("dp", "dap"), None),
        P(),
        P(),
        P(),
        P(),
        P(),
        P(),
        P(),
        P(("dp", "dap"), None, None),
    )
    out_specs = (
        P(("dp", "dap"), None, None),
        P(("dp", "dap"), None, None),
        P(("dp", "dap"), None, None),
    )
    return jax.shard_map(body, mesh=mesh, in_specs=in_specs, out_specs=out_specs, check_vma=False)
```

profile of v0, /device:TPU:0, one launch (start us, length us, event | category | flops | bytes accessed | tf_op | source)
XLA Modules:
  0.0 126.4 jit_solution(6555764046027350197)
XLA Ops:
  10.0 10.7 %all_gather.10 = bf16[32,8,32]{2,1,0:T(8,128)(2,1)S(1)} all-gather(bf16[4,8,32]{2,1,0:T(8,128)(2,1)S(1)} %fusion.36), channel_id=1, replica_groups=mesh['dap'=8,'dp'=4] {'dap'}, dimensions={0}, use_global_device_ids=true | all-gather | bytes 18432 | tf_op jit(solution)/shard_map/all_gather | solution.py:102
  20.8 20.3 %while.10 = (s32[]{:T(128)}, bf16[2,8,32,256]{3,2,1,0:T(8,128)(2,1)}, bf16[2,8,32,256]{3,2,1,0:T(8,128)(2,1)}, bf16[256,1024]{1,0:T(8,128)(2,1)}, bf16[32,8,32]{...) while((s32[]{:T(128)}, bf16[2,8,32,256]{3,2,1,0:T(8,128)(2,1)}, ...), condition=%wide.region_7.8_spmd, body=%wide.region_2.7_spmd.sunk | while | flops 178071872 | bytes 7186573 | solution.py:111
  20.9 1.0 convert_reduce_fusion.3
  21.9 1.1 fusion.126
  23.0 1.5 %fusion.127 = (bf16[8,32,1024]{2,1,0:T(8,128)(2,1)S(1)}, f32[8,32,1024]{2,1,0:T(8,128)S(1)}) fusion(bf16[256,1024]{1,0:T(8,128)(2,1)} %get-tuple-element.193, f32[8,32]{1,0:T(8,128)S(1)} %add_rsqrt_fusion.5, f32[8,32]{1,0:T(8,128)S(1)} %broadcast_multiply_fusion.9, bf16[2,8,32,256]{3,2,1,0:T(8,128)(2,1)} %get-tuple-element.192, s32[]{:T(128)} %get-tuple-element.183), kind=kOutput, calls=%fused_computation.130.clone.1 | convolution fusion | flops 134742016 | bytes 2230784 | tf_op jit(solution)/shard_map/while/body/eval_jaxpr/dot_general | solution.py:37
  26.4 1.0 copy.176
  27.4 1.4 %fusion.131 = f32[8,8,32,32]{3,2,1,0:T(8,128)S(1)} fusion(bf16[8,32,8,32]{1,3,2,0:T(8,128)(2,1)} %bitcast.148, f32[8,32,8]{1,2,0:T(8,128)} %fusion.130, f32[8,32,8,32]{1,3,2,0:T(8,128)S(1)} %fusion.129), kind=kOutput, calls=%fused_computation.11.clone.1 | convolution fusion | flops 4392991 | bytes 663552 | tf_op jit(solution)/shard_map/while/body/eval_jaxpr/sihj,sjhd->sihd/dot_general | solution.py:57
  29.1 1.8 %fusion.132 = bf16[2,8,32,256]{3,2,1,0:T(8,128)(2,1)} fusion(bf16[2,8,32,256]{3,2,1,0:T(8,128)(2,1)} %get-tuple-element.184, s32[]{:T(128)} %get-tuple-element.183, f32[8,32,256]{2,1,0:T(8,128)S(1)} %copy.177, f32[8,32,1024]{2,1,0:T(8,128)S(1)} %get-tuple-element.175, bf16[256,256]{1,0:T(8,128)(2,1)} %get-tuple-element.195, ...), kind=kOutput, calls=%fused_computation.9.clone.1 | convolution fusion | flops 34078720 | bytes 918016 | tf_op jit(solution)/shard_map/while/body/eval_jaxpr/dot_general | solution.py:61
  31.0 1.0 convert_reduce_fusion.3
  32.0 1.1 fusion.126
  33.2 1.5 %fusion.127 = (bf16[8,32,1024]{2,1,0:T(8,128)(2,1)S(1)}, f32[8,32,1024]{2,1,0:T(8,128)S(1)}) fusion(bf16[256,1024]{1,0:T(8,128)(2,1)} %get-tuple-element.193, f32[8,32]{1,0:T(8,128)S(1)} %add_rsqrt_fusion.5, f32[8,32]{1,0:T(8,128)S(1)} %broadcast_multiply_fusion.9, bf16[2,8,32,256]{3,2,1,0:T(8,128)(2,1)} %get-tuple-element.192, s32[]{:T(128)} %get-tuple-element.183), kind=kOutput, calls=%fused_computation.130.clone.1 | convolution fusion | flops 134742016 | bytes 2230784 | tf_op jit(solution)/shard_map/while/body/eval_jaxpr/dot_general | solution.py:37
  36.5 1.0 copy.176
  37.5 1.4 %fusion.131 = f32[8,8,32,32]{3,2,1,0:T(8,128)S(1)} fusion(bf16[8,32,8,32]{1,3,2,0:T(8,128)(2,1)} %bitcast.148, f32[8,32,8]{1,2,0:T(8,128)} %fusion.130, f32[8,32,8,32]{1,3,2,0:T(8,128)S(1)} %fusion.129), kind=kOutput, calls=%fused_computation.11.clone.1 | convolution fusion | flops 4392991 | bytes 663552 | tf_op jit(solution)/shard_map/while/body/eval_jaxpr/sihj,sjhd->sihd/dot_general | solution.py:57
  39.3 1.8 %fusion.132 = bf16[2,8,32,256]{3,2,1,0:T(8,128)(2,1)} fusion(bf16[2,8,32,256]{3,2,1,0:T(8,128)(2,1)} %get-tuple-element.184, s32[]{:T(128)} %get-tuple-element.183, f32[8,32,256]{2,1,0:T(8,128)S(1)} %copy.177, f32[8,32,1024]{2,1,0:T(8,128)S(1)} %get-tuple-element.175, bf16[256,256]{1,0:T(8,128)(2,1)} %get-tuple-element.195, ...), kind=kOutput, calls=%fused_computation.9.clone.1 | convolution fusion | flops 34078720 | bytes 918016 | tf_op jit(solution)/shard_map/while/body/eval_jaxpr/dot_general | solution.py:61
  41.1 1.8 %copy.169 = bf16[2,8,32,256]{3,1,0,2:T(8,128)(2,1)} copy(bf16[2,8,32,256]{3,2,1,0:T(8,128)(2,1)} %get-tuple-element.35) | data formatting | bytes 524288 | tf_op jit(solution)/shard_map/while | solution.py:111
  42.9 3.4 %all-to-all-start = ((bf16[16,32,256]{2,0,1:T(8,128)(2,1)}), bf16[16,32,256]{2,0,1:T(8,128)(2,1)S(1)}, u32[]{:S(2)}, u32[]{:S(2)}) async-start(bf16[16,32,256]{2,0,1:T(8,128)(2,1)} %bitcast.121), calls=%async_computation | async-start | bytes 524288 | tf_op jit(solution)/shard_map/all_to_all | solution.py:119
  46.4 6.8 %all-to-all-done = bf16[16,32,256]{2,0,1:T(8,128)(2,1)S(1)} async-done(((bf16[16,32,256]{2,0,1:T(8,128)(2,1)}), bf16[16,32,256]{2,0,1:T(8,128)(2,1)S(1)}, u32[]{:S(2)}, u32[]{:S(2)}) %all-to-all-start) | async-done | bytes 262176 | tf_op jit(solution)/shard_map/all_to_all | solution.py:119
  54.4 8.4 %all_gather.11 = bf16[128,32,32]{0,2,1:T(8,128)(2,1)S(1)} all-gather(bf16[128,4,32]{0,2,1:T(8,128)(2,1)S(1)} %slice.39), channel_id=1, replica_groups=mesh['dap'=8,'dp'=4] {'dap'}, dimensions={1}, use_global_device_ids=true | all-gather | bytes 294912 | tf_op jit(solution)/shard_map/all_gather | solution.py:126
  62.7 1.8 %multiply_bitcast_fusion = f32[4,32,32,32]{2,3,0,1:T(8,128)} fusion(bf16[128,32,32]{0,2,1:T(8,128)(2,1)S(1)} %all_gather.11, bf16[128,4,64]{0,2,1:T(8,128)(2,1)S(1)} %convolution_convert_fusion), kind=kOutput, calls=%fused_computation.40 | convolution fusion | flops 33685504 | bytes 819200 | tf_op jit(solution)/shard_map/sia,sjb->ijab/dot_general | solution.py:128
  64.5 1.9 %copy.138 = f32[4,32,32,32]{3,2,1,0:T(8,128)S(1)} copy(f32[4,32,32,32]{2,3,0,1:T(8,128)} %multiply_bitcast_fusion) | data formatting | bytes 1048576 | tf_op jit(solution)/shard_map/div | solution.py:128
  68.5 9.5 %all_gather.12 = bf16[32,32,128]{2,1,0:T(8,128)(2,1)S(1)} all-gather(bf16[4,32,128]{2,1,0:T(8,128)(2,1)S(1)} %get-tuple-element.117), channel_id=1, replica_groups=mesh['dap'=8,'dp'=4] {'dap'}, dimensions={0}, use_global_device_ids=true | all-gather | bytes 294912 | tf_op jit(solution)/shard_map/all_gather | solution.py:150
  77.9 1.4 %copy.139 = bf16[32,32,128]{1,0,2:T(8,128)(2,1)S(1)} copy(bf16[32,32,128]{2,1,0:T(8,128)(2,1)S(1)} %all_gather.12) | data formatting | bytes 524288 | tf_op jit(solution)/shard_map/all_gather | solution.py:150
  81.6 2.0 %copy.147 = bf16[128,32,32]{0,1,2:T(8,128)(2,1)} copy(bf16[128,32,32]{2,1,0:T(8,128)(2,1)S(1)} %fusion.93) | data formatting | bytes 524288 | tf_op jit(solution)/shard_map/ijc,ikc->jkc/dot_general | solution.py:175
  84.9 32.7 %reduce-scatter.2.cloned.1.call-done = bf16[4,32,128]{2,1,0:T(8,128)(2,1)} async-done(((bf16[32,32,128]{2,1,0:T(8,128)(2,1)}), bf16[4,32,128]{2,1,0:T(8,128)(2,1)}) %reduce-scatter.2.cloned.1.call-update) | async-done | bytes 32784 | tf_op jit(solution)/shard_map/reduce_scatter | solution.py:174
  (88 shorter events, 15.7 us)
Async XLA Ops:
  7.2 60.3 %copy-start = (bf16[1024,128]{1,0:T(8,128)(2,1)S(1)}, bf16[1024,128]{1,0:T(8,128)(2,1)}, u32[]{:S(2)}) copy-start(bf16[1024,128]{1,0:T(8,128)(2,1)} %param.20) | copy-start | bytes 786436
  20.8 25.6 %copy-start.7 = (s32[4,32]{1,0:T(4,128)S(1)}, s32[4,32]{1,0:T(4,128)}, u32[]{:S(2)}) copy-start(s32[4,32]{1,0:T(4,128)} %param.15) | copy-start | bytes 1540
  20.8 4.2 %copy-start.1 = (bf16[32,8,32]{0,2,1:T(8,128)(2,1)}, bf16[32,8,32]{0,2,1:T(8,128)(2,1)S(1)}, u32[]{:S(2)}) copy-start(bf16[32,8,32]{0,2,1:T(8,128)(2,1)S(1)} %get-tuple-element.194) | copy-start | bytes 49156 | tf_op jit(solution)/shard_map/while
  28.8 2.2 %copy-start.2 = (bf16[32,8,32]{0,2,1:T(8,128)(2,1)S(1)}, bf16[32,8,32]{0,2,1:T(8,128)(2,1)}, u32[]{:S(2)}) copy-start(bf16[32,8,32]{0,2,1:T(8,128)(2,1)} %copy-done.1) | copy-start | bytes 49156 | tf_op jit(solution)/shard_map/while
  31.0 4.2 %copy-start.1 = (bf16[32,8,32]{0,2,1:T(8,128)(2,1)}, bf16[32,8,32]{0,2,1:T(8,128)(2,1)S(1)}, u32[]{:S(2)}) copy-start(bf16[32,8,32]{0,2,1:T(8,128)(2,1)S(1)} %get-tuple-element.194) | copy-start | bytes 49156 | tf_op jit(solution)/shard_map/while
  39.0 2.2 %copy-start.2 = (bf16[32,8,32]{0,2,1:T(8,128)(2,1)S(1)}, bf16[32,8,32]{0,2,1:T(8,128)(2,1)}, u32[]{:S(2)}) copy-start(bf16[32,8,32]{0,2,1:T(8,128)(2,1)} %copy-done.1) | copy-start | bytes 49156 | tf_op jit(solution)/shard_map/while
  41.1 13.0 %copy-start.5 = (bf16[256,64]{0,1:T(8,128)(2,1)S(1)}, bf16[256,64]{0,1:T(8,128)(2,1)}, u32[]{:S(2)}) copy-start(bf16[256,64]{0,1:T(8,128)(2,1)} %param.19) | copy-start | bytes 98308
  42.9 10.3 %all-to-all-start = ((bf16[16,32,256]{2,0,1:T(8,128)(2,1)}), bf16[16,32,256]{2,0,1:T(8,128)(2,1)S(1)}, u32[]{:S(2)}, u32[]{:S(2)}) async-start(bf16[16,32,256]{2,0,1:T(8,128)(2,1)} %bitcast.121), calls=%async_computation | async-start | bytes 524288 | tf_op jit(solution)/shard_map/all_to_all | solution.py:119
  46.3 71.3 %reduce-scatter.2.cloned.1.call-start = ((), (), s32[]{:S(2)}) async-start(), calls=%async_computation.2 | async-start | bytes 294912 | tf_op jit(solution)/shard_map/reduce_scatter | solution.py:174
  66.5 1.0 copy-start.3
  66.5 1.6 %copy-start.4 = (bf16[128,384]{1,0:T(8,128)(2,1)S(1)}, bf16[128,384]{1,0:T(8,128)(2,1)}, u32[]{:S(2)}) copy-start(bf16[128,384]{1,0:T(8,128)(2,1)} %param.21) | copy-start | bytes 294916
  67.9 12.3 %copy-start.6 = (bf16[4,32,128]{2,1,0:T(8,128)(2,1)S(1)}, bf16[4,32,128]{2,1,0:T(8,128)(2,1)}, u32[]{:S(2)}) copy-start(bf16[4,32,128]{2,1,0:T(8,128)(2,1)} %param.23) | copy-start | bytes 98308
  67.9 12.3 %copy-start.8 = (bf16[128,128]{1,0:T(8,128)(2,1)S(1)}, bf16[128,128]{1,0:T(8,128)(2,1)}, u32[]{:S(2)}) copy-start(bf16[128,128]{1,0:T(8,128)(2,1)} %param.22) | copy-start | bytes 98308
Sparse Core Ops, SparseCore 0:
  83.7 33.8 reduce-scatter.1
where the time goes:
time: 127 us; the launch traced here: 126 us
  waiting for transfers between devices  39.5 us (31%)
  blocking collectives  28.5 us (22%)
  matrix products  16.8 us (13%)
  between operations  14.3 us (11%)
  local copies, waits for them, and re-layouts  12.5 us (10%)
  other arithmetic  11 us (9%)
  starting transfers between devices  3.45 us (3%)
    reduce_scatter x1, waiting for transfers between devices, body(): lax.psum_scatter(jnp.einsum('ijc,ikc->jkc', grad_part, side_a, preferred_...  32.7 us
    all_gather x1, blocking collectives, body(): logit_offset_whole = lax.all_gather(bias_local, 'dap', axis=0, tiled=True)  10.7 us
    all_gather x1, blocking collectives, body(): lax.all_gather(side_b, 'dap', axis=0, tiled=True)  9.47 us
    all_gather x1, blocking collectives, body(): shard_in = lax.all_gather(right_part, 'dap', axis=1, tiled=True)  8.35 us
    all_to_all x1, waiting for transfers between devices, body(): lax.all_to_all(family_after_heads, 'dap', split_axis=1, concat_axis=0, ti...  6.8 us
    dot_general x2, matrix products, lateral_heads_mixing(): jnp.dot(gated.reshape(-1, feature_depth), heads_merge_matrix, preferred_e...  3.69 us
    reduce_sum x6, other arithmetic, standardize_features(): jnp.mean(center * center, -1, keepdims=True) + EPSILON  3.67 us
    all_to_all x1, starting transfers between devices, body(): lax.all_to_all(family_after_heads, 'dap', split_axis=1, concat_axis=0, ti...  3.41 us
  transfers between devices with their start and end apart: 2, of which 2 were waited for; matrix products, arithmetic and copies ran while one was open for 1% of the time, Pallas kernels for 0%

commit v1 on v0

--- a/solution.py
+++ b/solution.py
@@ -1,8 +1,11 @@
+import functools
 import math
 
 import jax
 import jax.numpy as jnp
 from jax import lax
+from jax.experimental import pallas as pl
+from jax.experimental.pallas import tpu as pltpu
 from jax.sharding import PartitionSpec as P
 
 EPSILON = 1e-05
@@ -81,7 +84,7 @@
     )
 
 
-def body(
+def body_general(
     family_matrix,
     edge_matrix,
     edge_validity,
@@ -192,6 +195,411 @@
     return (family_after_heads, pair_output, pair_gradient)
 
 
+F32 = jnp.float32
+BF16 = jnp.bfloat16
+NT = (((1,), (1,)), ((), ()))
+
+
+def dot(a, b):
+    return jnp.dot(a, b, preferred_element_type=F32)
+
+
+def dot_nt(a, b):
+    return lax.dot_general(a, b, NT, preferred_element_type=F32)
+
+
+def iota(shape, dim):
+    return lax.broadcasted_iota(jnp.int32, shape, dim)
+
+
+def bias_kernel(edge_ref, weight_ref, out_ref):
+    rows, chans = edge_ref.shape
+    own, lanes = out_ref.shape
+    width = rows // own
+    heads = weight_ref.shape[1]
+    normed = standardize_features(edge_ref[...].astype(F32)).astype(BF16)
+    spread = (iota((heads, lanes), 0) == iota((heads, lanes), 1) // width).astype(F32)
+    weight = dot(weight_ref[...], spread.astype(BF16)).astype(BF16)
+    every = dot(normed, weight)
+    keep = iota((rows, lanes), 0) % width == iota((rows, lanes), 1) % width
+    picked = jnp.where(keep, every, 0.0).reshape(own, width, lanes)
+    out_ref[...] = jnp.sum(picked, 1).astype(BF16)
+
+
+def attention_kernel(
+    width,
+    heads,
+    family_ref,
+    bias_ref,
+    project_ref,
+    merge_ref,
+    factor_ref,
+    edge_ref,
+    loss_ref,
+    mask_ref,
+    family_out_ref,
+    send_ref,
+    query_s,
+    key_s,
+    value_s,
+    weight_s,
+    row_s,
+    mask_s,
+):
+    rows, depth = family_ref.shape
+    seqs = rows // width
+    tiles = depth // 128
+    group = 128 // width
+    source = family_ref[...].astype(F32)
+    normed = standardize_features(source).astype(BF16)
+    query_s[...] = dot(normed, project_ref[:, :depth]).astype(BF16)
+    key_s[...] = dot(normed, project_ref[:, depth : 2 * depth]).astype(BF16)
+    value_s[...] = dot(normed, project_ref[:, 2 * depth : 3 * depth]).astype(BF16)
+    gating = jax.nn.sigmoid(dot(normed, project_ref[:, 3 * depth :]))
+    same = (iota((128, 128), 0) // width == iota((128, 128), 1) // width).astype(F32).astype(BF16)
+    lane_group = iota((rows, 128), 1) // width
+    scale = 1.0 / math.sqrt(depth // heads)
+    gated = []
+    for t in range(tiles):
+        cols = slice(128 * t, 128 * t + 128)
+        bias = bias_ref[:, cols].astype(F32)
+        parts = []
+        for s in range(seqs):
+            span = slice(width * s, width * s + width)
+            keys = jnp.concatenate([key_s[span, cols]] * group, 0) * same
+            parts.append(dot_nt(query_s[span, cols], keys) * scale + bias)
+        logits = jnp.concatenate(parts, 0)
+        top = jnp.full(logits.shape, -jnp.inf, F32)
+        for h in range(group):
+            best = jnp.max(
+                jnp.where(lane_group == h, logits, -jnp.inf), axis=-1, keepdims=True
+            )
+            top = jnp.where(lane_group == h, best, top)
+        weight_s[...] = jnp.exp(logits - top).astype(BF16)
+        total = dot(weight_s[...], same)
+        parts = []
+        for s in range(seqs):
+            span = slice(width * s, width * s + width)
+            values = jnp.concatenate([value_s[span, cols]] * group, 0) * same
+            parts.append(dot(weight_s[span, :], values))
+        mixed = jnp.concatenate(parts, 0) / total
+        gated.append((gating[:, cols] * mixed).astype(BF16))
+    after = (source + dot(jnp.concatenate(gated, 1), merge_ref[...])).astype(BF16)
+    family_out_ref[...] = after
+    ready = standardize_features(after.astype(F32))
+    for t in range(tiles):
+        row_s[rows * t : rows * (t + 1), :] = ready[:, 128 * t : 128 * t + 128]
+    hidden = factor_ref.shape[1] // 2
+    placed = jnp.zeros((width // group * seqs, 256), F32)
+    for q in range(group):
+        picked = jnp.concatenate(
+            [
+                jnp.concatenate(
+                    [
+                        row_s[pl.ds(rows * t + group * g + q, seqs, stride=width), :]
+                        for g in range(width // group)
+                    ],
+                    0,
+                )
+                for t in range(tiles)
+            ],
+            1,
+        ).astype(BF16)
+        both = dot(picked, factor_ref[...]).astype(BF16)
+        src = iota((2 * hidden, 256), 0)
+        dst = iota((2 * hidden, 256), 1)
+        goal = src % hidden + hidden * q + 128 * (src // hidden)
+        placed = placed + dot(both, (goal == dst).astype(F32).astype(BF16))
+    groups = width // group
+    for g in range(groups):
+        span = slice(seqs * g, seqs * g + seqs)
+        send_ref[seqs * g : seqs * (g + 1), :] = placed[span, :128].astype(BF16)
+        base = seqs * groups
+        send_ref[base + seqs * g : base + seqs * (g + 1), :] = placed[span, 128:].astype(BF16)
+    base = 2 * seqs * groups
+    pairs = edge_ref.shape[0]
+    send_ref[base : base + pairs, :] = edge_ref[...]
+    send_ref[base + pairs : base + 2 * pairs, :] = loss_ref[...]
+    own = mask_ref.shape[0]
+    mask_s[...] = jnp.zeros(mask_s.shape, F32)
+    mask_s[:own, :] = mask_ref[...].astype(F32)
+    eye = (iota((width, width), 0) == iota((width, width), 1)).astype(F32).astype(BF16)
+    send_ref[base + 2 * pairs :, :] = dot_nt(eye, mask_s[...].astype(BF16)).astype(BF16)
+
+
+def block_transpose(blocks, step):
+    lane = iota(blocks[0].shape, 1)
+    for shift in (2 * step, step):
+        low = lane // shift % 2 == 0
+        stride = shift // step
+        out = list(blocks)
+        for q in range(len(blocks)):
+            if q // stride % 2 == 0:
+                x, y = blocks[q], blocks[q + stride]
+                up = pltpu.roll(y, shift, 1)
+                down = pltpu.roll(x, 4 * step - shift, 1)
+                out[q] = jnp.where(low, x, up)
+                out[q + stride] = jnp.where(low, down, y)
+        blocks = out
+    return blocks
+
+
+def pair_kernel(
+    axis,
+    width,
+    own,
+    hidden,
+    seqs,
+    all_ref,
+    covariance_ref,
+    edges_ref,
+    cycle_ref,
+    out_ref,
+    grad_ref,
+    turn_s,
+    right_s,
+    cov_s,
+    cov_bf_s,
+    mid_s,
+    a_s,
+    b_s,
+    loss_s,
+    own_a_s,
+    own_b_s,
+    tri_s,
+):
+    me = lax.axis_index(axis)
+    n = all_ref.shape[0]
+    group = 128 // hidden
+    groups = width // group
+    base = 2 * seqs * groups
+    pairs = own * width
+    chans = 128
+
+    def gathered(first, count):
+        return jnp.concatenate([all_ref[d, first : first + count, :] for d in range(n)], 0)
+
+    for g in range(groups):
+        right = gathered(seqs * groups + seqs * g, seqs).astype(F32)
+        turn_s[128 * g : 128 * g + 128, :] = right.T
+    cov_s[...] = covariance_ref[...].astype(F32)
+    for b in range(hidden):
+        span = slice(width * b, width * b + width)
+        right_s[span, :] = turn_s[pl.ds(b, width, stride=hidden), :].astype(BF16)
+        span = slice(hidden * b, hidden * b + hidden)
+        cov_bf_s[span, :] = cov_s[pl.ds(b, hidden, stride=hidden), :].astype(BF16)
+    for g in range(groups):
+        left = gathered(seqs * g, seqs)
+        outer = dot(right_s[...], left)
+        columns = []
+        for p in range(hidden // group):
+            first = 128 * p
+            columns.append(
+                block_transpose(
+                    [outer[first + width * q : first + width * (q + 1), :] for q in range(group)],
+                    hidden,
+                )
+            )
+        flat = jnp.concatenate(
+            [jnp.concatenate([c[i] for c in columns], 1) for i in range(group)], 0
+        )
+        high = flat.astype(BF16)
+        low = (flat - high.astype(F32)).astype(BF16)
+        added = (dot(high, cov_bf_s[...]) + dot(low, cov_bf_s[...])) * (1.0 / (seqs * n))
+        span = slice(pairs * g, pairs * (g + 1))
+        edge = all_ref[g, base : base + pairs, :].astype(F32)
+        mid = (edge + added).astype(BF16).astype(F32)
+        mid_s[span, :] = mid
+        normed = standardize_features(mid).astype(BF16)
+        sides = dot(normed, edges_ref[:, : 2 * chans])
+        mask = all_ref[g, base + 2 * pairs :, :].astype(F32)
+        keep = jnp.concatenate(
+            [jnp.broadcast_to(mask[:, r : r + 1], (width, chans)) for r in range(own)], 0
+        )
+        a_s[span, :] = (keep * sides[:, :chans]).astype(BF16).astype(F32)
+        b_s[span, :] = (keep * sides[:, chans:]).astype(BF16).astype(F32)
+        loss_s[span, :] = all_ref[g, base + pairs : base + 2 * pairs, :].astype(F32)
+
+    rows = pl.ds(pl.multiple_of(me * pairs, pairs), pairs)
+
+    def rows_and_columns(ref):
+        return jnp.concatenate(
+            [ref[rows, :]] + [ref[pl.ds(me * own + r, width, stride=width), :] for r in range(own)],
+            0,
+        )
+
+    mid = rows_and_columns(mid_s)
+    loss = rows_and_columns(loss_s)
+    own_a_s[...] = a_s[rows, :]
+    own_b_s[...] = b_s[rows, :]
+    normed = standardize_features(mid).astype(BF16)
+    gating = jax.nn.sigmoid(dot(normed, edges_ref[:, 2 * chans :]))
+
+    def row(ref, r):
+        return jnp.broadcast_to(ref[r : r + 1, :], (width, chans))
+
+    acc = [jnp.zeros((width, chans), F32) for _ in range(2 * own)]
+    for k in range(width):
+        b_k = b_s[pl.ds(k, width, stride=width), :]
+        a_k = a_s[pl.ds(k, width, stride=width), :]
+        for r in range(own):
+            acc[r] = acc[r] + row(own_a_s, width * r + k) * b_k
+            acc[own + r] = acc[own + r] + row(own_b_s, width * r + k) * a_k
+    tri = jnp.concatenate(acc, 0)
+    center = tri - jnp.mean(tri, -1, keepdims=True)
+    scale_inv = lax.rsqrt(jnp.mean(center * center, -1, keepdims=True) + EPSILON)
+    unit = center * scale_inv
+    update = dot(unit[:pairs].astype(BF16), cycle_ref[...])
+    out_ref[...] = (mid[:pairs] + gating[:pairs] * update).astype(BF16)
+    grad_normed = dot_nt((loss * gating).astype(BF16), cycle_ref[...])
+    tri_s[...] = (
+        (
+            scale_inv
+            * (
+                grad_normed
+                - jnp.mean(grad_normed, -1, keepdims=True)
+                - unit * jnp.mean(grad_normed * unit, -1, keepdims=True)
+            )
+        )
+        .astype(BF16)
+        .astype(F32)
+    )
+    acc = [jnp.zeros((width, chans), F32) for _ in range(2 * own)]
+    for j in range(width):
+        span = slice(width * j, width * j + width)
+        b_j = b_s[span, :]
+        a_j = a_s[span, :]
+        for r in range(own):
+            acc[r] = acc[r] + row(tri_s, width * r + j) * b_j
+            acc[own + r] = acc[own + r] + row(tri_s, pairs + width * r + j) * a_j
+    mask = all_ref[me, base + 2 * pairs :, :].astype(F32)
+    keep = jnp.concatenate(
+        [jnp.broadcast_to(mask[:, r : r + 1], (width, chans)) for r in range(own)], 0
+    )
+    gate_own = gating[:pairs]
+    grad_gate = loss[:pairs] * update * gate_own * (1.0 - gate_own)
+    grad_proj = jnp.concatenate(
+        [
+            keep * jnp.concatenate(acc[:own], 0),
+            keep * jnp.concatenate(acc[own:], 0),
+            grad_gate,
+        ],
+        1,
+    ).astype(BF16)
+    grad_input = dot_nt(grad_proj, edges_ref[...])
+    grad_ref[...] = loss[:pairs] + norm_back(mid[:pairs], grad_input)
+
+
+def body_resident(
+    family_matrix,
+    edge_matrix,
+    edge_validity,
+    query_key_value_gate_matrix,
+    logit_offset_matrix,
+    heads_merge_matrix,
+    left_right_factor_matrix,
+    covariance_merge_matrix,
+    edges_gate_factor_matrix,
+    cycle_merge_matrix,
+    loss_sensitivity,
+):
+    seqs, width, depth = family_matrix.shape
+    own, _, chans = edge_matrix.shape
+    heads = logit_offset_matrix.shape[1]
+    hidden = left_right_factor_matrix.shape[1] // 2
+    pairs = own * width
+    every = width * width
+    edge = edge_matrix.reshape(pairs, chans)
+    loss = loss_sensitivity.reshape(pairs, chans)
+    vmem = pl.BlockSpec(memory_space=pltpu.VMEM)
+    bias = pl.pallas_call(
+        bias_kernel,
+        out_shape=jax.ShapeDtypeStruct((own, heads * width), BF16),
+        in_specs=[vmem] * 2,
+        out_specs=vmem,
+        name="pair_bias",
+    )(edge, logit_offset_matrix)
+    bias_all = lax.all_gather(bias, "dap", axis=0, tiled=True)
+    sent = 2 * seqs * width * hidden // 128 + 2 * pairs + width
+    family_out, send = pl.pallas_call(
+        functools.partial(attention_kernel, width, heads),
+        out_shape=(
+            jax.ShapeDtypeStruct((seqs * width, depth), BF16),
+            jax.ShapeDtypeStruct((sent, chans), BF16),
+        ),
+        in_specs=[vmem] * 8,
+        out_specs=(vmem, vmem),
+        scratch_shapes=[pltpu.VMEM((seqs * width, depth), BF16)] * 3
+        + [
+            pltpu.VMEM((seqs * width, 128), BF16),
+            pltpu.VMEM((seqs * width * depth // 128, 128), F32),
+            pltpu.VMEM((128, width), F32),
+        ],
+        name="row_attention",
+    )(
+        family_matrix.reshape(seqs * width, depth),
+        bias_all,
+        query_key_value_gate_matrix,
+        heads_merge_matrix,
+        left_right_factor_matrix,
+        edge,
+        loss,
+        edge_validity,
+    )
+    gathered = lax.all_gather(send, "dap", axis=0, tiled=False)
+    pair_out, pair_grad = pl.pallas_call(
+        functools.partial(pair_kernel, "dap", width, own, hidden, seqs),
+        out_shape=(
+            jax.ShapeDtypeStruct((pairs, chans), BF16),
+            jax.ShapeDtypeStruct((pairs, chans), F32),
+        ),
+        in_specs=[vmem] * 4,
+        out_specs=(vmem, vmem),
+        scratch_shapes=[
+            pltpu.VMEM((hidden * width, 128), F32),
+            pltpu.VMEM((hidden * width, 128), BF16),
+            pltpu.VMEM((hidden * hidden, chans), F32),
+            pltpu.VMEM((hidden * hidden, chans), BF16),
+            pltpu.VMEM((every, chans), F32),
+            pltpu.VMEM((every, chans), F32),
+            pltpu.VMEM((every, chans), F32),
+            pltpu.VMEM((every, chans), F32),
+            pltpu.VMEM((pairs, chans), F32),
+            pltpu.VMEM((pairs, chans), F32),
+            pltpu.VMEM((2 * pairs, chans), F32),
+        ],
+        name="pair_update",
+    )(gathered, covariance_merge_matrix, edges_gate_factor_matrix, cycle_merge_matrix)
+    return (
+        family_out.reshape(seqs, width, depth),
+        pair_out.reshape(own, width, chans),
+        pair_grad.reshape(own, width, chans),
+    )
+
+
+def fits_resident(dap, family, edge, logit, factor):
+    seqs, width, depth = family.shape
+    own, _, chans = edge.shape
+    return (
+        own * dap == width
+        and width == 32
+        and factor.shape[1] == 64
+        and depth == 32 * logit.shape[1]
+        and depth % 128 == 0
+        and chans == 128
+        and own * width == 128
+        and seqs % 16 == 0
+        and seqs * dap == 128
+    )
+
+
+def body(*args):
+    dap = lax.axis_size("dap")
+    if fits_resident(dap, args[0], args[1], args[4], args[6]):
+        return body_resident(*args)
+    return body_general(*args)
+
+
 def solution(mesh):
     in_specs = (
         P(("dp", "dap"), None, None),

time: 127 us -> 70.5 us (0.56)
  blocking collectives: 28.5 us -> 10.5 us
  Pallas kernels: 0 us -> 17.8 us
  matrix products: 16.8 us -> 0 us
  waiting for transfers between devices: 39.5 us -> 24.3 us
  other arithmetic: 11 us -> 0 us
  local copies, waits for them, and re-layouts: 12.5 us -> 3.5 us
  starting transfers between devices: 3.45 us -> 0.04 us
    reduce_scatter x1 -> x0, waiting for transfers between devices: 32.7 us -> none  [body(): lax.psum_scatter(jnp.einsum('ijc,ikc->jkc', grad_part, side_a, preferred_...]
    all_gather x0 -> x1, waiting for transfers between devices: none -> 24.2 us  [body_resident(): gathered = lax.all_gather(send, 'dap', axis=0, tiled=False)]
    all_gather x3 -> x1, blocking collectives: 28.5 us -> 10.5 us  [body_resident(): bias_all = lax.all_gather(bias, 'dap', axis=0, tiled=True)]
    pallas_call x0 -> x3, Pallas kernels: none -> 17.8 us  [the longest x1 11.4 us: body_resident(): pl.pallas_call(functools.partial(pair_kernel, 'dap', width, own, hidden,...]
    dot_general x19 -> x0, matrix products: 16.8 us -> none  [the longest x2 3.69 us: lateral_heads_mixing(): jnp.dot(gated.reshape(-1, feature_depth), heads_merge_matrix, preferred_e...]
    reduce_sum x11 -> x0, other arithmetic: 6.94 us -> none  [the longest x6 3.67 us: standardize_features(): jnp.mean(center * center, -1, keepdims=True) + EPSILON]
    all_to_all x1 -> x0, waiting for transfers between devices: 6.8 us -> none  [body(): lax.all_to_all(family_after_heads, 'dap', split_axis=1, concat_axis=0, ti...]
    reshape x8 -> x0, local copies, waits for them, and re-layouts: 3.55 us -> none  [the longest x2 2 us: lateral_heads_mixing(): value_rows = projected[..., 2 * feature_depth:3 * feature_depth].astype(j...]
  transfers between devices with their start and end apart: 2 -> 1, of which waited for: 2 -> 1; matrix products, arithmetic and copies ran while one was open for 1% -> 0% of each run, Pallas kernels for 0% -> 0%
where the time goes in v1:
time: 70.5 us; the launch traced here: 70.1 us
  waiting for transfers between devices  24.3 us (34%)
  Pallas kernels  17.8 us (25%)
  between operations  14 us (20%)
  blocking collectives  10.5 us (15%)
  local copies, waits for them, and re-layouts  3.5 us (5%)
    all_gather x1, waiting for transfers between devices, body_resident(): gathered = lax.all_gather(send, 'dap', axis=0, tiled=False)  24.2 us
    pallas_call x1, Pallas kernels, body_resident(): pl.pallas_call(functools.partial(pair_kernel, 'dap', width, own, hidden,...  11.4 us
    all_gather x1, blocking collectives, body_resident(): bias_all = lax.all_gather(bias, 'dap', axis=0, tiled=True)  10.5 us
    pallas_call x1, Pallas kernels, body_resident(): pl.pallas_call(functools.partial(attention_kernel, width, heads), out_sha...  4.77 us
    unnamed x3, local copies, waits for them, and re-layouts  3.5 us
    pallas_call x1, Pallas kernels, body_resident(): pl.pallas_call(bias_kernel, out_shape=jax.ShapeDtypeStruct((own, heads *...  1.68 us
  transfers between devices with their start and end apart: 1, of which 1 were waited for; matrix products, arithmetic and copies ran while one was open for 0% of the time, Pallas kernels for 0%

profile of v1, /device:TPU:0, one launch (start us, length us, event | category | flops | bytes accessed | tf_op | source)
XLA Modules:
  0.0 70.1 jit_solution(6366612263724014765)
XLA Ops:
  7.2 0.0 all-gather.4.cloned.1.call-start
  7.2 1.4 %copy.16.weight_ref = bf16[128,8]{1,0:T(8,128)(2,1)} copy(bf16[128,8]{0,1:T(8,128)(2,1)} %param.15) | data formatting | bytes 4096 | tf_op args[4]
  8.6 1.7 %pair_bias.1 = bf16[4,256]{1,0:T(4,128)(2,1)} custom-call(bf16[128,128]{1,0:T(8,128)(2,1)} %bitcast.10, bf16[128,8]{1,0:T(8,128)(2,1)} %copy.16.weight_ref), custom_call_target="tpu_custom_call" | custom-call | tf_op jit(solution)/shard_map/pair_bias/pallas_call | solution.py:515
  10.3 10.5 %all-gather.1 = bf16[8,4,256]{2,1,0:T(4,128)(2,1)S(1)} all-gather(bf16[1,4,256]{2,1,0:T(4,128)(2,1)} %bitcast.13), channel_id=1, replica_groups=mesh['dap'=8,'dp'=4] {'dap'}, dimensions={0}, use_global_device_ids=true | all-gather | bytes 18432 | tf_op jit(solution)/shard_map/all_gather | solution.py:522
  20.8 0.6 reshape.32.bias_ref
  21.4 1.5 %copy.17.factor_ref = bf16[256,64]{1,0:T(8,128)(2,1)} copy(bf16[256,64]{0,1:T(8,128)(2,1)} %param.17) | data formatting | bytes 65536 | tf_op args[6]
  22.9 4.8 %row_attention.1 = (bf16[512,256]{1,0:T(8,128)(2,1)}, bf16[544,128]{1,0:T(8,128)(2,1)}) custom-call(bf16[512,256]{1,0:T(8,128)(2,1)} %bitcast.9, bf16[32,256]{1,0:T(8,128)(2,1)} %reshape.32.bias_ref, bf16[256,1024]{1,0:T(8,128)(2,1)} %project_ref.1, bf16[256,256]{1,0:T(8,128)(2,1)} %merge_ref.1, bf16[256,64]{1,0:T(8,128)(2,1)} %copy.17.factor_ref, ...), custom_call_target="tpu_custom_call" | custom-call | tf_op jit(solution)/shard_map/row_attention/pallas_call | solution.py:524
  27.6 0.0 all-gather.4.cloned.1.call-update
  27.7 24.2 %all-gather.4.cloned.1.call-done = bf16[4352,128]{1,0:T(8,128)(2,1)} async-done(((bf16[544,128]{1,0:T(8,128)(2,1)}), bf16[4352,128]{1,0:T(8,128)(2,1)}) %all-gather.4.cloned.1.call-update) | async-done | bytes 1114128 | tf_op jit(solution)/shard_map/all_gather | solution.py:549
  51.9 11.4 %pair_update.1 = (bf16[128,128]{1,0:T(8,128)(2,1)}, f32[128,128]{1,0:T(8,128)}) custom-call(bf16[8,544,128]{2,1,0:T(8,128)(2,1)} %bitcast.8, bf16[1024,128]{1,0:T(8,128)(2,1)} %covariance_ref.1, bf16[128,384]{1,0:T(8,128)(2,1)} %edges_ref.1, bf16[128,128]{1,0:T(8,128)(2,1)} %cycle_ref.1), custom_call_target="tpu_custom_call" | custom-call | tf_op jit(solution)/shard_map/pair_update/pallas_call | solution.py:550
Async XLA Ops:
  7.2 44.7 %all-gather.4.cloned.1.call-start = ((), (), s32[]{:S(2)}) async-start(), calls=%async_computation | async-start | bytes 1253376 | tf_op jit(solution)/shard_map/all_gather | solution.py:549
Sparse Core Ops, SparseCore 0:
  27.8 24.0 all-gather.3

commit v2 on v1

--- a/solution.py
+++ b/solution.py
@@ -212,31 +212,44 @@
     return lax.broadcasted_iota(jnp.int32, shape, dim)
 
 
-def bias_kernel(edge_ref, weight_ref, out_ref):
+def pack_kernel(width, edge_ref, weight_ref, loss_ref, mask_ref, send_ref, mask_s):
     rows, chans = edge_ref.shape
-    own, lanes = out_ref.shape
-    width = rows // own
-    heads = weight_ref.shape[1]
+    heads = weight_ref.shape[0]
+    own = rows // width
+    lanes = heads * width
+    send_ref[:rows, :] = edge_ref[...]
+    send_ref[rows : 2 * rows, :] = loss_ref[...]
+    mask_s[...] = jnp.zeros(mask_s.shape, F32)
+    mask_s[:own, :] = mask_ref[...].astype(F32)
+    eye = (iota((width, width), 0) == iota((width, width), 1)).astype(F32).astype(BF16)
+    base = 2 * rows
+    send_ref[base : base + width, :] = dot_nt(eye, mask_s[...].astype(BF16)).astype(BF16)
     normed = standardize_features(edge_ref[...].astype(F32)).astype(BF16)
     spread = (iota((heads, lanes), 0) == iota((heads, lanes), 1) // width).astype(F32)
-    weight = dot(weight_ref[...], spread.astype(BF16)).astype(BF16)
+    weight = lax.dot_general(
+        weight_ref[...], spread.astype(BF16), (((0,), (0,)), ((), ())), preferred_element_type=F32
+    ).astype(BF16)
     every = dot(normed, weight)
     keep = iota((rows, lanes), 0) % width == iota((rows, lanes), 1) % width
-    picked = jnp.where(keep, every, 0.0).reshape(own, width, lanes)
-    out_ref[...] = jnp.sum(picked, 1).astype(BF16)
+    picked = jnp.where(keep, every, 0.0).astype(BF16)
+    packed = jnp.zeros((16, 128), F32)
+    for t in range(lanes // 128):
+        place = iota((16, rows), 0) == 8 * t + iota((16, rows), 1) // width
+        packed = packed + dot(
+            place.astype(F32).astype(BF16), picked[:, 128 * t : 128 * t + 128]
+        )
+    send_ref[base + width :, :] = packed.astype(BF16)
 
 
 def attention_kernel(
     width,
     heads,
+    own,
     family_ref,
-    bias_ref,
+    all_ref,
     project_ref,
     merge_ref,
     factor_ref,
-    edge_ref,
-    loss_ref,
-    mask_ref,
     family_out_ref,
     send_ref,
     query_s,
@@ -244,7 +257,6 @@
     value_s,
     weight_s,
     row_s,
-    mask_s,
 ):
     rows, depth = family_ref.shape
     seqs = rows // width
@@ -260,9 +272,13 @@
     lane_group = iota((rows, 128), 1) // width
     scale = 1.0 / math.sqrt(depth // heads)
     gated = []
+    base = all_ref.shape[1] - 16
+    biases = jnp.concatenate([all_ref[d, base:, :] for d in range(all_ref.shape[0])], 0)
     for t in range(tiles):
         cols = slice(128 * t, 128 * t + 128)
-        bias = bias_ref[:, cols].astype(F32)
+        row = iota((width, biases.shape[0]), 0)
+        take = iota((width, biases.shape[0]), 1) == 16 * (row // own) + 8 * t + row % own
+        bias = dot(take.astype(F32).astype(BF16), biases)
         parts = []
         for s in range(seqs):
             span = slice(width * s, width * s + width)
@@ -289,7 +305,7 @@
     ready = standardize_features(after.astype(F32))
     for t in range(tiles):
         row_s[rows * t : rows * (t + 1), :] = ready[:, 128 * t : 128 * t + 128]
-    hidden = factor_ref.shape[1] // 2
+    hidden = factor_ref.shape[0] // 2
     placed = jnp.zeros((width // group * seqs, 256), F32)
     for q in range(group):
         picked = jnp.concatenate(
@@ -305,7 +321,7 @@
             ],
             1,
         ).astype(BF16)
-        both = dot(picked, factor_ref[...]).astype(BF16)
+        both = dot_nt(picked, factor_ref[...]).astype(BF16)
         src = iota((2 * hidden, 256), 0)
         dst = iota((2 * hidden, 256), 1)
         goal = src % hidden + hidden * q + 128 * (src // hidden)
@@ -316,15 +332,6 @@
         send_ref[seqs * g : seqs * (g + 1), :] = placed[span, :128].astype(BF16)
         base = seqs * groups
         send_ref[base + seqs * g : base + seqs * (g + 1), :] = placed[span, 128:].astype(BF16)
-    base = 2 * seqs * groups
-    pairs = edge_ref.shape[0]
-    send_ref[base : base + pairs, :] = edge_ref[...]
-    send_ref[base + pairs : base + 2 * pairs, :] = loss_ref[...]
-    own = mask_ref.shape[0]
-    mask_s[...] = jnp.zeros(mask_s.shape, F32)
-    mask_s[:own, :] = mask_ref[...].astype(F32)
-    eye = (iota((width, width), 0) == iota((width, width), 1)).astype(F32).astype(BF16)
-    send_ref[base + 2 * pairs :, :] = dot_nt(eye, mask_s[...].astype(BF16)).astype(BF16)
 
 
 def block_transpose(blocks, step):
@@ -350,6 +357,7 @@
     own,
     hidden,
     seqs,
+    sides_ref,
     all_ref,
     covariance_ref,
     edges_ref,
@@ -372,12 +380,11 @@
     n = all_ref.shape[0]
     group = 128 // hidden
     groups = width // group
-    base = 2 * seqs * groups
     pairs = own * width
     chans = 128
 
     def gathered(first, count):
-        return jnp.concatenate([all_ref[d, first : first + count, :] for d in range(n)], 0)
+        return jnp.concatenate([sides_ref[d, first : first + count, :] for d in range(n)], 0)
 
     for g in range(groups):
         right = gathered(seqs * groups + seqs * g, seqs).astype(F32)
@@ -407,18 +414,18 @@
         low = (flat - high.astype(F32)).astype(BF16)
         added = (dot(high, cov_bf_s[...]) + dot(low, cov_bf_s[...])) * (1.0 / (seqs * n))
         span = slice(pairs * g, pairs * (g + 1))
-        edge = all_ref[g, base : base + pairs, :].astype(F32)
+        edge = all_ref[g, :pairs, :].astype(F32)
         mid = (edge + added).astype(BF16).astype(F32)
         mid_s[span, :] = mid
         normed = standardize_features(mid).astype(BF16)
         sides = dot(normed, edges_ref[:, : 2 * chans])
-        mask = all_ref[g, base + 2 * pairs :, :].astype(F32)
+        mask = all_ref[g, 2 * pairs : 2 * pairs + width, :].astype(F32)
         keep = jnp.concatenate(
             [jnp.broadcast_to(mask[:, r : r + 1], (width, chans)) for r in range(own)], 0
         )
         a_s[span, :] = (keep * sides[:, :chans]).astype(BF16).astype(F32)
         b_s[span, :] = (keep * sides[:, chans:]).astype(BF16).astype(F32)
-        loss_s[span, :] = all_ref[g, base + pairs : base + 2 * pairs, :].astype(F32)
+        loss_s[span, :] = all_ref[g, pairs : 2 * pairs, :].astype(F32)
 
     rows = pl.ds(pl.multiple_of(me * pairs, pairs), pairs)
 
@@ -472,7 +479,7 @@
         for r in range(own):
             acc[r] = acc[r] + row(tri_s, width * r + j) * b_j
             acc[own + r] = acc[own + r] + row(tri_s, pairs + width * r + j) * a_j
-    mask = all_ref[me, base + 2 * pairs :, :].astype(F32)
+    mask = all_ref[me, 2 * pairs : 2 * pairs + width, :].astype(F32)
     keep = jnp.concatenate(
         [jnp.broadcast_to(mask[:, r : r + 1], (width, chans)) for r in range(own)], 0
     )
@@ -512,39 +519,35 @@
     edge = edge_matrix.reshape(pairs, chans)
     loss = loss_sensitivity.reshape(pairs, chans)
     vmem = pl.BlockSpec(memory_space=pltpu.VMEM)
-    bias = pl.pallas_call(
-        bias_kernel,
-        out_shape=jax.ShapeDtypeStruct((own, heads * width), BF16),
-        in_specs=[vmem] * 2,
+    packed = pl.pallas_call(
+        functools.partial(pack_kernel, width),
+        out_shape=jax.ShapeDtypeStruct((2 * pairs + width + 16, chans), BF16),
+        in_specs=[vmem] * 4,
         out_specs=vmem,
-        name="pair_bias",
-    )(edge, logit_offset_matrix)
-    bias_all = lax.all_gather(bias, "dap", axis=0, tiled=True)
-    sent = 2 * seqs * width * hidden // 128 + 2 * pairs + width
+        scratch_shapes=[pltpu.VMEM((128, width), F32)],
+        name="pack_pairs",
+    )(edge, logit_offset_matrix.T, loss, edge_validity)
+    packed_all = lax.all_gather(packed, "dap", axis=0, tiled=False)
     family_out, send = pl.pallas_call(
-        functools.partial(attention_kernel, width, heads),
+        functools.partial(attention_kernel, width, heads, own),
         out_shape=(
             jax.ShapeDtypeStruct((seqs * width, depth), BF16),
-            jax.ShapeDtypeStruct((sent, chans), BF16),
+            jax.ShapeDtypeStruct((2 * seqs * width * hidden // 128, 128), BF16),
         ),
-        in_specs=[vmem] * 8,
+        in_specs=[vmem] * 5,
         out_specs=(vmem, vmem),
         scratch_shapes=[pltpu.VMEM((seqs * width, depth), BF16)] * 3
         + [
             pltpu.VMEM((seqs * width, 128), BF16),
             pltpu.VMEM((seqs * width * depth // 128, 128), F32),
-            pltpu.VMEM((128, width), F32),
         ],
         name="row_attention",
     )(
         family_matrix.reshape(seqs * width, depth),
-        bias_all,
+        packed_all,
         query_key_value_gate_matrix,
         heads_merge_matrix,
-        left_right_factor_matrix,
-        edge,
-        loss,
-        edge_validity,
+        left_right_factor_matrix.T,
     )
     gathered = lax.all_gather(send, "dap", axis=0, tiled=False)
     pair_out, pair_grad = pl.pallas_call(
@@ -553,7 +556,7 @@
             jax.ShapeDtypeStruct((pairs, chans), BF16),
             jax.ShapeDtypeStruct((pairs, chans), F32),
         ),
-        in_specs=[vmem] * 4,
+        in_specs=[vmem] * 5,
         out_specs=(vmem, vmem),
         scratch_shapes=[
             pltpu.VMEM((hidden * width, 128), F32),
@@ -569,7 +572,7 @@
             pltpu.VMEM((2 * pairs, chans), F32),
         ],
         name="pair_update",
-    )(gathered, covariance_merge_matrix, edges_gate_factor_matrix, cycle_merge_matrix)
+    )(gathered, packed_all, covariance_merge_matrix, edges_gate_factor_matrix, cycle_merge_matrix)
     return (
         family_out.reshape(seqs, width, depth),
         pair_out.reshape(own, width, chans),

time: 70.5 us -> 43.5 us (0.62)
  waiting for transfers between devices: 24.3 us -> 0 us
  blocking collectives: 10.5 us -> 24.3 us
  between operations: 14 us -> 0.63 us
  local copies, waits for them, and re-layouts: 3.5 us -> 0 us
    all_gather x1 -> x0, waiting for transfers between devices: 24.2 us -> none  [body_resident(): gathered = lax.all_gather(send, 'dap', axis=0, tiled=False)]
    all_gather x1 -> x2, blocking collectives: 10.5 us -> 24.3 us  [the longest x1 13.5 us: body_resident(): packed_all = lax.all_gather(packed, 'dap', axis=0, tiled=False)]
    unnamed x3 -> x0, local copies, waits for them, and re-layouts: 3.5 us -> none
  transfers between devices with their start and end apart: 1 -> 0, of which waited for: 1 -> 0; matrix products, arithmetic and copies ran while one was open for 0% -> 0% of each run, Pallas kernels for 0% -> 0%
where the time goes in v2:
time: 43.5 us; the launch traced here: 43.1 us
  blocking collectives  24.3 us (56%)
  Pallas kernels  18.2 us (42%)
  between operations  0.63 us (1%)
    all_gather x1, blocking collectives, body_resident(): packed_all = lax.all_gather(packed, 'dap', axis=0, tiled=False)  13.5 us
    pallas_call x1, Pallas kernels, body_resident(): pl.pallas_call(functools.partial(pair_kernel, 'dap', width, own, hidden,...  11.4 us
    all_gather x1, blocking collectives, body_resident(): gathered = lax.all_gather(send, 'dap', axis=0, tiled=False)  10.8 us
    pallas_call x1, Pallas kernels, body_resident(): pl.pallas_call(functools.partial(attention_kernel, width, heads, own), ou...  4.91 us
    pallas_call x1, Pallas kernels, body_resident(): pl.pallas_call(functools.partial(pack_kernel, width), out_shape=jax.Shape...  1.91 us

profile of v2, /device:TPU:0, one launch (start us, length us, event | category | flops | bytes accessed | tf_op | source)
XLA Modules:
  0.0 43.1 jit_solution(8419675497389909194)
XLA Ops:
  0.6 1.9 %pack_pairs.1 = bf16[304,128]{1,0:T(8,128)(2,1)} custom-call(bf16[128,128]{1,0:T(8,128)(2,1)} %bitcast.15, bf16[8,128]{1,0:T(8,128)(2,1)} %bitcast.17, bf16[128,128]{1,0:T(8,128)(2,1)} %bitcast.16, s32[4,32]{1,0:T(4,128)} %mask_ref.1), custom_call_target="tpu_custom_call" | custom-call | tf_op jit(solution)/shard_map/pack_pairs/pallas_call | solution.py:522
  2.5 13.5 %all-gather = bf16[2432,128]{1,0:T(8,128)(2,1)} all-gather(bf16[304,128]{1,0:T(8,128)(2,1)} %pack_pairs.1), channel_id=2, replica_groups=mesh['dap'=8,'dp'=4] {'dap'}, dimensions={0}, use_global_device_ids=true | all-gather | bytes 700416 | tf_op jit(solution)/shard_map/all_gather | solution.py:530
  16.1 4.9 %row_attention.1 = (bf16[512,256]{1,0:T(8,128)(2,1)}, bf16[256,128]{1,0:T(8,128)(2,1)}) custom-call(bf16[512,256]{1,0:T(8,128)(2,1)} %bitcast.13, bf16[8,304,128]{2,1,0:T(8,128)(2,1)} %bitcast.10, bf16[256,1024]{1,0:T(8,128)(2,1)} %project_ref.1, bf16[256,256]{1,0:T(8,128)(2,1)} %merge_ref.1, bf16[64,256]{1,0:T(8,128)(2,1)} %bitcast.14), custom_call_target="tpu_custom_call" | custom-call | tf_op jit(solution)/shard_map/row_attention/pallas_call | solution.py:531
  21.0 10.8 %all-gather.1 = bf16[2048,128]{1,0:T(8,128)(2,1)} all-gather(bf16[256,128]{1,0:T(8,128)(2,1)} %get-tuple-element.8), channel_id=3, replica_groups=mesh['dap'=8,'dp'=4] {'dap'}, dimensions={0}, use_global_device_ids=true | all-gather | bytes 589824 | tf_op jit(solution)/shard_map/all_gather | solution.py:552
  31.7 11.4 %pair_update.1 = (bf16[128,128]{1,0:T(8,128)(2,1)}, f32[128,128]{1,0:T(8,128)}) custom-call(bf16[8,256,128]{2,1,0:T(8,128)(2,1)} %bitcast.12, bf16[8,304,128]{2,1,0:T(8,128)(2,1)} %bitcast.11, bf16[1024,128]{1,0:T(8,128)(2,1)} %covariance_ref.1, bf16[128,384]{1,0:T(8,128)(2,1)} %edges_ref.1, bf16[128,128]{1,0:T(8,128)(2,1)} %cycle_ref.1), custom_call_target="tpu_custom_call" | custom-call | tf_op jit(solution)/shard_map/pair_update/pallas_call | solution.py:553

commit v3 on v2

--- a/solution.py
+++ b/solution.py
@@ -257,6 +257,8 @@
     value_s,
     weight_s,
     row_s,
+    turn_s,
+    line_s,
 ):
     rows, depth = family_ref.shape
     seqs = rows // width
@@ -302,36 +304,35 @@
         gated.append((gating[:, cols] * mixed).astype(BF16))
     after = (source + dot(jnp.concatenate(gated, 1), merge_ref[...])).astype(BF16)
     family_out_ref[...] = after
-    ready = standardize_features(after.astype(F32))
-    for t in range(tiles):
-        row_s[rows * t : rows * (t + 1), :] = ready[:, 128 * t : 128 * t + 128]
+    ready = standardize_features(after.astype(F32)).astype(BF16)
     hidden = factor_ref.shape[0] // 2
-    placed = jnp.zeros((width // group * seqs, 256), F32)
+    groups = width // group
+    row_s[:, : 2 * hidden] = dot_nt(ready, factor_ref[...])
+    placed = jnp.zeros((groups * seqs, 128), F32)
     for q in range(group):
         picked = jnp.concatenate(
-            [
-                jnp.concatenate(
-                    [
-                        row_s[pl.ds(rows * t + group * g + q, seqs, stride=width), :]
-                        for g in range(width // group)
-                    ],
-                    0,
-                )
-                for t in range(tiles)
-            ],
-            1,
-        ).astype(BF16)
-        both = dot_nt(picked, factor_ref[...]).astype(BF16)
-        src = iota((2 * hidden, 256), 0)
-        dst = iota((2 * hidden, 256), 1)
-        goal = src % hidden + hidden * q + 128 * (src // hidden)
-        placed = placed + dot(both, (goal == dst).astype(F32).astype(BF16))
-    groups = width // group
+            [row_s[pl.ds(group * g + q, seqs, stride=width), :] for g in range(groups)], 0
+        )[:, :hidden].astype(BF16)
+        here = iota((hidden, 128), 0) + hidden * q == iota((hidden, 128), 1)
+        placed = placed + dot(picked, here.astype(F32).astype(BF16))
     for g in range(groups):
-        span = slice(seqs * g, seqs * g + seqs)
-        send_ref[seqs * g : seqs * (g + 1), :] = placed[span, :128].astype(BF16)
-        base = seqs * groups
-        send_ref[base + seqs * g : base + seqs * (g + 1), :] = placed[span, 128:].astype(BF16)
+        send_ref[seqs * g : seqs * (g + 1), :] = placed[seqs * g : seqs * (g + 1), :].astype(BF16)
+    turned = dot_nt(factor_ref[hidden : 2 * hidden, :], ready)
+    for k in range(rows // 128):
+        turn_s[hidden * k : hidden * (k + 1), :] = turned[:, 128 * k : 128 * k + 128]
+    chunks = hidden // group
+    for k in range(rows // 128):
+        blocks = [
+            turn_s[pl.ds(hidden * k + q, chunks, stride=group), :] for q in range(group)
+        ]
+        for p, block in enumerate(block_transpose(blocks, width)):
+            first = chunks * (group * k + p)
+            line_s[first : first + chunks, :] = block
+    base = seqs * groups
+    for g in range(chunks):
+        send_ref[base + seqs * g : base + seqs * (g + 1), :] = line_s[
+            pl.ds(g, seqs, stride=chunks), :
+        ].astype(BF16)
 
 
 def block_transpose(blocks, step):
@@ -351,6 +352,30 @@
     return blocks
 
 
+def average(values, weights):
+    high = values.astype(BF16)
+    low = (values - high.astype(F32)).astype(BF16)
+    return dot(jnp.concatenate([high, low], 1), weights)
+
+
+def center_and_scale(values, weights):
+    center = values - average(values, weights)
+    return center, lax.rsqrt(average(center * center, weights) + EPSILON)
+
+
+def merge_rows(parts):
+    row = iota(parts[0].shape, 0)
+    step = 1
+    while len(parts) > 1:
+        low = row // step % 2 == 0
+        parts = [
+            jnp.where(low, x, y) + pltpu.roll(jnp.where(low, y, x), step, 0)
+            for x, y in zip(parts[::2], parts[1::2])
+        ]
+        step *= 2
+    return parts[0]
+
+
 def pair_kernel(
     axis,
     width,
@@ -364,68 +389,94 @@
     cycle_ref,
     out_ref,
     grad_ref,
-    turn_s,
     right_s,
     cov_s,
     cov_bf_s,
+    flat_s,
     mid_s,
+    unit_s,
+    scale_s,
+    gate_s,
     a_s,
     b_s,
     loss_s,
-    own_a_s,
-    own_b_s,
     tri_s,
 ):
     me = lax.axis_index(axis)
     n = all_ref.shape[0]
     group = 128 // hidden
     groups = width // group
+    chunks = hidden // group
     pairs = own * width
     chans = 128
-
-    def gathered(first, count):
-        return jnp.concatenate([sides_ref[d, first : first + count, :] for d in range(n)], 0)
-
-    for g in range(groups):
-        right = gathered(seqs * groups + seqs * g, seqs).astype(F32)
-        turn_s[128 * g : 128 * g + 128, :] = right.T
+    total = seqs * n
+
+    def gathered(first):
+        return jnp.concatenate([sides_ref[d, first : first + seqs, :] for d in range(n)], 0)
+
+    eye = (iota((128, 128), 0) == iota((128, 128), 1)).astype(F32).astype(BF16)
+    for g in range(chunks):
+        turned = dot_nt(eye, gathered(seqs * (groups + g))).astype(BF16)
+        for q in range(group):
+            right_s[width * g : width * (g + 1), total * q : total * (q + 1)] = turned[
+                width * q : width * (q + 1), :
+            ]
     cov_s[...] = covariance_ref[...].astype(F32)
     for b in range(hidden):
-        span = slice(width * b, width * b + width)
-        right_s[span, :] = turn_s[pl.ds(b, width, stride=hidden), :].astype(BF16)
         span = slice(hidden * b, hidden * b + hidden)
         cov_bf_s[span, :] = cov_s[pl.ds(b, hidden, stride=hidden), :].astype(BF16)
+    weights = jnp.full((2 * chans, chans), 1.0 / chans, BF16)
+    block = iota((total, 128), 1) // hidden
     for g in range(groups):
-        left = gathered(seqs * g, seqs)
-        outer = dot(right_s[...], left)
-        columns = []
-        for p in range(hidden // group):
-            first = 128 * p
-            columns.append(
-                block_transpose(
-                    [outer[first + width * q : first + width * (q + 1), :] for q in range(group)],
-                    hidden,
+        left = gathered(seqs * g).astype(F32)
+        rolled = [left] + [pltpu.roll(left, hidden * d, 1) for d in range(1, group)]
+        for half in range(group // 2):
+            columns = []
+            for i in (2 * half, 2 * half + 1):
+                columns.append(
+                    jnp.concatenate(
+                        [
+                            jnp.where(block == q, rolled[(q - i) % group], 0.0).astype(BF16)
+                            for q in range(group)
+                        ],
+                        0,
+                    )
                 )
+            outer = dot(right_s[...], jnp.concatenate(columns, 1)).astype(BF16)
+            for k in range(2):
+                i = group * g + 2 * half + k
+                for c in range(chunks):
+                    flat_s[width * i : width * (i + 1), 128 * c : 128 * c + 128] = outer[
+                        width * c : width * (c + 1), 128 * k : 128 * k + 128
+                    ]
+    part = n * pairs // 2
+    spans = [slice(part * h, part * (h + 1)) for h in range(2)]
+    added = [dot(flat_s[span, :], cov_bf_s[...]) for span in spans]
+    mids = []
+    for h, span in enumerate(spans):
+        devices = range(n // 2 * h, n // 2 * (h + 1))
+        edge = jnp.concatenate([all_ref[d, :pairs, :] for d in devices], 0).astype(F32)
+        mids.append((edge + added[h] * (1.0 / total)).astype(BF16))
+        mid_s[span, :] = mids[h].astype(F32)
+    centers = [mid.astype(F32) - dot(mid, weights[:chans]) for mid in mids]
+    scales = [lax.rsqrt(average(c * c, weights) + EPSILON) for c in centers]
+    units = [c * scale for c, scale in zip(centers, scales)]
+    sides = [dot(unit.astype(BF16), edges_ref[...]) for unit in units]
+    for h, span in enumerate(spans):
+        scale_s[span, :] = scales[h]
+        unit_s[span, :] = units[h]
+        gate_s[span, :] = sides[h][:, 2 * chans :]
+        for d in range(n // 2):
+            g = n // 2 * h + d
+            mask = all_ref[g, 2 * pairs : 2 * pairs + width, :].astype(F32)
+            keep = jnp.concatenate(
+                [jnp.broadcast_to(mask[:, r : r + 1], (width, chans)) for r in range(own)], 0
             )
-        flat = jnp.concatenate(
-            [jnp.concatenate([c[i] for c in columns], 1) for i in range(group)], 0
-        )
-        high = flat.astype(BF16)
-        low = (flat - high.astype(F32)).astype(BF16)
-        added = (dot(high, cov_bf_s[...]) + dot(low, cov_bf_s[...])) * (1.0 / (seqs * n))
-        span = slice(pairs * g, pairs * (g + 1))
-        edge = all_ref[g, :pairs, :].astype(F32)
-        mid = (edge + added).astype(BF16).astype(F32)
-        mid_s[span, :] = mid
-        normed = standardize_features(mid).astype(BF16)
-        sides = dot(normed, edges_ref[:, : 2 * chans])
-        mask = all_ref[g, 2 * pairs : 2 * pairs + width, :].astype(F32)
-        keep = jnp.concatenate(
-            [jnp.broadcast_to(mask[:, r : r + 1], (width, chans)) for r in range(own)], 0
-        )
-        a_s[span, :] = (keep * sides[:, :chans]).astype(BF16).astype(F32)
-        b_s[span, :] = (keep * sides[:, chans:]).astype(BF16).astype(F32)
-        loss_s[span, :] = all_ref[g, pairs : 2 * pairs, :].astype(F32)
+            here = slice(pairs * d, pairs * (d + 1))
+            there = slice(pairs * g, pairs * (g + 1))
+            a_s[there, :] = (keep * sides[h][here, :chans]).astype(BF16).astype(F32)
+            b_s[there, :] = (keep * sides[h][here, chans : 2 * chans]).astype(BF16).astype(F32)
+            loss_s[there, :] = all_ref[g, pairs : 2 * pairs, :].astype(F32)
 
     rows = pl.ds(pl.multiple_of(me * pairs, pairs), pairs)
 
@@ -435,42 +486,45 @@
             0,
         )
 
-    mid = rows_and_columns(mid_s)
+    mid = mid_s[rows, :]
     loss = rows_and_columns(loss_s)
-    own_a_s[...] = a_s[rows, :]
-    own_b_s[...] = b_s[rows, :]
-    normed = standardize_features(mid).astype(BF16)
-    gating = jax.nn.sigmoid(dot(normed, edges_ref[:, 2 * chans :]))
-
-    def row(ref, r):
-        return jnp.broadcast_to(ref[r : r + 1, :], (width, chans))
-
-    acc = [jnp.zeros((width, chans), F32) for _ in range(2 * own)]
-    for k in range(width):
-        b_k = b_s[pl.ds(k, width, stride=width), :]
-        a_k = a_s[pl.ds(k, width, stride=width), :]
+    gating = jax.nn.sigmoid(rows_and_columns(gate_s))
+    tri = []
+    for fixed, moving in ((a_s, b_s), (b_s, a_s)):
+        held = fixed[rows, :]
         for r in range(own):
-            acc[r] = acc[r] + row(own_a_s, width * r + k) * b_k
-            acc[own + r] = acc[own + r] + row(own_b_s, width * r + k) * a_k
-    tri = jnp.concatenate(acc, 0)
-    center = tri - jnp.mean(tri, -1, keepdims=True)
-    scale_inv = lax.rsqrt(jnp.mean(center * center, -1, keepdims=True) + EPSILON)
+            mine = [held[width * r + 8 * v : width * r + 8 * v + 8] for v in range(width // 8)]
+            for j in range(0, width, 8):
+                parts = []
+                for jj in range(j, j + 8):
+                    prods = [
+                        mine[v] * moving[width * jj + 8 * v : width * jj + 8 * v + 8, :]
+                        for v in range(width // 8)
+                    ]
+                    parts.append(functools.reduce(jnp.add, prods))
+                tri.append(merge_rows(parts))
+    tri = jnp.concatenate(tri, 0)
+    center, scale_inv = center_and_scale(tri, weights)
     unit = center * scale_inv
     update = dot(unit[:pairs].astype(BF16), cycle_ref[...])
-    out_ref[...] = (mid[:pairs] + gating[:pairs] * update).astype(BF16)
+    out_ref[...] = (mid + gating[:pairs] * update).astype(BF16)
     grad_normed = dot_nt((loss * gating).astype(BF16), cycle_ref[...])
     tri_s[...] = (
         (
             scale_inv
             * (
                 grad_normed
-                - jnp.mean(grad_normed, -1, keepdims=True)
-                - unit * jnp.mean(grad_normed * unit, -1, keepdims=True)
+                - average(grad_normed, weights)
+                - unit * average(grad_normed * unit, weights)
             )
         )
         .astype(BF16)
         .astype(F32)
     )
+
+    def row(ref, r):
+        return jnp.broadcast_to(ref[r : r + 1, :], (width, chans))
+
     acc = [jnp.zeros((width, chans), F32) for _ in range(2 * own)]
     for j in range(width):
         span = slice(width * j, width * j + width)
@@ -494,7 +548,11 @@
         1,
     ).astype(BF16)
     grad_input = dot_nt(grad_proj, edges_ref[...])
-    grad_ref[...] = loss[:pairs] + norm_back(mid[:pairs], grad_input)
+    scale_inv = scale_s[rows, :]
+    unit = unit_s[rows, :]
+    grad_ref[...] = loss[:pairs] + scale_inv * (
+        grad_input - average(grad_input, weights) - unit * average(grad_input * unit, weights)
+    )
 
 
 def body_resident(
@@ -539,8 +597,11 @@
         scratch_shapes=[pltpu.VMEM((seqs * width, depth), BF16)] * 3
         + [
             pltpu.VMEM((seqs * width, 128), BF16),
-            pltpu.VMEM((seqs * width * depth // 128, 128), F32),
+            pltpu.VMEM((seqs * width, 128), F32),
+            pltpu.VMEM((seqs * width * hidden // 128, 128), F32),
+            pltpu.VMEM((seqs * width * hidden // 128, 128), F32),
         ],
+        compiler_params=pltpu.CompilerParams(vmem_limit_bytes=16 << 20),
         name="row_attention",
     )(
         family_matrix.reshape(seqs * width, depth),
@@ -559,18 +620,20 @@
         in_specs=[vmem] * 5,
         out_specs=(vmem, vmem),
         scratch_shapes=[
-            pltpu.VMEM((hidden * width, 128), F32),
-            pltpu.VMEM((hidden * width, 128), BF16),
+            pltpu.VMEM((width * hidden * hidden // 128, 128 // hidden * 128), BF16),
             pltpu.VMEM((hidden * hidden, chans), F32),
             pltpu.VMEM((hidden * hidden, chans), BF16),
+            pltpu.VMEM((every, hidden * hidden), BF16),
             pltpu.VMEM((every, chans), F32),
             pltpu.VMEM((every, chans), F32),
             pltpu.VMEM((every, chans), F32),
             pltpu.VMEM((every, chans), F32),
-            pltpu.VMEM((pairs, chans), F32),
-            pltpu.VMEM((pairs, chans), F32),
+            pltpu.VMEM((every, chans), F32),
+            pltpu.VMEM((every, chans), F32),
+            pltpu.VMEM((every, chans), F32),
             pltpu.VMEM((2 * pairs, chans), F32),
         ],
+        compiler_params=pltpu.CompilerParams(vmem_limit_bytes=16 << 20),
         name="pair_update",
     )(gathered, packed_all, covariance_merge_matrix, edges_gate_factor_matrix, cycle_merge_matrix)
     return (

time: 43.5 us -> 33 us (0.76)
  Pallas kernels: 18.2 us -> 9.55 us
  blocking collectives: 24.3 us -> 21.7 us
  local copies, waits for them, and re-layouts: 0 us -> 0.92 us
    pallas_call x1, Pallas kernels: 11.4 us -> 4.8 us  [body_resident(): pl.pallas_call(functools.partial(pair_kernel, 'dap', width, own, hidden,...]
    pallas_call x1, Pallas kernels: 4.91 us -> 2.78 us  [body_resident(): pl.pallas_call(functools.partial(attention_kernel, width, heads, own), ou...]
    all_gather x1, blocking collectives: 13.5 us -> 12 us  [body_resident(): packed_all = lax.all_gather(packed, 'dap', axis=0, tiled=False)]
    all_gather x1, blocking collectives: 10.8 us -> 9.63 us  [body_resident(): gathered = lax.all_gather(send, 'dap', axis=0, tiled=False)]
    unnamed x0 -> x14, local copies, waits for them, and re-layouts: none -> 0.92 us
where the time goes in v3:
time: 33 us; the launch traced here: 32.8 us
  blocking collectives  21.7 us (66%)
  Pallas kernels  9.55 us (29%)
  local copies, waits for them, and re-layouts  0.92 us (3%)
  between operations  0.65 us (2%)
    all_gather x1, blocking collectives, body_resident(): packed_all = lax.all_gather(packed, 'dap', axis=0, tiled=False)  12 us
    all_gather x1, blocking collectives, body_resident(): gathered = lax.all_gather(send, 'dap', axis=0, tiled=False)  9.63 us
    pallas_call x1, Pallas kernels, body_resident(): pl.pallas_call(functools.partial(pair_kernel, 'dap', width, own, hidden,...  4.8 us
    pallas_call x1, Pallas kernels, body_resident(): pl.pallas_call(functools.partial(attention_kernel, width, heads, own), ou...  2.78 us
    pallas_call x1, Pallas kernels, body_resident(): pl.pallas_call(functools.partial(pack_kernel, width), out_shape=jax.Shape...  1.97 us
    unnamed x14, local copies, waits for them, and re-layouts  0.92 us

profile of v3, /device:TPU:0, one launch (start us, length us, event | category | flops | bytes accessed | tf_op | source)
XLA Modules:
  0.0 32.8 jit_solution(9515457743564641223)
XLA Ops:
  0.6 0.0 copy-start
  0.6 2.0 %pack_pairs.1 = bf16[304,128]{1,0:T(8,128)(2,1)} custom-call(bf16[128,128]{1,0:T(8,128)(2,1)} %bitcast.15, bf16[8,128]{1,0:T(8,128)(2,1)} %bitcast.17, bf16[128,128]{1,0:T(8,128)(2,1)} %bitcast.16, s32[4,32]{1,0:T(4,128)} %mask_ref.1), custom_call_target="tpu_custom_call" | custom-call | tf_op jit(solution)/shard_map/pack_pairs/pallas_call | solution.py:580
  2.6 0.0 copy-start.1
  2.6 0.0 copy-start.5
  2.6 12.0 %all-gather = bf16[2432,128]{1,0:T(8,128)(2,1)S(1)} all-gather(bf16[304,128]{1,0:T(8,128)(2,1)} %pack_pairs.1), channel_id=2, replica_groups=mesh['dap'=8,'dp'=4] {'dap'}, dimensions={0}, use_global_device_ids=true | all-gather | bytes 700416 | tf_op jit(solution)/shard_map/all_gather | solution.py:588
  14.7 0.0 copy-done
  14.7 0.0 copy-done.1
  14.7 0.0 copy-done.5
  14.7 0.0 copy-start.3
  14.7 0.9 %copy-done.3 = bf16[256,256]{1,0:T(8,128)(2,1)S(1)} copy-done((bf16[256,256]{1,0:T(8,128)(2,1)S(1)}, bf16[256,256]{1,0:T(8,128)(2,1)}, u32[]{:S(2)}) %copy-start.3) | copy-done | bytes 131096
  15.6 2.8 %row_attention.1 = (bf16[512,256]{1,0:T(8,128)(2,1)}, bf16[256,128]{1,0:T(8,128)(2,1)S(1)}) custom-call(bf16[512,256]{1,0:T(8,128)(2,1)S(1)} %bitcast.13, bf16[8,304,128]{2,1,0:T(8,128)(2,1)S(1)} %bitcast.10, bf16[256,1024]{1,0:T(8,128)(2,1)S(1)} %copy-done, bf16[256,256]{1,0:T(8,128)(2,1)S(1)} %copy-done.3, bf16[64,256]{1,0:T(8,128)(2,1)S(1)} %bitcast.14), custom_call_target="tpu_custom_call" | custom-call | tf_op jit(solution)/shard_map/row_attention/pallas_call | solution.py:589
  18.3 0.0 copy-start.2
  18.4 0.0 copy-start.4
  18.4 0.0 copy-start.6
  18.4 9.6 %all-gather.1 = bf16[2048,128]{1,0:T(8,128)(2,1)S(1)} all-gather(bf16[256,128]{1,0:T(8,128)(2,1)S(1)} %get-tuple-element.8), channel_id=3, replica_groups=mesh['dap'=8,'dp'=4] {'dap'}, dimensions={0}, use_global_device_ids=true | all-gather | bytes 589824 | tf_op jit(solution)/shard_map/all_gather | solution.py:613
  28.0 0.0 copy-done.2
  28.0 0.0 copy-done.4
  28.0 0.0 copy-done.6
  28.0 4.8 %pair_update.1 = (bf16[128,128]{1,0:T(8,128)(2,1)}, f32[128,128]{1,0:T(8,128)}) custom-call(bf16[8,256,128]{2,1,0:T(8,128)(2,1)S(1)} %bitcast.12, bf16[8,304,128]{2,1,0:T(8,128)(2,1)S(1)} %bitcast.11, bf16[1024,128]{1,0:T(8,128)(2,1)S(1)} %copy-done.2, bf16[128,384]{1,0:T(8,128)(2,1)S(1)} %copy-done.4, bf16[128,128]{1,0:T(8,128)(2,1)S(1)} %copy-done.6), custom_call_target="tpu_custom_call" | custom-call | tf_op jit(solution)/shard_map/pair_update/pallas_call | solution.py:614
Async XLA Ops:
  0.6 14.0 %copy-start = (bf16[256,1024]{1,0:T(8,128)(2,1)S(1)}, bf16[256,1024]{1,0:T(8,128)(2,1)}, u32[]{:S(2)}) copy-start(bf16[256,1024]{1,0:T(8,128)(2,1)} %project_ref.1) | copy-start | bytes 1572868
  2.6 12.0 %copy-start.1 = (bf16[16,32,256]{2,1,0:T(8,128)(2,1)S(1)}, bf16[16,32,256]{2,1,0:T(8,128)(2,1)}, u32[]{:S(2)}) copy-start(bf16[16,32,256]{2,1,0:T(8,128)(2,1)} %param.11) | copy-start | bytes 786436
  2.6 12.0 %copy-start.5 = (bf16[256,64]{0,1:T(8,128)(2,1)S(1)}, bf16[256,64]{0,1:T(8,128)(2,1)}, u32[]{:S(2)}) copy-start(bf16[256,64]{0,1:T(8,128)(2,1)} %param.17) | copy-start | bytes 98308
  14.7 0.9 %copy-start.3 = (bf16[256,256]{1,0:T(8,128)(2,1)S(1)}, bf16[256,256]{1,0:T(8,128)(2,1)}, u32[]{:S(2)}) copy-start(bf16[256,256]{1,0:T(8,128)(2,1)} %merge_ref.1) | copy-start | bytes 393220
  18.3 9.6 %copy-start.2 = (bf16[1024,128]{1,0:T(8,128)(2,1)S(1)}, bf16[1024,128]{1,0:T(8,128)(2,1)}, u32[]{:S(2)}) copy-start(bf16[1024,128]{1,0:T(8,128)(2,1)} %covariance_ref.1) | copy-start | bytes 786436
  18.4 9.6 %copy-start.4 = (bf16[128,384]{1,0:T(8,128)(2,1)S(1)}, bf16[128,384]{1,0:T(8,128)(2,1)}, u32[]{:S(2)}) copy-start(bf16[128,384]{1,0:T(8,128)(2,1)} %edges_ref.1) | copy-start | bytes 294916
  18.4 9.6 %copy-start.6 = (bf16[128,128]{1,0:T(8,128)(2,1)S(1)}, bf16[128,128]{1,0:T(8,128)(2,1)}, u32[]{:S(2)}) copy-start(bf16[128,128]{1,0:T(8,128)(2,1)} %cycle_ref.1) | copy-start | bytes 98308

commit v4 on v3

--- a/solution.py
+++ b/solution.py
@@ -212,98 +212,150 @@
     return lax.broadcasted_iota(jnp.int32, shape, dim)
 
 
-def pack_kernel(width, edge_ref, weight_ref, loss_ref, mask_ref, send_ref, mask_s):
-    rows, chans = edge_ref.shape
-    heads = weight_ref.shape[0]
+def pack_kernel(
+    width, edge_ref, weight_ref, loss_ref, mask_ref, send_ref, edge_s, weight_s, loss_s, mask_s,
+    tile_s, sems
+):
+    copies = [
+        pltpu.make_async_copy(source, target, sems.at[k])
+        for k, (source, target) in enumerate(
+            (
+                (edge_ref, edge_s),
+                (weight_ref, weight_s),
+                (loss_ref, loss_s),
+                (mask_ref, mask_s),
+            )
+        )
+    ]
+    for copy in copies:
+        copy.start()
+    for copy in copies:
+        copy.wait()
+    rows, chans = edge_s.shape
+    heads = weight_s.shape[0]
     own = rows // width
     lanes = heads * width
-    send_ref[:rows, :] = edge_ref[...]
-    send_ref[rows : 2 * rows, :] = loss_ref[...]
-    mask_s[...] = jnp.zeros(mask_s.shape, F32)
-    mask_s[:own, :] = mask_ref[...].astype(F32)
-    eye = (iota((width, width), 0) == iota((width, width), 1)).astype(F32).astype(BF16)
-    base = 2 * rows
-    send_ref[base : base + width, :] = dot_nt(eye, mask_s[...].astype(BF16)).astype(BF16)
-    normed = standardize_features(edge_ref[...].astype(F32)).astype(BF16)
+    peers = width // own
+    tile_s[...] = jnp.zeros(tile_s.shape, F32)
+    tile_s[2 * own : 3 * own, :width] = mask_s[...].astype(F32)
+    normed = standardize_features(edge_s[...].astype(F32)).astype(BF16)
     spread = (iota((heads, lanes), 0) == iota((heads, lanes), 1) // width).astype(F32)
     weight = lax.dot_general(
-        weight_ref[...], spread.astype(BF16), (((0,), (0,)), ((), ())), preferred_element_type=F32
+        weight_s[...], spread.astype(BF16), (((0,), (0,)), ((), ())), preferred_element_type=F32
     ).astype(BF16)
     every = dot(normed, weight)
     keep = iota((rows, lanes), 0) % width == iota((rows, lanes), 1) % width
     picked = jnp.where(keep, every, 0.0).astype(BF16)
-    packed = jnp.zeros((16, 128), F32)
+    packed = tile_s[...]
     for t in range(lanes // 128):
-        place = iota((16, rows), 0) == 8 * t + iota((16, rows), 1) // width
+        place = iota((16, rows), 0) == own * t + iota((16, rows), 1) // width
         packed = packed + dot(
             place.astype(F32).astype(BF16), picked[:, 128 * t : 128 * t + 128]
         )
-    send_ref[base + width :, :] = packed.astype(BF16)
+    packed = packed.astype(BF16)
+    goal = iota((rows, rows), 0)
+    source = goal % own * width + goal // (own * own) * own + goal // own % own
+    place = (source == iota((rows, rows), 1)).astype(F32).astype(BF16)
+    losses = dot(place, loss_s[...]).astype(BF16)
+    for e in range(peers):
+        send_ref[32 * e : 32 * e + 16, :] = packed
+        send_ref[32 * e + 16 : 32 * e + 32, :] = losses[16 * e : 16 * e + 16]
+
+
+def project_kernel(
+    width,
+    heads,
+    hidden,
+    family_ref,
+    project_ref,
+    covariance_ref,
+    logits_ref,
+    value_ref,
+    gating_ref,
+    cov_ref,
+    query_s,
+    key_s,
+    cov_s,
+):
+    rows, depth = family_ref.shape
+    seqs = rows // width
+    group = 128 // width
+    normed = standardize_features(family_ref[...].astype(F32)).astype(BF16)
+    query_s[...] = dot(normed, project_ref[:, :depth]).astype(BF16)
+    key_s[...] = dot(normed, project_ref[:, depth : 2 * depth]).astype(BF16)
+    value_ref[...] = dot(normed, project_ref[:, 2 * depth : 3 * depth]).astype(BF16)
+    gating_ref[...] = jax.nn.sigmoid(dot(normed, project_ref[:, 3 * depth :]))
+    same = (iota((128, 128), 0) // width == iota((128, 128), 1) // width).astype(F32).astype(BF16)
+    scale = 1.0 / math.sqrt(depth // heads)
+    for t in range(depth // 128):
+        cols = slice(128 * t, 128 * t + 128)
+        for s in range(seqs):
+            span = slice(width * s, width * s + width)
+            keys = jnp.concatenate([key_s[span, cols]] * group, 0) * same
+            logits_ref[span, cols] = dot_nt(query_s[span, cols], keys) * scale
+    cov_s[...] = covariance_ref[...].astype(F32)
+    for b in range(hidden):
+        span = slice(hidden * b, hidden * b + hidden)
+        cov_ref[span, :] = cov_s[pl.ds(b, hidden, stride=hidden), :].astype(BF16)
 
 
 def attention_kernel(
     width,
-    heads,
     own,
     family_ref,
-    all_ref,
-    project_ref,
+    got_ref,
+    logits_ref,
+    value_ref,
+    gating_ref,
     merge_ref,
     factor_ref,
+    edge_ref,
     family_out_ref,
     send_ref,
-    query_s,
-    key_s,
-    value_s,
+    after_s,
     weight_s,
     row_s,
     turn_s,
     line_s,
+    sem,
 ):
     rows, depth = family_ref.shape
     seqs = rows // width
     tiles = depth // 128
     group = 128 // width
-    source = family_ref[...].astype(F32)
-    normed = standardize_features(source).astype(BF16)
-    query_s[...] = dot(normed, project_ref[:, :depth]).astype(BF16)
-    key_s[...] = dot(normed, project_ref[:, depth : 2 * depth]).astype(BF16)
-    value_s[...] = dot(normed, project_ref[:, 2 * depth : 3 * depth]).astype(BF16)
-    gating = jax.nn.sigmoid(dot(normed, project_ref[:, 3 * depth :]))
     same = (iota((128, 128), 0) // width == iota((128, 128), 1) // width).astype(F32).astype(BF16)
     lane_group = iota((rows, 128), 1) // width
-    scale = 1.0 / math.sqrt(depth // heads)
+    biases = jnp.concatenate([got_ref[d, :16, :] for d in range(got_ref.shape[0])], 0)
     gated = []
-    base = all_ref.shape[1] - 16
-    biases = jnp.concatenate([all_ref[d, base:, :] for d in range(all_ref.shape[0])], 0)
     for t in range(tiles):
         cols = slice(128 * t, 128 * t + 128)
         row = iota((width, biases.shape[0]), 0)
-        take = iota((width, biases.shape[0]), 1) == 16 * (row // own) + 8 * t + row % own
+        take = iota((width, biases.shape[0]), 1) == 16 * (row // own) + own * t + row % own
         bias = dot(take.astype(F32).astype(BF16), biases)
-        parts = []
-        for s in range(seqs):
-            span = slice(width * s, width * s + width)
-            keys = jnp.concatenate([key_s[span, cols]] * group, 0) * same
-            parts.append(dot_nt(query_s[span, cols], keys) * scale + bias)
-        logits = jnp.concatenate(parts, 0)
+        logits = jnp.concatenate(
+            [logits_ref[width * s : width * (s + 1), cols] + bias for s in range(seqs)], 0
+        )
         top = jnp.full(logits.shape, -jnp.inf, F32)
         for h in range(group):
             best = jnp.max(
                 jnp.where(lane_group == h, logits, -jnp.inf), axis=-1, keepdims=True
             )
             top = jnp.where(lane_group == h, best, top)
-        weight_s[...] = jnp.exp(logits - top).astype(BF16)
-        total = dot(weight_s[...], same)
+        weight_s[:, cols] = jnp.exp(logits - top).astype(BF16)
+        total = dot(weight_s[:, cols], same)
         parts = []
         for s in range(seqs):
             span = slice(width * s, width * s + width)
-            values = jnp.concatenate([value_s[span, cols]] * group, 0) * same
-            parts.append(dot(weight_s[span, :], values))
+            values = jnp.concatenate([value_ref[span, cols]] * group, 0) * same
+            parts.append(dot(weight_s[span, cols], values))
         mixed = jnp.concatenate(parts, 0) / total
-        gated.append((gating[:, cols] * mixed).astype(BF16))
-    after = (source + dot(jnp.concatenate(gated, 1), merge_ref[...])).astype(BF16)
-    family_out_ref[...] = after
+        gated.append((gating_ref[:, cols] * mixed).astype(BF16))
+    after = (
+        family_ref[...].astype(F32) + dot(jnp.concatenate(gated, 1), merge_ref[...])
+    ).astype(BF16)
+    after_s[...] = after
+    leave = pltpu.make_async_copy(after_s, family_out_ref, sem)
+    leave.start()
     ready = standardize_features(after.astype(F32)).astype(BF16)
     hidden = factor_ref.shape[0] // 2
     groups = width // group
@@ -333,6 +385,8 @@
         send_ref[base + seqs * g : base + seqs * (g + 1), :] = line_s[
             pl.ds(g, seqs, stride=chunks), :
         ].astype(BF16)
+    send_ref[2 * base :, :] = edge_ref[...]
+    leave.wait()
 
 
 def block_transpose(blocks, step):
@@ -383,15 +437,14 @@
     hidden,
     seqs,
     sides_ref,
-    all_ref,
+    got_ref,
+    own_loss_ref,
     covariance_ref,
     edges_ref,
     cycle_ref,
     out_ref,
     grad_ref,
     right_s,
-    cov_s,
-    cov_bf_s,
     flat_s,
     mid_s,
     unit_s,
@@ -399,17 +452,17 @@
     gate_s,
     a_s,
     b_s,
-    loss_s,
     tri_s,
 ):
     me = lax.axis_index(axis)
-    n = all_ref.shape[0]
+    n = sides_ref.shape[0]
     group = 128 // hidden
     groups = width // group
     chunks = hidden // group
     pairs = own * width
     chans = 128
     total = seqs * n
+    base = 2 * seqs * groups
 
     def gathered(first):
         return jnp.concatenate([sides_ref[d, first : first + seqs, :] for d in range(n)], 0)
@@ -421,10 +474,6 @@
             right_s[width * g : width * (g + 1), total * q : total * (q + 1)] = turned[
                 width * q : width * (q + 1), :
             ]
-    cov_s[...] = covariance_ref[...].astype(F32)
-    for b in range(hidden):
-        span = slice(hidden * b, hidden * b + hidden)
-        cov_bf_s[span, :] = cov_s[pl.ds(b, hidden, stride=hidden), :].astype(BF16)
     weights = jnp.full((2 * chans, chans), 1.0 / chans, BF16)
     block = iota((total, 128), 1) // hidden
     for g in range(groups):
@@ -451,11 +500,24 @@
                     ]
     part = n * pairs // 2
     spans = [slice(part * h, part * (h + 1)) for h in range(2)]
-    added = [dot(flat_s[span, :], cov_bf_s[...]) for span in spans]
+    tiles = jnp.concatenate([got_ref[d, :16, :] for d in range(n)], 0)
+    pick = (iota((width, 128), 0) == iota((width, 128), 1)).astype(F32).astype(BF16)
+    masks = dot_nt(pick, tiles)
+
+    def kept(columns, first):
+        return jnp.concatenate(
+            [
+                jnp.broadcast_to(columns[:, first + r : first + r + 1], (width, chans))
+                for r in range(own)
+            ],
+            0,
+        )
+
+    added = [dot(flat_s[span, :], covariance_ref[...]) for span in spans]
     mids = []
     for h, span in enumerate(spans):
         devices = range(n // 2 * h, n // 2 * (h + 1))
-        edge = jnp.concatenate([all_ref[d, :pairs, :] for d in devices], 0).astype(F32)
+        edge = jnp.concatenate([sides_ref[d, base:, :] for d in devices], 0).astype(F32)
         mids.append((edge + added[h] * (1.0 / total)).astype(BF16))
         mid_s[span, :] = mids[h].astype(F32)
     centers = [mid.astype(F32) - dot(mid, weights[:chans]) for mid in mids]
@@ -468,15 +530,11 @@
         gate_s[span, :] = sides[h][:, 2 * chans :]
         for d in range(n // 2):
             g = n // 2 * h + d
-            mask = all_ref[g, 2 * pairs : 2 * pairs + width, :].astype(F32)
-            keep = jnp.concatenate(
-                [jnp.broadcast_to(mask[:, r : r + 1], (width, chans)) for r in range(own)], 0
-            )
+            keep = kept(masks, 16 * g + 2 * own)
             here = slice(pairs * d, pairs * (d + 1))
             there = slice(pairs * g, pairs * (g + 1))
             a_s[there, :] = (keep * sides[h][here, :chans]).astype(BF16).astype(F32)
             b_s[there, :] = (keep * sides[h][here, chans : 2 * chans]).astype(BF16).astype(F32)
-            loss_s[there, :] = all_ref[g, pairs : 2 * pairs, :].astype(F32)
 
     rows = pl.ds(pl.multiple_of(me * pairs, pairs), pairs)
 
@@ -487,7 +545,11 @@
         )
 
     mid = mid_s[rows, :]
-    loss = rows_and_columns(loss_s)
+    losses = jnp.concatenate([got_ref[d, 16:, :] for d in range(n)], 0)
+    goal = iota((pairs, pairs), 0)
+    source = goal % width // own * 16 + goal // width * own + goal % own
+    place = (source == iota((pairs, pairs), 1)).astype(F32).astype(BF16)
+    loss = jnp.concatenate([own_loss_ref[...].astype(F32), dot(place, losses)], 0)
     gating = jax.nn.sigmoid(rows_and_columns(gate_s))
     tri = []
     for fixed, moving in ((a_s, b_s), (b_s, a_s)):
@@ -533,10 +595,7 @@
         for r in range(own):
             acc[r] = acc[r] + row(tri_s, width * r + j) * b_j
             acc[own + r] = acc[own + r] + row(tri_s, pairs + width * r + j) * a_j
-    mask = all_ref[me, 2 * pairs : 2 * pairs + width, :].astype(F32)
-    keep = jnp.concatenate(
-        [jnp.broadcast_to(mask[:, r : r + 1], (width, chans)) for r in range(own)], 0
-    )
+    keep = kept(dot_nt(pick, got_ref[me, :16, :]), 2 * own)
     gate_own = gating[:pairs]
     grad_gate = loss[:pairs] * update * gate_own * (1.0 - gate_own)
     grad_proj = jnp.concatenate(
@@ -577,39 +636,67 @@
     edge = edge_matrix.reshape(pairs, chans)
     loss = loss_sensitivity.reshape(pairs, chans)
     vmem = pl.BlockSpec(memory_space=pltpu.VMEM)
+    hbm = pl.BlockSpec(memory_space=pltpu.HBM)
+    family = family_matrix.reshape(seqs * width, depth)
+    factor = left_right_factor_matrix.T
+    sided = 2 * seqs * width * hidden // 128
+    peers = width // own
     packed = pl.pallas_call(
         functools.partial(pack_kernel, width),
-        out_shape=jax.ShapeDtypeStruct((2 * pairs + width + 16, chans), BF16),
-        in_specs=[vmem] * 4,
+        out_shape=jax.ShapeDtypeStruct((32 * peers, chans), BF16),
+        in_specs=[hbm] * 4,
         out_specs=vmem,
-        scratch_shapes=[pltpu.VMEM((128, width), F32)],
+        scratch_shapes=[
+            pltpu.VMEM((pairs, chans), BF16),
+            pltpu.VMEM((heads, chans), BF16),
+            pltpu.VMEM((pairs, chans), BF16),
+            pltpu.VMEM((own, width), jnp.int32),
+            pltpu.VMEM((16, 128), F32),
+            pltpu.SemaphoreType.DMA((4,)),
+        ],
         name="pack_pairs",
     )(edge, logit_offset_matrix.T, loss, edge_validity)
-    packed_all = lax.all_gather(packed, "dap", axis=0, tiled=False)
+    got = lax.all_to_all(packed, "dap", split_axis=0, concat_axis=0, tiled=True)
+    got = got.reshape(peers, 32, chans)
+    logits, value, gating, covariance = pl.pallas_call(
+        functools.partial(project_kernel, width, heads, hidden),
+        out_shape=(
+            jax.ShapeDtypeStruct((seqs * width, depth), F32),
+            jax.ShapeDtypeStruct((seqs * width, depth), BF16),
+            jax.ShapeDtypeStruct((seqs * width, depth), F32),
+            jax.ShapeDtypeStruct((hidden * hidden, chans), BF16),
+        ),
+        in_specs=[vmem] * 3,
+        out_specs=(vmem,) * 4,
+        scratch_shapes=[pltpu.VMEM((seqs * width, depth), BF16)] * 2
+        + [pltpu.VMEM((hidden * hidden, chans), F32)],
+        compiler_params=pltpu.CompilerParams(vmem_limit_bytes=16 << 20),
+        cost_estimate=pl.CostEstimate(
+            flops=16 * seqs * width * depth * depth,
+            bytes_accessed=32 * seqs * width * depth,
+            transcendentals=seqs * width * depth,
+        ),
+        name="project_family",
+    )(family, query_key_value_gate_matrix, covariance_merge_matrix)
     family_out, send = pl.pallas_call(
-        functools.partial(attention_kernel, width, heads, own),
+        functools.partial(attention_kernel, width, own),
         out_shape=(
             jax.ShapeDtypeStruct((seqs * width, depth), BF16),
-            jax.ShapeDtypeStruct((2 * seqs * width * hidden // 128, 128), BF16),
+            jax.ShapeDtypeStruct((sided + pairs, 128), BF16),
         ),
-        in_specs=[vmem] * 5,
-        out_specs=(vmem, vmem),
-        scratch_shapes=[pltpu.VMEM((seqs * width, depth), BF16)] * 3
-        + [
-            pltpu.VMEM((seqs * width, 128), BF16),
+        in_specs=[vmem] * 8,
+        out_specs=(hbm, vmem),
+        scratch_shapes=[
+            pltpu.VMEM((seqs * width, depth), BF16),
+            pltpu.VMEM((seqs * width, depth), BF16),
             pltpu.VMEM((seqs * width, 128), F32),
             pltpu.VMEM((seqs * width * hidden // 128, 128), F32),
             pltpu.VMEM((seqs * width * hidden // 128, 128), F32),
+            pltpu.SemaphoreType.DMA(()),
         ],
         compiler_params=pltpu.CompilerParams(vmem_limit_bytes=16 << 20),
         name="row_attention",
-    )(
-        family_matrix.reshape(seqs * width, depth),
-        packed_all,
-        query_key_value_gate_matrix,
-        heads_merge_matrix,
-        left_right_factor_matrix.T,
-    )
+    )(family, got, logits, value, gating, heads_merge_matrix, factor, edge)
     gathered = lax.all_gather(send, "dap", axis=0, tiled=False)
     pair_out, pair_grad = pl.pallas_call(
         functools.partial(pair_kernel, "dap", width, own, hidden, seqs),
@@ -617,14 +704,11 @@
             jax.ShapeDtypeStruct((pairs, chans), BF16),
             jax.ShapeDtypeStruct((pairs, chans), F32),
         ),
-        in_specs=[vmem] * 5,
+        in_specs=[vmem] * 6,
         out_specs=(vmem, vmem),
         scratch_shapes=[
             pltpu.VMEM((width * hidden * hidden // 128, 128 // hidden * 128), BF16),
-            pltpu.VMEM((hidden * hidden, chans), F32),
-            pltpu.VMEM((hidden * hidden, chans), BF16),
             pltpu.VMEM((every, hidden * hidden), BF16),
-            pltpu.VMEM((every, chans), F32),
             pltpu.VMEM((every, chans), F32),
             pltpu.VMEM((every, chans), F32),
             pltpu.VMEM((every, chans), F32),
@@ -635,7 +719,7 @@
         ],
         compiler_params=pltpu.CompilerParams(vmem_limit_bytes=16 << 20),
         name="pair_update",
-    )(gathered, packed_all, covariance_merge_matrix, edges_gate_factor_matrix, cycle_merge_matrix)
+    )(gathered, got, loss, covariance, edges_gate_factor_matrix, cycle_merge_matrix)
     return (
         family_out.reshape(seqs, width, depth),
         pair_out.reshape(own, width, chans),

time: 33 us -> 29.8 us (0.903)
  blocking collectives: 21.7 us -> 9.59 us
  starting transfers between devices: 0 us -> 5.18 us
  waiting for transfers between devices: 0 us -> 1.58 us
  local copies, waits for them, and re-layouts: 0.92 us -> 2.02 us
  Pallas kernels: 9.55 us -> 10.3 us
    all_gather x1 -> x0, blocking collectives: 12 us -> none  [body_resident(): packed_all = lax.all_gather(packed, 'dap', axis=0, tiled=False)]
    all_to_all x0 -> x1, starting transfers between devices: none -> 5.18 us  [body_resident(): got = lax.all_to_all(packed, 'dap', split_axis=0, concat_axis=0, tiled=True)]
    all_to_all x0 -> x1, waiting for transfers between devices: none -> 1.58 us  [body_resident(): got = lax.all_to_all(packed, 'dap', split_axis=0, concat_axis=0, tiled=True)]
    unnamed x14 -> x18, local copies, waits for them, and re-layouts: 0.92 us -> 2.02 us
    pallas_call x1 -> x2, Pallas kernels: 2.78 us -> 3.63 us  [the longest x1 2.2 us: body_resident(): pl.pallas_call(functools.partial(attention_kernel, width, own), out_shape...]
  transfers between devices with their start and end apart: 0 -> 1, of which waited for: 0 -> 1; matrix products, arithmetic and copies ran while one was open for 0% -> 0% of each run, Pallas kernels for 0% -> 5%
where the time goes in v4:
time: 29.8 us; the launch traced here: 29.4 us
  Pallas kernels  10.3 us (35%)
  blocking collectives  9.59 us (32%)
  starting transfers between devices  5.18 us (17%)
  local copies, waits for them, and re-layouts  2.02 us (7%)
  waiting for transfers between devices  1.58 us (5%)
  between operations  0.71 us (2%)
    all_gather x1, blocking collectives, body_resident(): gathered = lax.all_gather(send, 'dap', axis=0, tiled=False)  9.59 us
    all_to_all x1, starting transfers between devices, body_resident(): got = lax.all_to_all(packed, 'dap', split_axis=0, concat_axis=0, tiled=True)  5.18 us
    pallas_call x1, Pallas kernels, body_resident(): pl.pallas_call(functools.partial(pair_kernel, 'dap', width, own, hidden,...  4.73 us
    pallas_call x1, Pallas kernels, body_resident(): pl.pallas_call(functools.partial(attention_kernel, width, own), out_shape...  2.2 us
    unnamed x18, local copies, waits for them, and re-layouts  2.02 us
    pallas_call x1, Pallas kernels, body_resident(): pl.pallas_call(functools.partial(pack_kernel, width), out_shape=jax.Shape...  1.99 us
    all_to_all x1, waiting for transfers between devices, body_resident(): got = lax.all_to_all(packed, 'dap', split_axis=0, concat_axis=0, tiled=True)  1.58 us
    pallas_call x1, Pallas kernels, body_resident(): pl.pallas_call(functools.partial(project_kernel, width, heads, hidden), o...  1.43 us
  transfers between devices with their start and end apart: 1, of which 1 were waited for; matrix products, arithmetic and copies ran while one was open for 0% of the time, Pallas kernels for 5%

profile of v4, /device:TPU:0, one launch (start us, length us, event | category | flops | bytes accessed | tf_op | source)
XLA Modules:
  0.0 29.4 jit_solution(6140500639610795178)
XLA Ops:
  0.6 0.0 copy-start
  0.6 2.0 %pack_pairs.1 = bf16[256,128]{1,0:T(8,128)(2,1)} custom-call(bf16[128,128]{1,0:T(8,128)(2,1)} %bitcast.13, bf16[8,128]{1,0:T(8,128)(2,1)} %bitcast.19, bf16[128,128]{1,0:T(8,128)(2,1)} %bitcast.15, s32[4,32]{1,0:T(4,128)} %mask_ref.1), custom_call_target="tpu_custom_call" | custom-call | tf_op jit(solution)/shard_map/pack_pairs/pallas_call | solution.py:644
  2.6 5.2 %all-to-all-start = ((bf16[8,32,128]{2,1,0:T(8,128)(2,1)}), bf16[8,32,128]{2,1,0:T(8,128)(2,1)S(1)}, u32[]{:S(2)}, u32[]{:S(2)}) async-start(bf16[8,32,128]{2,1,0:T(8,128)(2,1)} %bitcast.18), calls=%async_computation | async-start | bytes 131072 | tf_op jit(solution)/shard_map/all_to_all | solution.py:659
  7.8 0.0 copy-done
  7.8 0.0 copy-start.7
  7.8 1.0 %copy-done.7 = bf16[256,1024]{1,0:T(8,128)(2,1)S(1)} copy-done((bf16[256,1024]{1,0:T(8,128)(2,1)S(1)}, bf16[256,1024]{1,0:T(8,128)(2,1)}, u32[]{:S(2)}) %copy-start.7) | copy-done | bytes 524312
  8.9 0.0 copy-start.8
  8.9 0.9 %copy-done.8 = bf16[1024,128]{1,0:T(8,128)(2,1)S(1)} copy-done((bf16[1024,128]{1,0:T(8,128)(2,1)S(1)}, bf16[1024,128]{1,0:T(8,128)(2,1)}, u32[]{:S(2)}) %copy-start.8) | copy-done | bytes 262168
  9.8 0.0 copy-start.1
  9.8 0.0 copy-start.2
  9.8 1.4 %project_family.1 = (f32[512,256]{1,0:T(8,128)S(1)}, bf16[512,256]{1,0:T(8,128)(2,1)S(1)}, f32[512,256]{1,0:T(8,128)S(1)}, bf16[1024,128]{1,0:T(8,128)(2,1)S(1)}) custom-call(bf16[512,256]{1,0:T(8,128)(2,1)S(1)} %bitcast.11, bf16[256,1024]{1,0:T(8,128)(2,1)S(1)} %copy-done.7, bf16[1024,128]{1,0:T(8,128)(2,1)S(1)} %copy-done.8), custom_call_target="tpu_custom_call" | custom-call | flops 536870912 | bytes 4194304 | tf_op jit(solution)/shard_map/project_family/pallas_call | solution.py:661
  11.3 1.6 %all-to-all-done.got_ref = bf16[8,32,128]{2,1,0:T(8,128)(2,1)S(1)} async-done(((bf16[8,32,128]{2,1,0:T(8,128)(2,1)}), bf16[8,32,128]{2,1,0:T(8,128)(2,1)S(1)}, u32[]{:S(2)}, u32[]{:S(2)}) %all-to-all-start) | async-done | bytes 65568 | tf_op jit(solution)/shard_map/all_to_all | solution.py:659
  12.8 0.0 copy-done.1
  12.8 0.0 copy-done.2
  12.8 0.0 copy-done.5
  12.8 2.2 %row_attention.1 = (bf16[512,256]{1,0:T(8,128)(2,1)}, bf16[384,128]{1,0:T(8,128)(2,1)S(1)}) custom-call(bf16[512,256]{1,0:T(8,128)(2,1)S(1)} %bitcast.12, bf16[8,32,128]{2,1,0:T(8,128)(2,1)S(1)} %all-to-all-done.got_ref, f32[512,256]{1,0:T(8,128)S(1)} %get-tuple-element.11.logits_ref, bf16[512,256]{1,0:T(8,128)(2,1)S(1)} %get-tuple-element.12.value_ref, ...), custom_call_target="tpu_custom_call" | custom-call | tf_op jit(solution)/shard_map/row_attention/pallas_call | solution.py:681
  15.1 0.0 copy-start.3
  15.1 0.0 copy-start.4
  15.1 0.0 copy-start.6
  15.1 9.6 %all-gather = bf16[3072,128]{1,0:T(8,128)(2,1)S(1)} all-gather(bf16[384,128]{1,0:T(8,128)(2,1)S(1)} %get-tuple-element.15), channel_id=2, replica_groups=mesh['dap'=8,'dp'=4] {'dap'}, dimensions={0}, use_global_device_ids=true | all-gather | bytes 884736 | tf_op jit(solution)/shard_map/all_gather | solution.py:700
  24.7 0.0 copy-done.3
  24.7 0.0 copy-done.4
  24.7 0.0 copy-done.6
  24.7 4.7 %pair_update.1 = (bf16[128,128]{1,0:T(8,128)(2,1)}, f32[128,128]{1,0:T(8,128)}) custom-call(bf16[8,384,128]{2,1,0:T(8,128)(2,1)S(1)} %bitcast.10, bf16[8,32,128]{2,1,0:T(8,128)(2,1)S(1)} %all-to-all-done.got_ref, bf16[128,128]{1,0:T(8,128)(2,1)S(1)} %bitcast.16, bf16[1024,128]{1,0:T(8,128)(2,1)S(1)} %get-tuple-element.16.covariance_ref, ...), custom_call_target="tpu_custom_call" | custom-call | tf_op jit(solution)/shard_map/pair_update/pallas_call | solution.py:701
  (1 shorter events, 0.0 us)
Async XLA Ops:
  0.6 7.2 %copy-start = (bf16[16,32,256]{2,1,0:T(8,128)(2,1)S(1)}, bf16[16,32,256]{2,1,0:T(8,128)(2,1)}, u32[]{:S(2)}) copy-start(bf16[16,32,256]{2,1,0:T(8,128)(2,1)} %param.11) | copy-start | bytes 786436
  2.6 10.2 %all-to-all-start = ((bf16[8,32,128]{2,1,0:T(8,128)(2,1)}), bf16[8,32,128]{2,1,0:T(8,128)(2,1)S(1)}, u32[]{:S(2)}, u32[]{:S(2)}) async-start(bf16[8,32,128]{2,1,0:T(8,128)(2,1)} %bitcast.18), calls=%async_computation | async-start | bytes 131072 | tf_op jit(solution)/shard_map/all_to_all | solution.py:659
  7.8 1.0 %copy-start.7 = (bf16[256,1024]{1,0:T(8,128)(2,1)S(1)}, bf16[256,1024]{1,0:T(8,128)(2,1)}, u32[]{:S(2)}) copy-start(bf16[256,1024]{1,0:T(8,128)(2,1)} %project_ref.1) | copy-start | bytes 1572868
  8.9 0.9 %copy-start.8 = (bf16[1024,128]{1,0:T(8,128)(2,1)S(1)}, bf16[1024,128]{1,0:T(8,128)(2,1)}, u32[]{:S(2)}) copy-start(bf16[1024,128]{1,0:T(8,128)(2,1)} %covariance_ref.1) | copy-start | bytes 786436
  9.8 3.0 %copy-start.1 = (bf16[4,32,128]{2,1,0:T(8,128)(2,1)S(1)}, bf16[4,32,128]{2,1,0:T(8,128)(2,1)}, u32[]{:S(2)}) copy-start(bf16[4,32,128]{2,1,0:T(8,128)(2,1)} %param.12) | copy-start | bytes 98308
  9.8 3.0 %copy-start.2 = (bf16[256,256]{1,0:T(8,128)(2,1)S(1)}, bf16[256,256]{1,0:T(8,128)(2,1)}, u32[]{:S(2)}) copy-start(bf16[256,256]{1,0:T(8,128)(2,1)} %merge_ref.1) | copy-start | bytes 393220
  9.8 3.0 %copy-start.5 = (bf16[256,64]{0,1:T(8,128)(2,1)S(1)}, bf16[256,64]{0,1:T(8,128)(2,1)}, u32[]{:S(2)}) copy-start(bf16[256,64]{0,1:T(8,128)(2,1)} %param.17) | copy-start | bytes 98308
  15.1 9.6 %copy-start.3 = (bf16[4,32,128]{2,1,0:T(8,128)(2,1)S(1)}, bf16[4,32,128]{2,1,0:T(8,128)(2,1)}, u32[]{:S(2)}) copy-start(bf16[4,32,128]{2,1,0:T(8,128)(2,1)} %param.21) | copy-start | bytes 98308
  15.1 9.6 %copy-start.4 = (bf16[128,384]{1,0:T(8,128)(2,1)S(1)}, bf16[128,384]{1,0:T(8,128)(2,1)}, u32[]{:S(2)}) copy-start(bf16[128,384]{1,0:T(8,128)(2,1)} %edges_ref.1) | copy-start | bytes 294916
  15.1 9.6 %copy-start.6 = (bf16[128,128]{1,0:T(8,128)(2,1)S(1)}, bf16[128,128]{1,0:T(8,128)(2,1)}, u32[]{:S(2)}) copy-start(bf16[128,128]{1,0:T(8,128)(2,1)} %cycle_ref.1) | copy-start | bytes 98308

commit v5 on v4

--- a/solution.py
+++ b/solution.py
@@ -198,6 +198,7 @@
 F32 = jnp.float32
 BF16 = jnp.bfloat16
 NT = (((1,), (1,)), ((), ()))
+PARTS = 2
 
 
 def dot(a, b):
@@ -275,6 +276,7 @@
     cov_ref,
     query_s,
     key_s,
+    value_s,
     cov_s,
 ):
     rows, depth = family_ref.shape
@@ -283,7 +285,7 @@
     normed = standardize_features(family_ref[...].astype(F32)).astype(BF16)
     query_s[...] = dot(normed, project_ref[:, :depth]).astype(BF16)
     key_s[...] = dot(normed, project_ref[:, depth : 2 * depth]).astype(BF16)
-    value_ref[...] = dot(normed, project_ref[:, 2 * depth : 3 * depth]).astype(BF16)
+    value_s[...] = dot(normed, project_ref[:, 2 * depth : 3 * depth]).astype(BF16)
     gating_ref[...] = jax.nn.sigmoid(dot(normed, project_ref[:, 3 * depth :]))
     same = (iota((128, 128), 0) // width == iota((128, 128), 1) // width).astype(F32).astype(BF16)
     scale = 1.0 / math.sqrt(depth // heads)
@@ -293,10 +295,14 @@
             span = slice(width * s, width * s + width)
             keys = jnp.concatenate([key_s[span, cols]] * group, 0) * same
             logits_ref[span, cols] = dot_nt(query_s[span, cols], keys) * scale
+            values = jnp.concatenate([value_s[span, cols]] * group, 0) * same
+            value_ref[128 * s : 128 * (s + 1), cols] = values
     cov_s[...] = covariance_ref[...].astype(F32)
     for b in range(hidden):
-        span = slice(hidden * b, hidden * b + hidden)
-        cov_ref[span, :] = cov_s[pl.ds(b, hidden, stride=hidden), :].astype(BF16)
+        rows_b = cov_s[pl.ds(b, hidden, stride=hidden), :].astype(BF16)
+        cov_ref[0, hidden * b : hidden * (b + 1), :] = rows_b
+        swapped = b ^ (group // 2)
+        cov_ref[1, hidden * swapped : hidden * (swapped + 1), :] = rows_b
 
 
 def attention_kernel(
@@ -323,8 +329,6 @@
     seqs = rows // width
     tiles = depth // 128
     group = 128 // width
-    same = (iota((128, 128), 0) // width == iota((128, 128), 1) // width).astype(F32).astype(BF16)
-    lane_group = iota((rows, 128), 1) // width
     biases = jnp.concatenate([got_ref[d, :16, :] for d in range(got_ref.shape[0])], 0)
     gated = []
     for t in range(tiles):
@@ -332,23 +336,24 @@
         row = iota((width, biases.shape[0]), 0)
         take = iota((width, biases.shape[0]), 1) == 16 * (row // own) + own * t + row % own
         bias = dot(take.astype(F32).astype(BF16), biases)
-        logits = jnp.concatenate(
-            [logits_ref[width * s : width * (s + 1), cols] + bias for s in range(seqs)], 0
+        for k in range(rows // 128):
+            span = slice(128 * k, 128 * (k + 1))
+            flipped = (logits_ref[span, cols] + jnp.concatenate([bias] * group, 0)).T
+            parts = []
+            for h in range(group):
+                some = flipped[width * h : width * (h + 1)]
+                raised = jnp.exp(some - jnp.max(some, 0, keepdims=True))
+                parts.append(raised * (1.0 / jnp.sum(raised, 0, keepdims=True)))
+            weight_s[span, cols] = jnp.concatenate(parts, 0).astype(BF16).T
+    for t in range(tiles):
+        cols = slice(128 * t, 128 * t + 128)
+        mixed = jnp.concatenate(
+            [
+                dot(weight_s[width * s : width * (s + 1), cols], value_ref[128 * s : 128 * (s + 1), cols])
+                for s in range(seqs)
+            ],
+            0,
         )
-        top = jnp.full(logits.shape, -jnp.inf, F32)
-        for h in range(group):
-            best = jnp.max(
-                jnp.where(lane_group == h, logits, -jnp.inf), axis=-1, keepdims=True
-            )
-            top = jnp.where(lane_group == h, best, top)
-        weight_s[:, cols] = jnp.exp(logits - top).astype(BF16)
-        total = dot(weight_s[:, cols], same)
-        parts = []
-        for s in range(seqs):
-            span = slice(width * s, width * s + width)
-            values = jnp.concatenate([value_ref[span, cols]] * group, 0) * same
-            parts.append(dot(weight_s[span, cols], values))
-        mixed = jnp.concatenate(parts, 0) / total
         gated.append((gating_ref[:, cols] * mixed).astype(BF16))
     after = (
         family_ref[...].astype(F32) + dot(jnp.concatenate(gated, 1), merge_ref[...])
@@ -406,15 +411,8 @@
     return blocks
 
 
-def average(values, weights):
-    high = values.astype(BF16)
-    low = (values - high.astype(F32)).astype(BF16)
-    return dot(jnp.concatenate([high, low], 1), weights)
-
-
-def center_and_scale(values, weights):
-    center = values - average(values, weights)
-    return center, lax.rsqrt(average(center * center, weights) + EPSILON)
+def mean(values):
+    return jnp.mean(values, -1, keepdims=True)
 
 
 def merge_rows(parts):
@@ -449,13 +447,13 @@
     mid_s,
     unit_s,
     scale_s,
-    gate_s,
     a_s,
     b_s,
     tri_s,
 ):
     me = lax.axis_index(axis)
     n = sides_ref.shape[0]
+    every = width * width
     group = 128 // hidden
     groups = width // group
     chunks = hidden // group
@@ -474,32 +472,47 @@
             right_s[width * g : width * (g + 1), total * q : total * (q + 1)] = turned[
                 width * q : width * (q + 1), :
             ]
-    weights = jnp.full((2 * chans, chans), 1.0 / chans, BF16)
     block = iota((total, 128), 1) // hidden
+    low_half = iota((width * chunks, 128), 1) < 64
+    zero = jnp.zeros((total, 128), BF16)
     for g in range(groups):
-        left = gathered(seqs * g).astype(F32)
-        rolled = [left] + [pltpu.roll(left, hidden * d, 1) for d in range(1, group)]
-        for half in range(group // 2):
+        left = gathered(seqs * g)
+        wide = left.astype(F32)
+        rolled = [left] + [
+            pltpu.roll(wide, hidden * d, 1).astype(BF16) for d in range(1, group)
+        ]
+
+        def placed(first, second, lane):
+            return jnp.where(
+                block == lane,
+                rolled[(lane - first) % group],
+                jnp.where(block == lane + 2, rolled[(lane + 2 - second) % group], zero),
+            )
+
+        halves = []
+        for h in range(2):
             columns = []
-            for i in (2 * half, 2 * half + 1):
+            for even in range(0, group, 2):
+                first, second = (even, even + 1) if h == 0 else (even + 1, even)
                 columns.append(
-                    jnp.concatenate(
-                        [
-                            jnp.where(block == q, rolled[(q - i) % group], 0.0).astype(BF16)
-                            for q in range(group)
-                        ],
-                        0,
-                    )
+                    jnp.concatenate([placed(first, second, lane) for lane in range(2)], 0)
                 )
-            outer = dot(right_s[...], jnp.concatenate(columns, 1)).astype(BF16)
-            for k in range(2):
-                i = group * g + 2 * half + k
+            halves.append(
+                dot(
+                    right_s[:, 2 * total * h : 2 * total * (h + 1)],
+                    jnp.concatenate(columns, 1),
+                ).astype(BF16)
+            )
+        for e in range(group // 2):
+            x, y = (half[:, 128 * e : 128 * e + 128] for half in halves)
+            for odd, outer in enumerate(
+                (jnp.where(low_half, x, y), jnp.where(low_half, y, x))
+            ):
+                first = every // 2 * odd + width * (group // 2 * g + e)
                 for c in range(chunks):
-                    flat_s[width * i : width * (i + 1), 128 * c : 128 * c + 128] = outer[
-                        width * c : width * (c + 1), 128 * k : 128 * k + 128
+                    flat_s[first : first + width, 128 * c : 128 * c + 128] = outer[
+                        width * c : width * (c + 1)
                     ]
-    part = n * pairs // 2
-    spans = [slice(part * h, part * (h + 1)) for h in range(2)]
     tiles = jnp.concatenate([got_ref[d, :16, :] for d in range(n)], 0)
     pick = (iota((width, 128), 0) == iota((width, 128), 1)).astype(F32).astype(BF16)
     masks = dot_nt(pick, tiles)
@@ -513,28 +526,49 @@
             0,
         )
 
-    added = [dot(flat_s[span, :], covariance_ref[...]) for span in spans]
+    count = width // PARTS
+    lists = [
+        [2 * (count * (p // 2) + k) + p % 2 for k in range(count)] for p in range(PARTS)
+    ]
+    centered = jnp.where(
+        iota((chans, chans), 0) == iota((chans, chans), 1), 1.0 - 1.0 / chans, -1.0 / chans
+    ).astype(BF16)
+    added = [
+        dot(
+            flat_s[
+                every // 2 * (p % 2) + width * count * (p // 2) : every // 2 * (p % 2)
+                + width * count * (p // 2 + 1),
+                :,
+            ],
+            covariance_ref[p % 2],
+        )
+        for p in range(PARTS)
+    ]
     mids = []
-    for h, span in enumerate(spans):
-        devices = range(n // 2 * h, n // 2 * (h + 1))
-        edge = jnp.concatenate([sides_ref[d, base:, :] for d in devices], 0).astype(F32)
-        mids.append((edge + added[h] * (1.0 / total)).astype(BF16))
-        mid_s[span, :] = mids[h].astype(F32)
-    centers = [mid.astype(F32) - dot(mid, weights[:chans]) for mid in mids]
-    scales = [lax.rsqrt(average(c * c, weights) + EPSILON) for c in centers]
+    for p, residues in enumerate(lists):
+        edge = jnp.concatenate(
+            [
+                sides_ref[i // own, base + width * (i % own) : base + width * (i % own + 1), :]
+                for i in residues
+            ],
+            0,
+        ).astype(F32)
+        mids.append((edge + added[p] * (1.0 / total)).astype(BF16))
+    centers = [dot(mid, centered) for mid in mids]
+    scales = [lax.rsqrt(mean(c * c) + EPSILON) for c in centers]
     units = [c * scale for c, scale in zip(centers, scales)]
-    sides = [dot(unit.astype(BF16), edges_ref[...]) for unit in units]
-    for h, span in enumerate(spans):
-        scale_s[span, :] = scales[h]
-        unit_s[span, :] = units[h]
-        gate_s[span, :] = sides[h][:, 2 * chans :]
-        for d in range(n // 2):
-            g = n // 2 * h + d
-            keep = kept(masks, 16 * g + 2 * own)
-            here = slice(pairs * d, pairs * (d + 1))
-            there = slice(pairs * g, pairs * (g + 1))
-            a_s[there, :] = (keep * sides[h][here, :chans]).astype(BF16).astype(F32)
-            b_s[there, :] = (keep * sides[h][here, chans : 2 * chans]).astype(BF16).astype(F32)
+    sides = [dot(unit.astype(BF16), edges_ref[:, : 2 * chans]) for unit in units]
+    for p, residues in enumerate(lists):
+        for k, i in enumerate(residues):
+            here = slice(width * k, width * (k + 1))
+            there = slice(width * i, width * (i + 1))
+            mid_s[there, :] = mids[p][here].astype(F32)
+            scale_s[there, :] = jnp.broadcast_to(scales[p][here], (width, chans))
+            unit_s[there, :] = units[p][here]
+            lane = 16 * (i // own) + 2 * own + i % own
+            keep = jnp.broadcast_to(masks[:, lane : lane + 1], (width, chans))
+            a_s[there, :] = (keep * sides[p][here, :chans]).astype(BF16).astype(F32)
+            b_s[there, :] = (keep * sides[p][here, chans:]).astype(BF16).astype(F32)
 
     rows = pl.ds(pl.multiple_of(me * pairs, pairs), pairs)
 
@@ -550,7 +584,9 @@
     source = goal % width // own * 16 + goal // width * own + goal % own
     place = (source == iota((pairs, pairs), 1)).astype(F32).astype(BF16)
     loss = jnp.concatenate([own_loss_ref[...].astype(F32), dot(place, losses)], 0)
-    gating = jax.nn.sigmoid(rows_and_columns(gate_s))
+    gating = jax.nn.sigmoid(
+        dot(rows_and_columns(unit_s).astype(BF16), edges_ref[:, 2 * chans :])
+    )
     tri = []
     for fixed, moving in ((a_s, b_s), (b_s, a_s)):
         held = fixed[rows, :]
@@ -566,7 +602,8 @@
                     parts.append(functools.reduce(jnp.add, prods))
                 tri.append(merge_rows(parts))
     tri = jnp.concatenate(tri, 0)
-    center, scale_inv = center_and_scale(tri, weights)
+    center = tri - mean(tri)
+    scale_inv = lax.rsqrt(mean(center * center) + EPSILON)
     unit = center * scale_inv
     update = dot(unit[:pairs].astype(BF16), cycle_ref[...])
     out_ref[...] = (mid + gating[:pairs] * update).astype(BF16)
@@ -575,9 +612,7 @@
         (
             scale_inv
             * (
-                grad_normed
-                - average(grad_normed, weights)
-                - unit * average(grad_normed * unit, weights)
+                grad_normed - mean(grad_normed) - unit * mean(grad_normed * unit)
             )
         )
         .astype(BF16)
@@ -610,7 +645,7 @@
     scale_inv = scale_s[rows, :]
     unit = unit_s[rows, :]
     grad_ref[...] = loss[:pairs] + scale_inv * (
-        grad_input - average(grad_input, weights) - unit * average(grad_input * unit, weights)
+        grad_input - mean(grad_input) - unit * mean(grad_input * unit)
     )
 
 
@@ -662,13 +697,13 @@
         functools.partial(project_kernel, width, heads, hidden),
         out_shape=(
             jax.ShapeDtypeStruct((seqs * width, depth), F32),
-            jax.ShapeDtypeStruct((seqs * width, depth), BF16),
+            jax.ShapeDtypeStruct((seqs * 128, depth), BF16),
             jax.ShapeDtypeStruct((seqs * width, depth), F32),
-            jax.ShapeDtypeStruct((hidden * hidden, chans), BF16),
+            jax.ShapeDtypeStruct((2, hidden * hidden, chans), BF16),
         ),
         in_specs=[vmem] * 3,
         out_specs=(vmem,) * 4,
-        scratch_shapes=[pltpu.VMEM((seqs * width, depth), BF16)] * 2
+        scratch_shapes=[pltpu.VMEM((seqs * width, depth), BF16)] * 3
         + [pltpu.VMEM((hidden * hidden, chans), F32)],
         compiler_params=pltpu.CompilerParams(vmem_limit_bytes=16 << 20),
         cost_estimate=pl.CostEstimate(
@@ -714,7 +749,6 @@
             pltpu.VMEM((every, chans), F32),
             pltpu.VMEM((every, chans), F32),
             pltpu.VMEM((every, chans), F32),
-            pltpu.VMEM((every, chans), F32),
             pltpu.VMEM((2 * pairs, chans), F32),
         ],
         compiler_params=pltpu.CompilerParams(vmem_limit_bytes=16 << 20),

time: 29.8 us -> 28.4 us (0.953)
  Pallas kernels: 10.3 us -> 9.05 us
    pallas_call x1, Pallas kernels: 4.73 us -> 3.87 us  [body_resident(): pl.pallas_call(functools.partial(pair_kernel, 'dap', width, own, hidden,...]
    pallas_call x1, Pallas kernels: 2.2 us -> 1.68 us  [body_resident(): pl.pallas_call(functools.partial(attention_kernel, width, own), out_shape...]
where the time goes in v5:
time: 28.4 us; the launch traced here: 28 us
  blocking collectives  9.59 us (34%)
  Pallas kernels  9.05 us (32%)
  starting transfers between devices  5.18 us (18%)
  local copies, waits for them, and re-layouts  2.02 us (7%)
  waiting for transfers between devices  1.49 us (5%)
  between operations  0.71 us (2%)
    all_gather x1, blocking collectives, body_resident(): gathered = lax.all_gather(send, 'dap', axis=0, tiled=False)  9.59 us
    all_to_all x1, starting transfers between devices, body_resident(): got = lax.all_to_all(packed, 'dap', split_axis=0, concat_axis=0, tiled=True)  5.18 us
    pallas_call x1, Pallas kernels, body_resident(): pl.pallas_call(functools.partial(pair_kernel, 'dap', width, own, hidden,...  3.87 us
    unnamed x18, local copies, waits for them, and re-layouts  2.02 us
    pallas_call x1, Pallas kernels, body_resident(): pl.pallas_call(functools.partial(pack_kernel, width), out_shape=jax.Shape...  1.99 us
    pallas_call x1, Pallas kernels, body_resident(): pl.pallas_call(functools.partial(attention_kernel, width, own), out_shape...  1.68 us
    pallas_call x1, Pallas kernels, body_resident(): pl.pallas_call(functools.partial(project_kernel, width, heads, hidden), o...  1.51 us
    all_to_all x1, waiting for transfers between devices, body_resident(): got = lax.all_to_all(packed, 'dap', split_axis=0, concat_axis=0, tiled=True)  1.49 us
  transfers between devices with their start and end apart: 1, of which 1 were waited for; matrix products, arithmetic and copies ran while one was open for 0% of the time, Pallas kernels for 5%

profile of v5, /device:TPU:0, one launch (start us, length us, event | category | flops | bytes accessed | tf_op | source)
XLA Modules:
  0.0 28.0 jit_solution(594017293554587967)
XLA Ops:
  0.6 0.0 copy-start
  0.6 2.0 %pack_pairs.1 = bf16[256,128]{1,0:T(8,128)(2,1)} custom-call(bf16[128,128]{1,0:T(8,128)(2,1)} %bitcast.13, bf16[8,128]{1,0:T(8,128)(2,1)} %bitcast.19, bf16[128,128]{1,0:T(8,128)(2,1)} %bitcast.15, s32[4,32]{1,0:T(4,128)} %mask_ref.1), custom_call_target="tpu_custom_call" | custom-call | tf_op jit(solution)/shard_map/pack_pairs/pallas_call | solution.py:679
  2.6 5.2 %all-to-all-start = ((bf16[8,32,128]{2,1,0:T(8,128)(2,1)}), bf16[8,32,128]{2,1,0:T(8,128)(2,1)S(1)}, u32[]{:S(2)}, u32[]{:S(2)}) async-start(bf16[8,32,128]{2,1,0:T(8,128)(2,1)} %bitcast.18), calls=%async_computation | async-start | bytes 131072 | tf_op jit(solution)/shard_map/all_to_all | solution.py:694
  7.8 0.0 copy-done
  7.8 0.0 copy-start.7
  7.8 1.0 %copy-done.7 = bf16[256,1024]{1,0:T(8,128)(2,1)S(1)} copy-done((bf16[256,1024]{1,0:T(8,128)(2,1)S(1)}, bf16[256,1024]{1,0:T(8,128)(2,1)}, u32[]{:S(2)}) %copy-start.7) | copy-done | bytes 524312
  8.9 0.0 copy-start.8
  8.9 0.9 %copy-done.8 = bf16[1024,128]{1,0:T(8,128)(2,1)S(1)} copy-done((bf16[1024,128]{1,0:T(8,128)(2,1)S(1)}, bf16[1024,128]{1,0:T(8,128)(2,1)}, u32[]{:S(2)}) %copy-start.8) | copy-done | bytes 262168
  9.8 0.0 copy-start.1
  9.8 0.0 copy-start.2
  9.8 1.5 %project_family.1 = (f32[512,256]{1,0:T(8,128)S(1)}, bf16[2048,256]{1,0:T(8,128)(2,1)S(1)}, f32[512,256]{1,0:T(8,128)S(1)}, bf16[2,1024,128]{2,1,0:T(8,128)(2,1)S(1)}) custom-call(bf16[512,256]{1,0:T(8,128)(2,1)S(1)} %bitcast.11, bf16[256,1024]{1,0:T(8,128)(2,1)S(1)} %copy-done.7, bf16[1024,128]{1,0:T(8,128)(2,1)S(1)} %copy-done.8), custom_call_target="tpu_custom_call" | custom-call | flops 536870912 | bytes 4194304 | tf_op jit(solution)/shard_map/project_family/pallas_call | solution.py:696
  11.3 1.5 %all-to-all-done.got_ref = bf16[8,32,128]{2,1,0:T(8,128)(2,1)S(1)} async-done(((bf16[8,32,128]{2,1,0:T(8,128)(2,1)}), bf16[8,32,128]{2,1,0:T(8,128)(2,1)S(1)}, u32[]{:S(2)}, u32[]{:S(2)}) %all-to-all-start) | async-done | bytes 65568 | tf_op jit(solution)/shard_map/all_to_all | solution.py:694
  12.8 0.0 copy-done.1
  12.8 0.0 copy-done.2
  12.8 0.0 copy-done.5
  12.8 1.7 %row_attention.1 = (bf16[512,256]{1,0:T(8,128)(2,1)}, bf16[384,128]{1,0:T(8,128)(2,1)S(1)}) custom-call(bf16[512,256]{1,0:T(8,128)(2,1)S(1)} %bitcast.12, bf16[8,32,128]{2,1,0:T(8,128)(2,1)S(1)} %all-to-all-done.got_ref, f32[512,256]{1,0:T(8,128)S(1)} %get-tuple-element.11.logits_ref, bf16[2048,256]{1,0:T(8,128)(2,1)S(1)} %get-tuple-element.12.value_ref, ...), custom_call_target="tpu_custom_call" | custom-call | tf_op jit(solution)/shard_map/row_attention/pallas_call | solution.py:716
  14.5 0.0 copy-start.3
  14.5 0.0 copy-start.4
  14.6 0.0 copy-start.6
  14.6 9.6 %all-gather = bf16[3072,128]{1,0:T(8,128)(2,1)S(1)} all-gather(bf16[384,128]{1,0:T(8,128)(2,1)S(1)} %get-tuple-element.15), channel_id=2, replica_groups=mesh['dap'=8,'dp'=4] {'dap'}, dimensions={0}, use_global_device_ids=true | all-gather | bytes 884736 | tf_op jit(solution)/shard_map/all_gather | solution.py:735
  24.2 0.0 copy-done.3
  24.2 0.0 copy-done.4
  24.2 0.0 copy-done.6
  24.2 3.9 %pair_update.1 = (bf16[128,128]{1,0:T(8,128)(2,1)}, f32[128,128]{1,0:T(8,128)}) custom-call(bf16[8,384,128]{2,1,0:T(8,128)(2,1)S(1)} %bitcast.10, bf16[8,32,128]{2,1,0:T(8,128)(2,1)S(1)} %all-to-all-done.got_ref, bf16[128,128]{1,0:T(8,128)(2,1)S(1)} %bitcast.16, bf16[2,1024,128]{2,1,0:T(8,128)(2,1)S(1)} %get-tuple-element.16.covariance_ref, ...), custom_call_target="tpu_custom_call" | custom-call | tf_op jit(solution)/shard_map/pair_update/pallas_call | solution.py:736
  (1 shorter events, 0.0 us)
Async XLA Ops:
  0.6 7.2 %copy-start = (bf16[16,32,256]{2,1,0:T(8,128)(2,1)S(1)}, bf16[16,32,256]{2,1,0:T(8,128)(2,1)}, u32[]{:S(2)}) copy-start(bf16[16,32,256]{2,1,0:T(8,128)(2,1)} %param.11) | copy-start | bytes 786436
  2.6 10.2 %all-to-all-start = ((bf16[8,32,128]{2,1,0:T(8,128)(2,1)}), bf16[8,32,128]{2,1,0:T(8,128)(2,1)S(1)}, u32[]{:S(2)}, u32[]{:S(2)}) async-start(bf16[8,32,128]{2,1,0:T(8,128)(2,1)} %bitcast.18), calls=%async_computation | async-start | bytes 131072 | tf_op jit(solution)/shard_map/all_to_all | solution.py:694
  7.8 1.0 %copy-start.7 = (bf16[256,1024]{1,0:T(8,128)(2,1)S(1)}, bf16[256,1024]{1,0:T(8,128)(2,1)}, u32[]{:S(2)}) copy-start(bf16[256,1024]{1,0:T(8,128)(2,1)} %project_ref.1) | copy-start | bytes 1572868
  8.9 0.9 %copy-start.8 = (bf16[1024,128]{1,0:T(8,128)(2,1)S(1)}, bf16[1024,128]{1,0:T(8,128)(2,1)}, u32[]{:S(2)}) copy-start(bf16[1024,128]{1,0:T(8,128)(2,1)} %covariance_ref.1) | copy-start | bytes 786436
  9.8 3.0 %copy-start.1 = (bf16[4,32,128]{2,1,0:T(8,128)(2,1)S(1)}, bf16[4,32,128]{2,1,0:T(8,128)(2,1)}, u32[]{:S(2)}) copy-start(bf16[4,32,128]{2,1,0:T(8,128)(2,1)} %param.12) | copy-start | bytes 98308
  9.8 3.0 %copy-start.2 = (bf16[256,256]{1,0:T(8,128)(2,1)S(1)}, bf16[256,256]{1,0:T(8,128)(2,1)}, u32[]{:S(2)}) copy-start(bf16[256,256]{1,0:T(8,128)(2,1)} %merge_ref.1) | copy-start | bytes 393220
  9.8 3.0 %copy-start.5 = (bf16[256,64]{0,1:T(8,128)(2,1)S(1)}, bf16[256,64]{0,1:T(8,128)(2,1)}, u32[]{:S(2)}) copy-start(bf16[256,64]{0,1:T(8,128)(2,1)} %param.17) | copy-start | bytes 98308
  14.5 9.6 %copy-start.3 = (bf16[4,32,128]{2,1,0:T(8,128)(2,1)S(1)}, bf16[4,32,128]{2,1,0:T(8,128)(2,1)}, u32[]{:S(2)}) copy-start(bf16[4,32,128]{2,1,0:T(8,128)(2,1)} %param.21) | copy-start | bytes 98308
  14.5 9.6 %copy-start.4 = (bf16[128,384]{1,0:T(8,128)(2,1)S(1)}, bf16[128,384]{1,0:T(8,128)(2,1)}, u32[]{:S(2)}) copy-start(bf16[128,384]{1,0:T(8,128)(2,1)} %edges_ref.1) | copy-start | bytes 294916
  14.6 9.6 %copy-start.6 = (bf16[128,128]{1,0:T(8,128)(2,1)S(1)}, bf16[128,128]{1,0:T(8,128)(2,1)}, u32[]{:S(2)}) copy-start(bf16[128,128]{1,0:T(8,128)(2,1)} %cycle_ref.1) | copy-start | bytes 98308

commit v6 on v5

--- a/solution.py
+++ b/solution.py
@@ -230,34 +230,40 @@
     ]
     for copy in copies:
         copy.start()
-    for copy in copies:
-        copy.wait()
     rows, chans = edge_s.shape
     heads = weight_s.shape[0]
     own = rows // width
     lanes = heads * width
     peers = width // own
+    spread = (iota((heads, lanes), 0) == iota((heads, lanes), 1) // width).astype(F32)
+    keep = iota((width, lanes), 0) == iota((width, lanes), 1) % width
+    goal = iota((rows, rows), 0)
+    source = goal % own * width + goal // (own * own) * own + goal // own % own
+    place = (source == iota((rows, rows), 1)).astype(F32).astype(BF16)
     tile_s[...] = jnp.zeros(tile_s.shape, F32)
-    tile_s[2 * own : 3 * own, :width] = mask_s[...].astype(F32)
-    normed = standardize_features(edge_s[...].astype(F32)).astype(BF16)
-    spread = (iota((heads, lanes), 0) == iota((heads, lanes), 1) // width).astype(F32)
+    for copy in copies:
+        copy.wait()
     weight = lax.dot_general(
         weight_s[...], spread.astype(BF16), (((0,), (0,)), ((), ())), preferred_element_type=F32
     ).astype(BF16)
-    every = dot(normed, weight)
-    keep = iota((rows, lanes), 0) % width == iota((rows, lanes), 1) % width
-    picked = jnp.where(keep, every, 0.0).astype(BF16)
+    column = dot(jnp.ones((8, chans), BF16), weight)[:1]
+    every = dot(edge_s[...], weight)
+    edge = edge_s[...].astype(F32)
+    middle = jnp.mean(edge, -1, keepdims=True)
+    center = edge - middle
+    scale = lax.rsqrt(jnp.mean(center * center, -1, keepdims=True) + EPSILON)
+    bias = scale * (every - middle * column)
+    losses = dot(place, loss_s[...]).astype(BF16)
+    tile_s[2 * own : 3 * own, :width] = mask_s[...].astype(F32)
     packed = tile_s[...]
-    for t in range(lanes // 128):
-        place = iota((16, rows), 0) == own * t + iota((16, rows), 1) // width
-        packed = packed + dot(
-            place.astype(F32).astype(BF16), picked[:, 128 * t : 128 * t + 128]
-        )
+    for r in range(own):
+        picked = jnp.where(keep, bias[width * r : width * (r + 1)], 0.0)
+        total = jnp.sum(picked, 0, keepdims=True)
+        for t in range(lanes // 128):
+            packed = jnp.where(
+                iota((16, 128), 0) == own * t + r, total[:, 128 * t : 128 * t + 128], packed
+            )
     packed = packed.astype(BF16)
-    goal = iota((rows, rows), 0)
-    source = goal % own * width + goal // (own * own) * own + goal // own % own
-    place = (source == iota((rows, rows), 1)).astype(F32).astype(BF16)
-    losses = dot(place, loss_s[...]).astype(BF16)
     for e in range(peers):
         send_ref[32 * e : 32 * e + 16, :] = packed
         send_ref[32 * e + 16 : 32 * e + 32, :] = losses[16 * e : 16 * e + 16]
@@ -268,21 +274,32 @@
     heads,
     hidden,
     family_ref,
-    project_ref,
-    covariance_ref,
+    project_hbm,
+    covariance_hbm,
     logits_ref,
     value_ref,
     gating_ref,
     cov_ref,
+    project_ref,
+    covariance_ref,
+    sems,
     query_s,
     key_s,
     value_s,
+    logits_s,
     cov_s,
 ):
+    copies = [
+        pltpu.make_async_copy(project_hbm, project_ref, sems.at[0]),
+        pltpu.make_async_copy(covariance_hbm, covariance_ref, sems.at[1]),
+    ]
+    for copy in copies:
+        copy.start()
     rows, depth = family_ref.shape
     seqs = rows // width
     group = 128 // width
     normed = standardize_features(family_ref[...].astype(F32)).astype(BF16)
+    copies[0].wait()
     query_s[...] = dot(normed, project_ref[:, :depth]).astype(BF16)
     key_s[...] = dot(normed, project_ref[:, depth : 2 * depth]).astype(BF16)
     value_s[...] = dot(normed, project_ref[:, 2 * depth : 3 * depth]).astype(BF16)
@@ -294,9 +311,13 @@
         for s in range(seqs):
             span = slice(width * s, width * s + width)
             keys = jnp.concatenate([key_s[span, cols]] * group, 0) * same
-            logits_ref[span, cols] = dot_nt(query_s[span, cols], keys) * scale
+            logits_s[span, :] = dot_nt(query_s[span, cols], keys) * scale
             values = jnp.concatenate([value_s[span, cols]] * group, 0) * same
             value_ref[128 * s : 128 * (s + 1), cols] = values
+        for k in range(rows // 128):
+            span = slice(128 * k, 128 * (k + 1))
+            logits_ref[span, cols] = logits_s[span, :].T
+    copies[1].wait()
     cov_s[...] = covariance_ref[...].astype(F32)
     for b in range(hidden):
         rows_b = cov_s[pl.ds(b, hidden, stride=hidden), :].astype(BF16)
@@ -333,12 +354,12 @@
     gated = []
     for t in range(tiles):
         cols = slice(128 * t, 128 * t + 128)
-        row = iota((width, biases.shape[0]), 0)
-        take = iota((width, biases.shape[0]), 1) == 16 * (row // own) + own * t + row % own
-        bias = dot(take.astype(F32).astype(BF16), biases)
+        row = iota((128, biases.shape[0]), 0) % width
+        take = iota((128, biases.shape[0]), 1) == 16 * (row // own) + own * t + row % own
+        bias = dot(take.astype(F32).astype(BF16), biases).T
         for k in range(rows // 128):
             span = slice(128 * k, 128 * (k + 1))
-            flipped = (logits_ref[span, cols] + jnp.concatenate([bias] * group, 0)).T
+            flipped = logits_ref[span, cols] + bias
             parts = []
             for h in range(group):
                 some = flipped[width * h : width * (h + 1)]
@@ -619,17 +640,16 @@
         .astype(F32)
     )
 
-    def row(ref, r):
-        return jnp.broadcast_to(ref[r : r + 1, :], (width, chans))
-
-    acc = [jnp.zeros((width, chans), F32) for _ in range(2 * own)]
-    for j in range(width):
-        span = slice(width * j, width * j + width)
-        b_j = b_s[span, :]
-        a_j = a_s[span, :]
-        for r in range(own):
-            acc[r] = acc[r] + row(tri_s, width * r + j) * b_j
-            acc[own + r] = acc[own + r] + row(tri_s, pairs + width * r + j) * a_j
+    acc = []
+    for first, ref in ((0, b_s), (own, a_s)):
+        sums = [[jnp.zeros((8, chans), F32) for _ in range(width // 8)] for _ in range(own)]
+        for j in range(width):
+            parts = [ref[width * j + 8 * v : width * j + 8 * v + 8, :] for v in range(width // 8)]
+            for r in range(own):
+                at = width * (first + r) + j
+                row = jnp.broadcast_to(tri_s[at : at + 1, :], (8, chans))
+                sums[r] = [old + row * part for old, part in zip(sums[r], parts)]
+        acc += [jnp.concatenate(vregs, 0) for vregs in sums]
     keep = kept(dot_nt(pick, got_ref[me, :16, :]), 2 * own)
     gate_own = gating[:pairs]
     grad_gate = loss[:pairs] * update * gate_own * (1.0 - gate_own)
@@ -701,9 +721,15 @@
             jax.ShapeDtypeStruct((seqs * width, depth), F32),
             jax.ShapeDtypeStruct((2, hidden * hidden, chans), BF16),
         ),
-        in_specs=[vmem] * 3,
+        in_specs=[vmem, hbm, hbm],
         out_specs=(vmem,) * 4,
-        scratch_shapes=[pltpu.VMEM((seqs * width, depth), BF16)] * 3
+        scratch_shapes=[
+            pltpu.VMEM(query_key_value_gate_matrix.shape, BF16),
+            pltpu.VMEM(covariance_merge_matrix.shape, BF16),
+            pltpu.SemaphoreType.DMA((2,)),
+        ]
+        + [pltpu.VMEM((seqs * width, depth), BF16)] * 3
+        + [pltpu.VMEM((seqs * width, 128), F32)]
         + [pltpu.VMEM((hidden * hidden, chans), F32)],
         compiler_params=pltpu.CompilerParams(vmem_limit_bytes=16 << 20),
         cost_estimate=pl.CostEstimate(
@@ -712,7 +738,11 @@
             transcendentals=seqs * width * depth,
         ),
         name="project_family",
-    )(family, query_key_value_gate_matrix, covariance_merge_matrix)
+    )(
+        family,
+        pltpu.with_memory_space_constraint(query_key_value_gate_matrix, pltpu.HBM),
+        pltpu.with_memory_space_constraint(covariance_merge_matrix, pltpu.HBM),
+    )
     family_out, send = pl.pallas_call(
         functools.partial(attention_kernel, width, own),
         out_shape=(

time: 28.4 us -> 28.1 us (0.989)
  local copies, waits for them, and re-layouts: 2.02 us -> 0.04 us
  waiting for transfers between devices: 1.49 us -> 2.41 us
  Pallas kernels: 9.05 us -> 9.9 us
    unnamed x18 -> x14, local copies, waits for them, and re-layouts: 2.02 us -> 0.04 us
    pallas_call x1, Pallas kernels: 1.51 us -> 2.56 us  [body_resident(): pl.pallas_call(functools.partial(project_kernel, width, heads, hidden), o...]
    all_to_all x1, waiting for transfers between devices: 1.49 us -> 2.41 us  [body_resident(): got = lax.all_to_all(packed, 'dap', split_axis=0, concat_axis=0, tiled=True)]
  transfers between devices with their start and end apart: 1 -> 1, of which waited for: 1 -> 1; matrix products, arithmetic and copies ran while one was open for 0% -> 0% of each run, Pallas kernels for 5% -> 9%
where the time goes in v6:
time: 28.1 us; the launch traced here: 27.9 us
  Pallas kernels  9.9 us (35%)
  blocking collectives  9.59 us (34%)
  starting transfers between devices  5.18 us (18%)
  waiting for transfers between devices  2.41 us (9%)
  between operations  0.72 us (3%)
    all_gather x1, blocking collectives, body_resident(): gathered = lax.all_gather(send, 'dap', axis=0, tiled=False)  9.59 us
    all_to_all x1, starting transfers between devices, body_resident(): got = lax.all_to_all(packed, 'dap', split_axis=0, concat_axis=0, tiled=True)  5.18 us
    pallas_call x1, Pallas kernels, body_resident(): pl.pallas_call(functools.partial(pair_kernel, 'dap', width, own, hidden,...  3.86 us
    pallas_call x1, Pallas kernels, body_resident(): pl.pallas_call(functools.partial(project_kernel, width, heads, hidden), o...  2.56 us
    all_to_all x1, waiting for transfers between devices, body_resident(): got = lax.all_to_all(packed, 'dap', split_axis=0, concat_axis=0, tiled=True)  2.41 us
    pallas_call x1, Pallas kernels, body_resident(): pl.pallas_call(functools.partial(pack_kernel, width), out_shape=jax.Shape...  1.88 us
    pallas_call x1, Pallas kernels, body_resident(): pl.pallas_call(functools.partial(attention_kernel, width, own), out_shape...  1.6 us
  transfers between devices with their start and end apart: 1, of which 1 were waited for; matrix products, arithmetic and copies ran while one was open for 0% of the time, Pallas kernels for 9%

profile of v6, /device:TPU:0, one launch (start us, length us, event | category | flops | bytes accessed | tf_op | source)
XLA Modules:
  0.0 27.9 jit_solution(4177296238387841042)
XLA Ops:
  0.6 0.0 copy-start
  0.6 1.9 %pack_pairs.1 = bf16[256,128]{1,0:T(8,128)(2,1)} custom-call(bf16[128,128]{1,0:T(8,128)(2,1)} %bitcast.13, bf16[8,128]{1,0:T(8,128)(2,1)} %bitcast.19, bf16[128,128]{1,0:T(8,128)(2,1)} %bitcast.15, s32[4,32]{1,0:T(4,128)} %mask_ref.1), custom_call_target="tpu_custom_call" | custom-call | tf_op jit(solution)/shard_map/pack_pairs/pallas_call | solution.py:699
  2.5 5.2 %all-to-all-start = ((bf16[8,32,128]{2,1,0:T(8,128)(2,1)}), bf16[8,32,128]{2,1,0:T(8,128)(2,1)S(1)}, u32[]{:S(2)}, u32[]{:S(2)}) async-start(bf16[8,32,128]{2,1,0:T(8,128)(2,1)} %bitcast.18), calls=%async_computation | async-start | bytes 131072 | tf_op jit(solution)/shard_map/all_to_all | solution.py:714
  7.7 0.0 copy-done
  7.7 0.0 copy-start.1
  7.7 0.0 copy-start.2
  7.7 0.0 copy-start.5
  7.8 2.6 %project_family.1 = (f32[512,256]{1,0:T(8,128)S(1)}, bf16[2048,256]{1,0:T(8,128)(2,1)S(1)}, f32[512,256]{1,0:T(8,128)S(1)}, bf16[2,1024,128]{2,1,0:T(8,128)(2,1)S(1)}) custom-call(bf16[512,256]{1,0:T(8,128)(2,1)S(1)} %bitcast.11, bf16[256,1024]{1,0:T(8,128)(2,1)} %project_hbm.1, bf16[1024,128]{1,0:T(8,128)(2,1)} %covariance_hbm.1), custom_call_target="tpu_custom_call" | custom-call | flops 536870912 | bytes 4194304 | tf_op jit(solution)/shard_map/project_family/pallas_call | solution.py:716
  10.3 2.4 %all-to-all-done.got_ref = bf16[8,32,128]{2,1,0:T(8,128)(2,1)S(1)} async-done(((bf16[8,32,128]{2,1,0:T(8,128)(2,1)}), bf16[8,32,128]{2,1,0:T(8,128)(2,1)S(1)}, u32[]{:S(2)}, u32[]{:S(2)}) %all-to-all-start) | async-done | bytes 65568 | tf_op jit(solution)/shard_map/all_to_all | solution.py:714
  12.7 0.0 copy-done.1
  12.7 0.0 copy-done.2
  12.7 0.0 copy-done.5
  12.7 1.6 %row_attention.1 = (bf16[512,256]{1,0:T(8,128)(2,1)}, bf16[384,128]{1,0:T(8,128)(2,1)S(1)}) custom-call(bf16[512,256]{1,0:T(8,128)(2,1)S(1)} %bitcast.12, bf16[8,32,128]{2,1,0:T(8,128)(2,1)S(1)} %all-to-all-done.got_ref, f32[512,256]{1,0:T(8,128)S(1)} %get-tuple-element.11.logits_ref, bf16[2048,256]{1,0:T(8,128)(2,1)S(1)} %get-tuple-element.12.value_ref, ...), custom_call_target="tpu_custom_call" | custom-call | tf_op jit(solution)/shard_map/row_attention/pallas_call | solution.py:746
  14.4 0.0 copy-start.3
  14.4 0.0 copy-start.4
  14.4 0.0 copy-start.6
  14.4 9.6 %all-gather = bf16[3072,128]{1,0:T(8,128)(2,1)S(1)} all-gather(bf16[384,128]{1,0:T(8,128)(2,1)S(1)} %get-tuple-element.15), channel_id=2, replica_groups=mesh['dap'=8,'dp'=4] {'dap'}, dimensions={0}, use_global_device_ids=true | all-gather | bytes 884736 | tf_op jit(solution)/shard_map/all_gather | solution.py:765
  24.0 0.0 copy-done.3
  24.0 0.0 copy-done.4
  24.0 0.0 copy-done.6
  24.0 3.9 %pair_update.1 = (bf16[128,128]{1,0:T(8,128)(2,1)}, f32[128,128]{1,0:T(8,128)}) custom-call(bf16[8,384,128]{2,1,0:T(8,128)(2,1)S(1)} %bitcast.10, bf16[8,32,128]{2,1,0:T(8,128)(2,1)S(1)} %all-to-all-done.got_ref, bf16[128,128]{1,0:T(8,128)(2,1)S(1)} %bitcast.16, bf16[2,1024,128]{2,1,0:T(8,128)(2,1)S(1)} %get-tuple-element.16.covariance_ref, ...), custom_call_target="tpu_custom_call" | custom-call | tf_op jit(solution)/shard_map/pair_update/pallas_call | solution.py:766
Async XLA Ops:
  0.6 7.1 %copy-start = (bf16[16,32,256]{2,1,0:T(8,128)(2,1)S(1)}, bf16[16,32,256]{2,1,0:T(8,128)(2,1)}, u32[]{:S(2)}) copy-start(bf16[16,32,256]{2,1,0:T(8,128)(2,1)} %param.11) | copy-start | bytes 786436
  2.5 10.2 %all-to-all-start = ((bf16[8,32,128]{2,1,0:T(8,128)(2,1)}), bf16[8,32,128]{2,1,0:T(8,128)(2,1)S(1)}, u32[]{:S(2)}, u32[]{:S(2)}) async-start(bf16[8,32,128]{2,1,0:T(8,128)(2,1)} %bitcast.18), calls=%async_computation | async-start | bytes 131072 | tf_op jit(solution)/shard_map/all_to_all | solution.py:714
  7.7 5.0 %copy-start.1 = (bf16[4,32,128]{2,1,0:T(8,128)(2,1)S(1)}, bf16[4,32,128]{2,1,0:T(8,128)(2,1)}, u32[]{:S(2)}) copy-start(bf16[4,32,128]{2,1,0:T(8,128)(2,1)} %param.12) | copy-start | bytes 98308
  7.7 5.0 %copy-start.2 = (bf16[256,256]{1,0:T(8,128)(2,1)S(1)}, bf16[256,256]{1,0:T(8,128)(2,1)}, u32[]{:S(2)}) copy-start(bf16[256,256]{1,0:T(8,128)(2,1)} %merge_ref.1) | copy-start | bytes 393220
  7.7 5.0 %copy-start.5 = (bf16[256,64]{0,1:T(8,128)(2,1)S(1)}, bf16[256,64]{0,1:T(8,128)(2,1)}, u32[]{:S(2)}) copy-start(bf16[256,64]{0,1:T(8,128)(2,1)} %param.17) | copy-start | bytes 98308
  14.4 9.6 %copy-start.3 = (bf16[4,32,128]{2,1,0:T(8,128)(2,1)S(1)}, bf16[4,32,128]{2,1,0:T(8,128)(2,1)}, u32[]{:S(2)}) copy-start(bf16[4,32,128]{2,1,0:T(8,128)(2,1)} %param.21) | copy-start | bytes 98308
  14.4 9.6 %copy-start.4 = (bf16[128,384]{1,0:T(8,128)(2,1)S(1)}, bf16[128,384]{1,0:T(8,128)(2,1)}, u32[]{:S(2)}) copy-start(bf16[128,384]{1,0:T(8,128)(2,1)} %edges_ref.1) | copy-start | bytes 294916
  14.4 9.6 %copy-start.6 = (bf16[128,128]{1,0:T(8,128)(2,1)S(1)}, bf16[128,128]{1,0:T(8,128)(2,1)}, u32[]{:S(2)}) copy-start(bf16[128,128]{1,0:T(8,128)(2,1)} %cycle_ref.1) | copy-start | bytes 98308

commit v7 on v6

--- a/solution.py
+++ b/solution.py
@@ -486,9 +486,8 @@
     def gathered(first):
         return jnp.concatenate([sides_ref[d, first : first + seqs, :] for d in range(n)], 0)
 
-    eye = (iota((128, 128), 0) == iota((128, 128), 1)).astype(F32).astype(BF16)
     for g in range(chunks):
-        turned = dot_nt(eye, gathered(seqs * (groups + g))).astype(BF16)
+        turned = gathered(seqs * (groups + g)).T
         for q in range(group):
             right_s[width * g : width * (g + 1), total * q : total * (q + 1)] = turned[
                 width * q : width * (q + 1), :

time: 28.1 us -> 28 us (level)
  no operation moved by 1% of the time
where the time goes in v7:
time: 28 us; the launch traced here: 27.7 us
  Pallas kernels  9.77 us (35%)
  blocking collectives  9.59 us (34%)
  starting transfers between devices  5.18 us (18%)
  waiting for transfers between devices  2.41 us (9%)
  between operations  0.72 us (3%)
    all_gather x1, blocking collectives, body_resident(): gathered = lax.all_gather(send, 'dap', axis=0, tiled=False)  9.59 us
    all_to_all x1, starting transfers between devices, body_resident(): got = lax.all_to_all(packed, 'dap', split_axis=0, concat_axis=0, tiled=True)  5.18 us
    pallas_call x1, Pallas kernels, body_resident(): pl.pallas_call(functools.partial(pair_kernel, 'dap', width, own, hidden,...  3.72 us
    pallas_call x1, Pallas kernels, body_resident(): pl.pallas_call(functools.partial(project_kernel, width, heads, hidden), o...  2.56 us
    all_to_all x1, waiting for transfers between devices, body_resident(): got = lax.all_to_all(packed, 'dap', split_axis=0, concat_axis=0, tiled=True)  2.41 us
    pallas_call x1, Pallas kernels, body_resident(): pl.pallas_call(functools.partial(pack_kernel, width), out_shape=jax.Shape...  1.88 us
    pallas_call x1, Pallas kernels, body_resident(): pl.pallas_call(functools.partial(attention_kernel, width, own), out_shape...  1.6 us
  transfers between devices with their start and end apart: 1, of which 1 were waited for; matrix products, arithmetic and copies ran while one was open for 0% of the time, Pallas kernels for 9%

profile of v7, /device:TPU:0, one launch (start us, length us, event | category | flops | bytes accessed | tf_op | source)
XLA Modules:
  0.0 27.7 jit_solution(2483237677935080595)
XLA Ops:
  0.6 0.0 copy-start
  0.6 1.9 %pack_pairs.1 = bf16[256,128]{1,0:T(8,128)(2,1)} custom-call(bf16[128,128]{1,0:T(8,128)(2,1)} %bitcast.13, bf16[8,128]{1,0:T(8,128)(2,1)} %bitcast.19, bf16[128,128]{1,0:T(8,128)(2,1)} %bitcast.15, s32[4,32]{1,0:T(4,128)} %mask_ref.1), custom_call_target="tpu_custom_call" | custom-call | tf_op jit(solution)/shard_map/pack_pairs/pallas_call | solution.py:698
  2.5 5.2 %all-to-all-start = ((bf16[8,32,128]{2,1,0:T(8,128)(2,1)}), bf16[8,32,128]{2,1,0:T(8,128)(2,1)S(1)}, u32[]{:S(2)}, u32[]{:S(2)}) async-start(bf16[8,32,128]{2,1,0:T(8,128)(2,1)} %bitcast.18), calls=%async_computation | async-start | bytes 131072 | tf_op jit(solution)/shard_map/all_to_all | solution.py:713
  7.7 0.0 copy-done
  7.7 0.0 copy-start.1
  7.7 0.0 copy-start.2
  7.7 0.0 copy-start.5
  7.8 2.6 %project_family.1 = (f32[512,256]{1,0:T(8,128)S(1)}, bf16[2048,256]{1,0:T(8,128)(2,1)S(1)}, f32[512,256]{1,0:T(8,128)S(1)}, bf16[2,1024,128]{2,1,0:T(8,128)(2,1)S(1)}) custom-call(bf16[512,256]{1,0:T(8,128)(2,1)S(1)} %bitcast.11, bf16[256,1024]{1,0:T(8,128)(2,1)} %project_hbm.1, bf16[1024,128]{1,0:T(8,128)(2,1)} %covariance_hbm.1), custom_call_target="tpu_custom_call" | custom-call | flops 536870912 | bytes 4194304 | tf_op jit(solution)/shard_map/project_family/pallas_call | solution.py:715
  10.3 2.4 %all-to-all-done.got_ref = bf16[8,32,128]{2,1,0:T(8,128)(2,1)S(1)} async-done(((bf16[8,32,128]{2,1,0:T(8,128)(2,1)}), bf16[8,32,128]{2,1,0:T(8,128)(2,1)S(1)}, u32[]{:S(2)}, u32[]{:S(2)}) %all-to-all-start) | async-done | bytes 65568 | tf_op jit(solution)/shard_map/all_to_all | solution.py:713
  12.7 0.0 copy-done.1
  12.7 0.0 copy-done.2
  12.7 0.0 copy-done.5
  12.7 1.6 %row_attention.1 = (bf16[512,256]{1,0:T(8,128)(2,1)}, bf16[384,128]{1,0:T(8,128)(2,1)S(1)}) custom-call(bf16[512,256]{1,0:T(8,128)(2,1)S(1)} %bitcast.12, bf16[8,32,128]{2,1,0:T(8,128)(2,1)S(1)} %all-to-all-done.got_ref, f32[512,256]{1,0:T(8,128)S(1)} %get-tuple-element.11.logits_ref, bf16[2048,256]{1,0:T(8,128)(2,1)S(1)} %get-tuple-element.12.value_ref, ...), custom_call_target="tpu_custom_call" | custom-call | tf_op jit(solution)/shard_map/row_attention/pallas_call | solution.py:745
  14.4 0.0 copy-start.3
  14.4 0.0 copy-start.4
  14.4 0.0 copy-start.6
  14.4 9.6 %all-gather = bf16[3072,128]{1,0:T(8,128)(2,1)S(1)} all-gather(bf16[384,128]{1,0:T(8,128)(2,1)S(1)} %get-tuple-element.15), channel_id=2, replica_groups=mesh['dap'=8,'dp'=4] {'dap'}, dimensions={0}, use_global_device_ids=true | all-gather | bytes 884736 | tf_op jit(solution)/shard_map/all_gather | solution.py:764
  24.0 0.0 copy-done.3
  24.0 0.0 copy-done.4
  24.0 0.0 copy-done.6
  24.0 3.7 %pair_update.1 = (bf16[128,128]{1,0:T(8,128)(2,1)}, f32[128,128]{1,0:T(8,128)}) custom-call(bf16[8,384,128]{2,1,0:T(8,128)(2,1)S(1)} %bitcast.10, bf16[8,32,128]{2,1,0:T(8,128)(2,1)S(1)} %all-to-all-done.got_ref, bf16[128,128]{1,0:T(8,128)(2,1)S(1)} %bitcast.16, bf16[2,1024,128]{2,1,0:T(8,128)(2,1)S(1)} %get-tuple-element.16.covariance_ref, ...), custom_call_target="tpu_custom_call" | custom-call | tf_op jit(solution)/shard_map/pair_update/pallas_call | solution.py:765
Async XLA Ops:
  0.6 7.1 %copy-start = (bf16[16,32,256]{2,1,0:T(8,128)(2,1)S(1)}, bf16[16,32,256]{2,1,0:T(8,128)(2,1)}, u32[]{:S(2)}) copy-start(bf16[16,32,256]{2,1,0:T(8,128)(2,1)} %param.11) | copy-start | bytes 786436
  2.5 10.2 %all-to-all-start = ((bf16[8,32,128]{2,1,0:T(8,128)(2,1)}), bf16[8,32,128]{2,1,0:T(8,128)(2,1)S(1)}, u32[]{:S(2)}, u32[]{:S(2)}) async-start(bf16[8,32,128]{2,1,0:T(8,128)(2,1)} %bitcast.18), calls=%async_computation | async-start | bytes 131072 | tf_op jit(solution)/shard_map/all_to_all | solution.py:713
  7.7 5.0 %copy-start.1 = (bf16[4,32,128]{2,1,0:T(8,128)(2,1)S(1)}, bf16[4,32,128]{2,1,0:T(8,128)(2,1)}, u32[]{:S(2)}) copy-start(bf16[4,32,128]{2,1,0:T(8,128)(2,1)} %param.12) | copy-start | bytes 98308
  7.7 5.0 %copy-start.2 = (bf16[256,256]{1,0:T(8,128)(2,1)S(1)}, bf16[256,256]{1,0:T(8,128)(2,1)}, u32[]{:S(2)}) copy-start(bf16[256,256]{1,0:T(8,128)(2,1)} %merge_ref.1) | copy-start | bytes 393220
  7.7 5.0 %copy-start.5 = (bf16[256,64]{0,1:T(8,128)(2,1)S(1)}, bf16[256,64]{0,1:T(8,128)(2,1)}, u32[]{:S(2)}) copy-start(bf16[256,64]{0,1:T(8,128)(2,1)} %param.17) | copy-start | bytes 98308
  14.4 9.6 %copy-start.3 = (bf16[4,32,128]{2,1,0:T(8,128)(2,1)S(1)}, bf16[4,32,128]{2,1,0:T(8,128)(2,1)}, u32[]{:S(2)}) copy-start(bf16[4,32,128]{2,1,0:T(8,128)(2,1)} %param.21) | copy-start | bytes 98308
  14.4 9.6 %copy-start.4 = (bf16[128,384]{1,0:T(8,128)(2,1)S(1)}, bf16[128,384]{1,0:T(8,128)(2,1)}, u32[]{:S(2)}) copy-start(bf16[128,384]{1,0:T(8,128)(2,1)} %edges_ref.1) | copy-start | bytes 294916
  14.4 9.6 %copy-start.6 = (bf16[128,128]{1,0:T(8,128)(2,1)S(1)}, bf16[128,128]{1,0:T(8,128)(2,1)}, u32[]{:S(2)}) copy-start(bf16[128,128]{1,0:T(8,128)(2,1)} %cycle_ref.1) | copy-start | bytes 98308

commit v8 on v7

--- a/solution.py
+++ b/solution.py
@@ -265,8 +265,9 @@
             )
     packed = packed.astype(BF16)
     for e in range(peers):
-        send_ref[32 * e : 32 * e + 16, :] = packed
-        send_ref[32 * e + 16 : 32 * e + 32, :] = losses[16 * e : 16 * e + 16]
+        rank = e ^ 1
+        send_ref[32 * rank : 32 * rank + 16, :] = packed
+        send_ref[32 * rank + 16 : 32 * rank + 32, :] = losses[16 * e : 16 * e + 16]
 
 
 def project_kernel(
@@ -350,7 +351,7 @@
     seqs = rows // width
     tiles = depth // 128
     group = 128 // width
-    biases = jnp.concatenate([got_ref[d, :16, :] for d in range(got_ref.shape[0])], 0)
+    biases = jnp.concatenate([got_ref[d ^ 1, :16, :] for d in range(got_ref.shape[0])], 0)
     gated = []
     for t in range(tiles):
         cols = slice(128 * t, 128 * t + 128)
@@ -473,6 +474,7 @@
     tri_s,
 ):
     me = lax.axis_index(axis)
+    rank = me + 1 - 2 * (me % 2)
     n = sides_ref.shape[0]
     every = width * width
     group = 128 // hidden
@@ -533,7 +535,7 @@
                     flat_s[first : first + width, 128 * c : 128 * c + 128] = outer[
                         width * c : width * (c + 1)
                     ]
-    tiles = jnp.concatenate([got_ref[d, :16, :] for d in range(n)], 0)
+    tiles = jnp.concatenate([got_ref[d ^ 1, :16, :] for d in range(n)], 0)
     pick = (iota((width, 128), 0) == iota((width, 128), 1)).astype(F32).astype(BF16)
     masks = dot_nt(pick, tiles)
 
@@ -599,7 +601,7 @@
         )
 
     mid = mid_s[rows, :]
-    losses = jnp.concatenate([got_ref[d, 16:, :] for d in range(n)], 0)
+    losses = jnp.concatenate([got_ref[d ^ 1, 16:, :] for d in range(n)], 0)
     goal = iota((pairs, pairs), 0)
     source = goal % width // own * 16 + goal // width * own + goal % own
     place = (source == iota((pairs, pairs), 1)).astype(F32).astype(BF16)
@@ -649,7 +651,7 @@
                 row = jnp.broadcast_to(tri_s[at : at + 1, :], (8, chans))
                 sums[r] = [old + row * part for old, part in zip(sums[r], parts)]
         acc += [jnp.concatenate(vregs, 0) for vregs in sums]
-    keep = kept(dot_nt(pick, got_ref[me, :16, :]), 2 * own)
+    keep = kept(dot_nt(pick, got_ref[rank, :16, :]), 2 * own)
     gate_own = gating[:pairs]
     grad_gate = loss[:pairs] * update * gate_own * (1.0 - gate_own)
     grad_proj = jnp.concatenate(
@@ -710,7 +712,9 @@
         ],
         name="pack_pairs",
     )(edge, logit_offset_matrix.T, loss, edge_validity)
-    got = lax.all_to_all(packed, "dap", split_axis=0, concat_axis=0, tiled=True)
+    got = lax.all_to_all(
+        packed, "dap", split_axis=0, concat_axis=0, axis_index_groups=[[d ^ 1 for d in range(peers)]], tiled=True
+    )
     got = got.reshape(peers, 32, chans)
     logits, value, gating, covariance = pl.pallas_call(
         functools.partial(project_kernel, width, heads, hidden),
@@ -795,6 +799,7 @@
     own, _, chans = edge.shape
     return (
         own * dap == width
+        and dap % 2 == 0
         and width == 32
         and factor.shape[1] == 64
         and depth == 32 * logit.shape[1]

time: 28 us -> 27.7 us (0.989)
  waiting for transfers between devices: 2.41 us -> 1.89 us
    all_to_all x1, waiting for transfers between devices: 2.41 us -> 1.89 us  [body_resident(): lax.all_to_all(packed, 'dap', split_axis=0, concat_axis=0, axis_index_gro...]
where the time goes in v8:
time: 27.7 us; the launch traced here: 27.5 us
  Pallas kernels  9.77 us (35%)
  blocking collectives  9.77 us (35%)
  starting transfers between devices  5.29 us (19%)
  waiting for transfers between devices  1.89 us (7%)
  between operations  0.71 us (3%)
    all_gather x1, blocking collectives, body_resident(): gathered = lax.all_gather(send, 'dap', axis=0, tiled=False)  9.77 us
    all_to_all x1, starting transfers between devices, body_resident(): lax.all_to_all(packed, 'dap', split_axis=0, concat_axis=0, axis_index_gro...  5.29 us
    pallas_call x1, Pallas kernels, body_resident(): pl.pallas_call(functools.partial(pair_kernel, 'dap', width, own, hidden,...  3.72 us
    pallas_call x1, Pallas kernels, body_resident(): pl.pallas_call(functools.partial(project_kernel, width, heads, hidden), o...  2.57 us
    all_to_all x1, waiting for transfers between devices, body_resident(): lax.all_to_all(packed, 'dap', split_axis=0, concat_axis=0, axis_index_gro...  1.89 us
    pallas_call x1, Pallas kernels, body_resident(): pl.pallas_call(functools.partial(pack_kernel, width), out_shape=jax.Shape...  1.88 us
    pallas_call x1, Pallas kernels, body_resident(): pl.pallas_call(functools.partial(attention_kernel, width, own), out_shape...  1.6 us
  transfers between devices with their start and end apart: 1, of which 1 were waited for; matrix products, arithmetic and copies ran while one was open for 0% of the time, Pallas kernels for 9%

profile of v8, /device:TPU:0, one launch (start us, length us, event | category | flops | bytes accessed | tf_op | source)
XLA Modules:
  0.0 27.5 jit_solution(13232106143017720167)
XLA Ops:
  0.6 0.0 copy-start
  0.6 1.9 %pack_pairs.1 = bf16[256,128]{1,0:T(8,128)(2,1)} custom-call(bf16[128,128]{1,0:T(8,128)(2,1)} %bitcast.13, bf16[8,128]{1,0:T(8,128)(2,1)} %bitcast.19, bf16[128,128]{1,0:T(8,128)(2,1)} %bitcast.15, s32[4,32]{1,0:T(4,128)} %mask_ref.1), custom_call_target="tpu_custom_call" | custom-call | tf_op jit(solution)/shard_map/pack_pairs/pallas_call | solution.py:700
  2.5 5.3 %all-to-all-start = ((bf16[8,32,128]{2,1,0:T(8,128)(2,1)}), bf16[8,32,128]{2,1,0:T(8,128)(2,1)S(1)}, u32[]{:S(2)}, u32[]{:S(2)}) async-start(bf16[8,32,128]{2,1,0:T(8,128)(2,1)} %bitcast.18), calls=%async_computation | async-start | bytes 131072 | tf_op jit(solution)/shard_map/all_to_all | solution.py:715
  7.8 0.0 copy-done
  7.8 0.0 copy-start.1
  7.8 0.0 copy-start.2
  7.8 0.0 copy-start.5
  7.8 2.6 %project_family.1 = (f32[512,256]{1,0:T(8,128)S(1)}, bf16[2048,256]{1,0:T(8,128)(2,1)S(1)}, f32[512,256]{1,0:T(8,128)S(1)}, bf16[2,1024,128]{2,1,0:T(8,128)(2,1)S(1)}) custom-call(bf16[512,256]{1,0:T(8,128)(2,1)S(1)} %bitcast.11, bf16[256,1024]{1,0:T(8,128)(2,1)} %project_hbm.1, bf16[1024,128]{1,0:T(8,128)(2,1)} %covariance_hbm.1), custom_call_target="tpu_custom_call" | custom-call | flops 536870912 | bytes 4194304 | tf_op jit(solution)/shard_map/project_family/pallas_call | solution.py:719
  10.4 1.9 %all-to-all-done.got_ref = bf16[8,32,128]{2,1,0:T(8,128)(2,1)S(1)} async-done(((bf16[8,32,128]{2,1,0:T(8,128)(2,1)}), bf16[8,32,128]{2,1,0:T(8,128)(2,1)S(1)}, u32[]{:S(2)}, u32[]{:S(2)}) %all-to-all-start) | async-done | bytes 65568 | tf_op jit(solution)/shard_map/all_to_all | solution.py:715
  12.3 0.0 copy-done.1
  12.3 0.0 copy-done.2
  12.3 0.0 copy-done.5
  12.3 1.6 %row_attention.1 = (bf16[512,256]{1,0:T(8,128)(2,1)}, bf16[384,128]{1,0:T(8,128)(2,1)S(1)}) custom-call(bf16[512,256]{1,0:T(8,128)(2,1)S(1)} %bitcast.12, bf16[8,32,128]{2,1,0:T(8,128)(2,1)S(1)} %all-to-all-done.got_ref, f32[512,256]{1,0:T(8,128)S(1)} %get-tuple-element.11.logits_ref, bf16[2048,256]{1,0:T(8,128)(2,1)S(1)} %get-tuple-element.12.value_ref, ...), custom_call_target="tpu_custom_call" | custom-call | tf_op jit(solution)/shard_map/row_attention/pallas_call | solution.py:749
  13.9 0.0 copy-start.3
  13.9 0.0 copy-start.4
  14.0 0.0 copy-start.6
  14.0 9.8 %all-gather = bf16[3072,128]{1,0:T(8,128)(2,1)S(1)} all-gather(bf16[384,128]{1,0:T(8,128)(2,1)S(1)} %get-tuple-element.15), channel_id=2, replica_groups=mesh['dap'=8,'dp'=4] {'dap'}, dimensions={0}, use_global_device_ids=true | all-gather | bytes 884736 | tf_op jit(solution)/shard_map/all_gather | solution.py:768
  23.7 0.0 copy-done.3
  23.7 0.0 copy-done.4
  23.7 0.0 copy-done.6
  23.7 3.7 %pair_update.1 = (bf16[128,128]{1,0:T(8,128)(2,1)}, f32[128,128]{1,0:T(8,128)}) custom-call(bf16[8,384,128]{2,1,0:T(8,128)(2,1)S(1)} %bitcast.10, bf16[8,32,128]{2,1,0:T(8,128)(2,1)S(1)} %all-to-all-done.got_ref, bf16[128,128]{1,0:T(8,128)(2,1)S(1)} %bitcast.16, bf16[2,1024,128]{2,1,0:T(8,128)(2,1)S(1)} %get-tuple-element.16.covariance_ref, ...), custom_call_target="tpu_custom_call" | custom-call | tf_op jit(solution)/shard_map/pair_update/pallas_call | solution.py:769
Async XLA Ops:
  0.6 7.2 %copy-start = (bf16[16,32,256]{2,1,0:T(8,128)(2,1)S(1)}, bf16[16,32,256]{2,1,0:T(8,128)(2,1)}, u32[]{:S(2)}) copy-start(bf16[16,32,256]{2,1,0:T(8,128)(2,1)} %param.11) | copy-start | bytes 786436
  2.5 9.8 %all-to-all-start = ((bf16[8,32,128]{2,1,0:T(8,128)(2,1)}), bf16[8,32,128]{2,1,0:T(8,128)(2,1)S(1)}, u32[]{:S(2)}, u32[]{:S(2)}) async-start(bf16[8,32,128]{2,1,0:T(8,128)(2,1)} %bitcast.18), calls=%async_computation | async-start | bytes 131072 | tf_op jit(solution)/shard_map/all_to_all | solution.py:715
  7.8 4.5 %copy-start.1 = (bf16[4,32,128]{2,1,0:T(8,128)(2,1)S(1)}, bf16[4,32,128]{2,1,0:T(8,128)(2,1)}, u32[]{:S(2)}) copy-start(bf16[4,32,128]{2,1,0:T(8,128)(2,1)} %param.12) | copy-start | bytes 98308
  7.8 4.5 %copy-start.2 = (bf16[256,256]{1,0:T(8,128)(2,1)S(1)}, bf16[256,256]{1,0:T(8,128)(2,1)}, u32[]{:S(2)}) copy-start(bf16[256,256]{1,0:T(8,128)(2,1)} %merge_ref.1) | copy-start | bytes 393220
  7.8 4.5 %copy-start.5 = (bf16[256,64]{0,1:T(8,128)(2,1)S(1)}, bf16[256,64]{0,1:T(8,128)(2,1)}, u32[]{:S(2)}) copy-start(bf16[256,64]{0,1:T(8,128)(2,1)} %param.17) | copy-start | bytes 98308
  13.9 9.8 %copy-start.3 = (bf16[4,32,128]{2,1,0:T(8,128)(2,1)S(1)}, bf16[4,32,128]{2,1,0:T(8,128)(2,1)}, u32[]{:S(2)}) copy-start(bf16[4,32,128]{2,1,0:T(8,128)(2,1)} %param.21) | copy-start | bytes 98308
  13.9 9.8 %copy-start.4 = (bf16[128,384]{1,0:T(8,128)(2,1)S(1)}, bf16[128,384]{1,0:T(8,128)(2,1)}, u32[]{:S(2)}) copy-start(bf16[128,384]{1,0:T(8,128)(2,1)} %edges_ref.1) | copy-start | bytes 294916
  14.0 9.8 %copy-start.6 = (bf16[128,128]{1,0:T(8,128)(2,1)S(1)}, bf16[128,128]{1,0:T(8,128)(2,1)}, u32[]{:S(2)}) copy-start(bf16[128,128]{1,0:T(8,128)(2,1)} %cycle_ref.1) | copy-start | bytes 98308

commit v9 on v8

--- a/solution.py
+++ b/solution.py
@@ -274,13 +274,14 @@
     width,
     heads,
     hidden,
-    family_ref,
+    family_hbm,
     project_hbm,
     covariance_hbm,
     logits_ref,
     value_ref,
     gating_ref,
     cov_ref,
+    family_ref,
     project_ref,
     covariance_ref,
     sems,
@@ -291,6 +292,7 @@
     cov_s,
 ):
     copies = [
+        pltpu.make_async_copy(family_hbm, family_ref, sems.at[2]),
         pltpu.make_async_copy(project_hbm, project_ref, sems.at[0]),
         pltpu.make_async_copy(covariance_hbm, covariance_ref, sems.at[1]),
     ]
@@ -299,8 +301,9 @@
     rows, depth = family_ref.shape
     seqs = rows // width
     group = 128 // width
+    copies[0].wait()
     normed = standardize_features(family_ref[...].astype(F32)).astype(BF16)
-    copies[0].wait()
+    copies[1].wait()
     query_s[...] = dot(normed, project_ref[:, :depth]).astype(BF16)
     key_s[...] = dot(normed, project_ref[:, depth : 2 * depth]).astype(BF16)
     value_s[...] = dot(normed, project_ref[:, 2 * depth : 3 * depth]).astype(BF16)
@@ -318,7 +321,7 @@
         for k in range(rows // 128):
             span = slice(128 * k, 128 * (k + 1))
             logits_ref[span, cols] = logits_s[span, :].T
-    copies[1].wait()
+    copies[2].wait()
     cov_s[...] = covariance_ref[...].astype(F32)
     for b in range(hidden):
         rows_b = cov_s[pl.ds(b, hidden, stride=hidden), :].astype(BF16)
@@ -338,14 +341,12 @@
     merge_ref,
     factor_ref,
     edge_ref,
-    family_out_ref,
+    after_ref,
     send_ref,
-    after_s,
     weight_s,
     row_s,
     turn_s,
     line_s,
-    sem,
 ):
     rows, depth = family_ref.shape
     seqs = rows // width
@@ -380,9 +381,7 @@
     after = (
         family_ref[...].astype(F32) + dot(jnp.concatenate(gated, 1), merge_ref[...])
     ).astype(BF16)
-    after_s[...] = after
-    leave = pltpu.make_async_copy(after_s, family_out_ref, sem)
-    leave.start()
+    after_ref[...] = after
     ready = standardize_features(after.astype(F32)).astype(BF16)
     hidden = factor_ref.shape[0] // 2
     groups = width // group
@@ -413,7 +412,6 @@
             pl.ds(g, seqs, stride=chunks), :
         ].astype(BF16)
     send_ref[2 * base :, :] = edge_ref[...]
-    leave.wait()
 
 
 def block_transpose(blocks, step):
@@ -459,11 +457,14 @@
     sides_ref,
     got_ref,
     own_loss_ref,
+    after_ref,
     covariance_ref,
     edges_ref,
     cycle_ref,
+    family_out_ref,
     out_ref,
     grad_ref,
+    sem,
     right_s,
     flat_s,
     mid_s,
@@ -473,6 +474,8 @@
     b_s,
     tri_s,
 ):
+    leave = pltpu.make_async_copy(after_ref, family_out_ref, sem)
+    leave.start()
     me = lax.axis_index(axis)
     rank = me + 1 - 2 * (me % 2)
     n = sides_ref.shape[0]
@@ -609,6 +612,7 @@
     gating = jax.nn.sigmoid(
         dot(rows_and_columns(unit_s).astype(BF16), edges_ref[:, 2 * chans :])
     )
+    leave.wait()
     tri = []
     for fixed, moving in ((a_s, b_s), (b_s, a_s)):
         held = fixed[rows, :]
@@ -724,12 +728,13 @@
             jax.ShapeDtypeStruct((seqs * width, depth), F32),
             jax.ShapeDtypeStruct((2, hidden * hidden, chans), BF16),
         ),
-        in_specs=[vmem, hbm, hbm],
+        in_specs=[hbm, hbm, hbm],
         out_specs=(vmem,) * 4,
         scratch_shapes=[
+            pltpu.VMEM((seqs * width, depth), BF16),
             pltpu.VMEM(query_key_value_gate_matrix.shape, BF16),
             pltpu.VMEM(covariance_merge_matrix.shape, BF16),
-            pltpu.SemaphoreType.DMA((2,)),
+            pltpu.SemaphoreType.DMA((3,)),
         ]
         + [pltpu.VMEM((seqs * width, depth), BF16)] * 3
         + [pltpu.VMEM((seqs * width, 128), F32)]
@@ -742,39 +747,39 @@
         ),
         name="project_family",
     )(
-        family,
+        pltpu.with_memory_space_constraint(family, pltpu.HBM),
         pltpu.with_memory_space_constraint(query_key_value_gate_matrix, pltpu.HBM),
         pltpu.with_memory_space_constraint(covariance_merge_matrix, pltpu.HBM),
     )
-    family_out, send = pl.pallas_call(
+    after, send = pl.pallas_call(
         functools.partial(attention_kernel, width, own),
         out_shape=(
             jax.ShapeDtypeStruct((seqs * width, depth), BF16),
             jax.ShapeDtypeStruct((sided + pairs, 128), BF16),
         ),
         in_specs=[vmem] * 8,
-        out_specs=(hbm, vmem),
+        out_specs=(vmem, vmem),
         scratch_shapes=[
-            pltpu.VMEM((seqs * width, depth), BF16),
             pltpu.VMEM((seqs * width, depth), BF16),
             pltpu.VMEM((seqs * width, 128), F32),
             pltpu.VMEM((seqs * width * hidden // 128, 128), F32),
             pltpu.VMEM((seqs * width * hidden // 128, 128), F32),
-            pltpu.SemaphoreType.DMA(()),
         ],
         compiler_params=pltpu.CompilerParams(vmem_limit_bytes=16 << 20),
         name="row_attention",
     )(family, got, logits, value, gating, heads_merge_matrix, factor, edge)
     gathered = lax.all_gather(send, "dap", axis=0, tiled=False)
-    pair_out, pair_grad = pl.pallas_call(
+    family_out, pair_out, pair_grad = pl.pallas_call(
         functools.partial(pair_kernel, "dap", width, own, hidden, seqs),
         out_shape=(
+            jax.ShapeDtypeStruct((seqs * width, depth), BF16),
             jax.ShapeDtypeStruct((pairs, chans), BF16),
             jax.ShapeDtypeStruct((pairs, chans), F32),
         ),
-        in_specs=[vmem] * 6,
-        out_specs=(vmem, vmem),
+        in_specs=[vmem] * 7,
+        out_specs=(hbm, vmem, vmem),
         scratch_shapes=[
+            pltpu.SemaphoreType.DMA(()),
             pltpu.VMEM((width * hidden * hidden // 128, 128 // hidden * 128), BF16),
             pltpu.VMEM((every, hidden * hidden), BF16),
             pltpu.VMEM((every, chans), F32),
@@ -786,7 +791,7 @@
         ],
         compiler_params=pltpu.CompilerParams(vmem_limit_bytes=16 << 20),
         name="pair_update",
-    )(gathered, got, loss, covariance, edges_gate_factor_matrix, cycle_merge_matrix)
+    )(gathered, got, loss, after, covariance, edges_gate_factor_matrix, cycle_merge_matrix)
     return (
         family_out.reshape(seqs, width, depth),
         pair_out.reshape(own, width, chans),

time: 27.7 us -> 27.7 us (level)
  transfers between devices with their start and end apart: 1 -> 1, of which waited for: 1 -> 1; matrix products, arithmetic and copies ran while one was open for 0% -> 0% of each run, Pallas kernels for 9% -> 10%
where the time goes in v9:
time: 27.7 us; the launch traced here: 27.4 us
  Pallas kernels  9.83 us (35%)
  blocking collectives  9.77 us (35%)
  starting transfers between devices  5.29 us (19%)
  waiting for transfers between devices  1.76 us (6%)
  between operations  0.71 us (3%)
    all_gather x1, blocking collectives, body_resident(): gathered = lax.all_gather(send, 'dap', axis=0, tiled=False)  9.77 us
    all_to_all x1, starting transfers between devices, body_resident(): lax.all_to_all(packed, 'dap', split_axis=0, concat_axis=0, axis_index_gro...  5.29 us
    pallas_call x1, Pallas kernels, body_resident(): pl.pallas_call(functools.partial(pair_kernel, 'dap', width, own, hidden,...  3.8 us
    pallas_call x1, Pallas kernels, body_resident(): pl.pallas_call(functools.partial(project_kernel, width, heads, hidden), o...  2.7 us
    pallas_call x1, Pallas kernels, body_resident(): pl.pallas_call(functools.partial(pack_kernel, width), out_shape=jax.Shape...  1.84 us
    all_to_all x1, waiting for transfers between devices, body_resident(): lax.all_to_all(packed, 'dap', split_axis=0, concat_axis=0, axis_index_gro...  1.76 us
    pallas_call x1, Pallas kernels, body_resident(): pl.pallas_call(functools.partial(attention_kernel, width, own), out_shape...  1.48 us
  transfers between devices with their start and end apart: 1, of which 1 were waited for; matrix products, arithmetic and copies ran while one was open for 0% of the time, Pallas kernels for 10%

profile of v9, /device:TPU:0, one launch (start us, length us, event | category | flops | bytes accessed | tf_op | source)
XLA Modules:
  0.0 27.4 jit_solution(3976571460737464117)
XLA Ops:
  0.6 1.8 %pack_pairs.1 = bf16[256,128]{1,0:T(8,128)(2,1)} custom-call(bf16[128,128]{1,0:T(8,128)(2,1)} %bitcast.13, bf16[8,128]{1,0:T(8,128)(2,1)} %bitcast.19, bf16[128,128]{1,0:T(8,128)(2,1)} %bitcast.15, s32[4,32]{1,0:T(4,128)} %mask_ref.1), custom_call_target="tpu_custom_call" | custom-call | tf_op jit(solution)/shard_map/pack_pairs/pallas_call | solution.py:704
  2.5 5.3 %all-to-all-start = ((bf16[8,32,128]{2,1,0:T(8,128)(2,1)}), bf16[8,32,128]{2,1,0:T(8,128)(2,1)S(1)}, u32[]{:S(2)}, u32[]{:S(2)}) async-start(bf16[8,32,128]{2,1,0:T(8,128)(2,1)} %bitcast.18), calls=%async_computation | async-start | bytes 131072 | tf_op jit(solution)/shard_map/all_to_all | solution.py:719
  7.8 0.0 copy-start
  7.8 0.0 copy-start.1
  7.8 0.0 copy-start.3
  7.8 0.0 copy-start.5
  7.8 2.7 %project_family.1 = (f32[512,256]{1,0:T(8,128)S(1)}, bf16[2048,256]{1,0:T(8,128)(2,1)S(1)}, f32[512,256]{1,0:T(8,128)S(1)}, bf16[2,1024,128]{2,1,0:T(8,128)(2,1)S(1)}) custom-call(bf16[512,256]{1,0:T(8,128)(2,1)} %bitcast.11, bf16[256,1024]{1,0:T(8,128)(2,1)} %project_hbm.1, bf16[1024,128]{1,0:T(8,128)(2,1)} %covariance_hbm.1), custom_call_target="tpu_custom_call" | custom-call | flops 536870912 | bytes 4194304 | tf_op jit(solution)/shard_map/project_family/pallas_call | solution.py:723
  10.5 1.8 %all-to-all-done.got_ref = bf16[8,32,128]{2,1,0:T(8,128)(2,1)S(1)} async-done(((bf16[8,32,128]{2,1,0:T(8,128)(2,1)}), bf16[8,32,128]{2,1,0:T(8,128)(2,1)S(1)}, u32[]{:S(2)}, u32[]{:S(2)}) %all-to-all-start) | async-done | bytes 65568 | tf_op jit(solution)/shard_map/all_to_all | solution.py:719
  12.3 0.0 copy-done
  12.3 0.0 copy-done.1
  12.3 0.0 copy-done.3
  12.3 0.0 copy-done.5
  12.3 1.5 %row_attention.1 = (bf16[512,256]{1,0:T(8,128)(2,1)S(1)}, bf16[384,128]{1,0:T(8,128)(2,1)S(1)}) custom-call(bf16[512,256]{1,0:T(8,128)(2,1)S(1)} %bitcast.12, bf16[8,32,128]{2,1,0:T(8,128)(2,1)S(1)} %all-to-all-done.got_ref, f32[512,256]{1,0:T(8,128)S(1)} %get-tuple-element.12.logits_ref, bf16[2048,256]{1,0:T(8,128)(2,1)S(1)} %get-tuple-element.13.value_ref, ...), custom_call_target="tpu_custom_call" | custom-call | tf_op jit(solution)/shard_map/row_attention/pallas_call | solution.py:754
  13.8 0.0 copy-start.2
  13.8 0.0 copy-start.4
  13.8 0.0 copy-start.6
  13.8 9.8 %all-gather = bf16[3072,128]{1,0:T(8,128)(2,1)S(1)} all-gather(bf16[384,128]{1,0:T(8,128)(2,1)S(1)} %get-tuple-element.15), channel_id=2, replica_groups=mesh['dap'=8,'dp'=4] {'dap'}, dimensions={0}, use_global_device_ids=true | all-gather | bytes 884736 | tf_op jit(solution)/shard_map/all_gather | solution.py:771
  23.6 0.0 copy-done.2
  23.6 0.0 copy-done.4
  23.6 0.0 copy-done.6
  23.6 3.8 %pair_update.1 = (bf16[512,256]{1,0:T(8,128)(2,1)}, bf16[128,128]{1,0:T(8,128)(2,1)}, f32[128,128]{1,0:T(8,128)}) custom-call(bf16[8,384,128]{2,1,0:T(8,128)(2,1)S(1)} %bitcast.10, bf16[8,32,128]{2,1,0:T(8,128)(2,1)S(1)} %all-to-all-done.got_ref, bf16[128,128]{1,0:T(8,128)(2,1)S(1)} %bitcast.16, bf16[512,256]{1,0:T(8,128)(2,1)S(1)} %get-tuple-element.16.after_ref, ...), custom_call_target="tpu_custom_call" | custom-call | tf_op jit(solution)/shard_map/pair_update/pallas_call | solution.py:772
Async XLA Ops:
  2.5 9.8 %all-to-all-start = ((bf16[8,32,128]{2,1,0:T(8,128)(2,1)}), bf16[8,32,128]{2,1,0:T(8,128)(2,1)S(1)}, u32[]{:S(2)}, u32[]{:S(2)}) async-start(bf16[8,32,128]{2,1,0:T(8,128)(2,1)} %bitcast.18), calls=%async_computation | async-start | bytes 131072 | tf_op jit(solution)/shard_map/all_to_all | solution.py:719
  7.8 4.5 %copy-start = (bf16[16,32,256]{2,1,0:T(8,128)(2,1)S(1)}, bf16[16,32,256]{2,1,0:T(8,128)(2,1)}, u32[]{:S(2)}) copy-start(bf16[16,32,256]{2,1,0:T(8,128)(2,1)} %param.11) | copy-start | bytes 786436
  7.8 4.5 %copy-start.1 = (bf16[4,32,128]{2,1,0:T(8,128)(2,1)S(1)}, bf16[4,32,128]{2,1,0:T(8,128)(2,1)}, u32[]{:S(2)}) copy-start(bf16[4,32,128]{2,1,0:T(8,128)(2,1)} %param.12) | copy-start | bytes 98308
  7.8 4.5 %copy-start.3 = (bf16[256,256]{1,0:T(8,128)(2,1)S(1)}, bf16[256,256]{1,0:T(8,128)(2,1)}, u32[]{:S(2)}) copy-start(bf16[256,256]{1,0:T(8,128)(2,1)} %merge_ref.1) | copy-start | bytes 393220
  7.8 4.5 %copy-start.5 = (bf16[256,64]{0,1:T(8,128)(2,1)S(1)}, bf16[256,64]{0,1:T(8,128)(2,1)}, u32[]{:S(2)}) copy-start(bf16[256,64]{0,1:T(8,128)(2,1)} %param.17) | copy-start | bytes 98308
  13.8 9.8 %copy-start.2 = (bf16[4,32,128]{2,1,0:T(8,128)(2,1)S(1)}, bf16[4,32,128]{2,1,0:T(8,128)(2,1)}, u32[]{:S(2)}) copy-start(bf16[4,32,128]{2,1,0:T(8,128)(2,1)} %param.21) | copy-start | bytes 98308
  13.8 9.8 %copy-start.4 = (bf16[128,384]{1,0:T(8,128)(2,1)S(1)}, bf16[128,384]{1,0:T(8,128)(2,1)}, u32[]{:S(2)}) copy-start(bf16[128,384]{1,0:T(8,128)(2,1)} %edges_ref.1) | copy-start | bytes 294916
  13.8 9.8 %copy-start.6 = (bf16[128,128]{1,0:T(8,128)(2,1)S(1)}, bf16[128,128]{1,0:T(8,128)(2,1)}, u32[]{:S(2)}) copy-start(bf16[128,128]{1,0:T(8,128)(2,1)} %cycle_ref.1) | copy-start | bytes 98308

commit v10 on v9

--- a/solution.py
+++ b/solution.py
@@ -612,7 +612,6 @@
     gating = jax.nn.sigmoid(
         dot(rows_and_columns(unit_s).astype(BF16), edges_ref[:, 2 * chans :])
     )
-    leave.wait()
     tri = []
     for fixed, moving in ((a_s, b_s), (b_s, a_s)):
         held = fixed[rows, :]
@@ -627,6 +626,7 @@
                     ]
                     parts.append(functools.reduce(jnp.add, prods))
                 tri.append(merge_rows(parts))
+    leave.wait()
     tri = jnp.concatenate(tri, 0)
     center = tri - mean(tri)
     scale_inv = lax.rsqrt(mean(center * center) + EPSILON)

time: 27.7 us -> 27.8 us (level)
  no operation moved by 1% of the time
where the time goes in v10:
time: 27.8 us; the launch traced here: 27.5 us
  Pallas kernels  9.91 us (36%)
  blocking collectives  9.77 us (35%)
  starting transfers between devices  5.29 us (19%)
  waiting for transfers between devices  1.76 us (6%)
  between operations  0.71 us (3%)
    all_gather x1, blocking collectives, body_resident(): gathered = lax.all_gather(send, 'dap', axis=0, tiled=False)  9.77 us
    all_to_all x1, starting transfers between devices, body_resident(): lax.all_to_all(packed, 'dap', split_axis=0, concat_axis=0, axis_index_gro...  5.29 us
    pallas_call x1, Pallas kernels, body_resident(): pl.pallas_call(functools.partial(pair_kernel, 'dap', width, own, hidden,...  3.88 us
    pallas_call x1, Pallas kernels, body_resident(): pl.pallas_call(functools.partial(project_kernel, width, heads, hidden), o...  2.7 us
    pallas_call x1, Pallas kernels, body_resident(): pl.pallas_call(functools.partial(pack_kernel, width), out_shape=jax.Shape...  1.84 us
    all_to_all x1, waiting for transfers between devices, body_resident(): lax.all_to_all(packed, 'dap', split_axis=0, concat_axis=0, axis_index_gro...  1.76 us
    pallas_call x1, Pallas kernels, body_resident(): pl.pallas_call(functools.partial(attention_kernel, width, own), out_shape...  1.48 us
  transfers between devices with their start and end apart: 1, of which 1 were waited for; matrix products, arithmetic and copies ran while one was open for 0% of the time, Pallas kernels for 10%

profile of v10, /device:TPU:0, one launch (start us, length us, event | category | flops | bytes accessed | tf_op | source)
XLA Modules:
  0.0 27.5 jit_solution(7361348496478308088)
XLA Ops:
  0.6 1.8 %pack_pairs.1 = bf16[256,128]{1,0:T(8,128)(2,1)} custom-call(bf16[128,128]{1,0:T(8,128)(2,1)} %bitcast.13, bf16[8,128]{1,0:T(8,128)(2,1)} %bitcast.19, bf16[128,128]{1,0:T(8,128)(2,1)} %bitcast.15, s32[4,32]{1,0:T(4,128)} %mask_ref.1), custom_call_target="tpu_custom_call" | custom-call | tf_op jit(solution)/shard_map/pack_pairs/pallas_call | solution.py:704
  2.5 5.3 %all-to-all-start = ((bf16[8,32,128]{2,1,0:T(8,128)(2,1)}), bf16[8,32,128]{2,1,0:T(8,128)(2,1)S(1)}, u32[]{:S(2)}, u32[]{:S(2)}) async-start(bf16[8,32,128]{2,1,0:T(8,128)(2,1)} %bitcast.18), calls=%async_computation | async-start | bytes 131072 | tf_op jit(solution)/shard_map/all_to_all | solution.py:719
  7.8 0.0 copy-start
  7.8 0.0 copy-start.1
  7.8 0.0 copy-start.3
  7.8 0.0 copy-start.5
  7.8 2.7 %project_family.1 = (f32[512,256]{1,0:T(8,128)S(1)}, bf16[2048,256]{1,0:T(8,128)(2,1)S(1)}, f32[512,256]{1,0:T(8,128)S(1)}, bf16[2,1024,128]{2,1,0:T(8,128)(2,1)S(1)}) custom-call(bf16[512,256]{1,0:T(8,128)(2,1)} %bitcast.11, bf16[256,1024]{1,0:T(8,128)(2,1)} %project_hbm.1, bf16[1024,128]{1,0:T(8,128)(2,1)} %covariance_hbm.1), custom_call_target="tpu_custom_call" | custom-call | flops 536870912 | bytes 4194304 | tf_op jit(solution)/shard_map/project_family/pallas_call | solution.py:723
  10.5 1.8 %all-to-all-done.got_ref = bf16[8,32,128]{2,1,0:T(8,128)(2,1)S(1)} async-done(((bf16[8,32,128]{2,1,0:T(8,128)(2,1)}), bf16[8,32,128]{2,1,0:T(8,128)(2,1)S(1)}, u32[]{:S(2)}, u32[]{:S(2)}) %all-to-all-start) | async-done | bytes 65568 | tf_op jit(solution)/shard_map/all_to_all | solution.py:719
  12.3 0.0 copy-done
  12.3 0.0 copy-done.1
  12.3 0.0 copy-done.3
  12.3 0.0 copy-done.5
  12.3 1.5 %row_attention.1 = (bf16[512,256]{1,0:T(8,128)(2,1)S(1)}, bf16[384,128]{1,0:T(8,128)(2,1)S(1)}) custom-call(bf16[512,256]{1,0:T(8,128)(2,1)S(1)} %bitcast.12, bf16[8,32,128]{2,1,0:T(8,128)(2,1)S(1)} %all-to-all-done.got_ref, f32[512,256]{1,0:T(8,128)S(1)} %get-tuple-element.12.logits_ref, bf16[2048,256]{1,0:T(8,128)(2,1)S(1)} %get-tuple-element.13.value_ref, ...), custom_call_target="tpu_custom_call" | custom-call | tf_op jit(solution)/shard_map/row_attention/pallas_call | solution.py:754
  13.8 0.0 copy-start.2
  13.8 0.0 copy-start.4
  13.8 0.0 copy-start.6
  13.8 9.8 %all-gather = bf16[3072,128]{1,0:T(8,128)(2,1)S(1)} all-gather(bf16[384,128]{1,0:T(8,128)(2,1)S(1)} %get-tuple-element.15), channel_id=2, replica_groups=mesh['dap'=8,'dp'=4] {'dap'}, dimensions={0}, use_global_device_ids=true | all-gather | bytes 884736 | tf_op jit(solution)/shard_map/all_gather | solution.py:771
  23.6 0.0 copy-done.2
  23.6 0.0 copy-done.4
  23.6 0.0 copy-done.6
  23.6 3.9 %pair_update.1 = (bf16[512,256]{1,0:T(8,128)(2,1)}, bf16[128,128]{1,0:T(8,128)(2,1)}, f32[128,128]{1,0:T(8,128)}) custom-call(bf16[8,384,128]{2,1,0:T(8,128)(2,1)S(1)} %bitcast.10, bf16[8,32,128]{2,1,0:T(8,128)(2,1)S(1)} %all-to-all-done.got_ref, bf16[128,128]{1,0:T(8,128)(2,1)S(1)} %bitcast.16, bf16[512,256]{1,0:T(8,128)(2,1)S(1)} %get-tuple-element.16.after_ref, ...), custom_call_target="tpu_custom_call" | custom-call | tf_op jit(solution)/shard_map/pair_update/pallas_call | solution.py:772
Async XLA Ops:
  2.5 9.8 %all-to-all-start = ((bf16[8,32,128]{2,1,0:T(8,128)(2,1)}), bf16[8,32,128]{2,1,0:T(8,128)(2,1)S(1)}, u32[]{:S(2)}, u32[]{:S(2)}) async-start(bf16[8,32,128]{2,1,0:T(8,128)(2,1)} %bitcast.18), calls=%async_computation | async-start | bytes 131072 | tf_op jit(solution)/shard_map/all_to_all | solution.py:719
  7.8 4.5 %copy-start = (bf16[16,32,256]{2,1,0:T(8,128)(2,1)S(1)}, bf16[16,32,256]{2,1,0:T(8,128)(2,1)}, u32[]{:S(2)}) copy-start(bf16[16,32,256]{2,1,0:T(8,128)(2,1)} %param.11) | copy-start | bytes 786436
  7.8 4.5 %copy-start.1 = (bf16[4,32,128]{2,1,0:T(8,128)(2,1)S(1)}, bf16[4,32,128]{2,1,0:T(8,128)(2,1)}, u32[]{:S(2)}) copy-start(bf16[4,32,128]{2,1,0:T(8,128)(2,1)} %param.12) | copy-start | bytes 98308
  7.8 4.5 %copy-start.3 = (bf16[256,256]{1,0:T(8,128)(2,1)S(1)}, bf16[256,256]{1,0:T(8,128)(2,1)}, u32[]{:S(2)}) copy-start(bf16[256,256]{1,0:T(8,128)(2,1)} %merge_ref.1) | copy-start | bytes 393220
  7.8 4.5 %copy-start.5 = (bf16[256,64]{0,1:T(8,128)(2,1)S(1)}, bf16[256,64]{0,1:T(8,128)(2,1)}, u32[]{:S(2)}) copy-start(bf16[256,64]{0,1:T(8,128)(2,1)} %param.17) | copy-start | bytes 98308
  13.8 9.8 %copy-start.2 = (bf16[4,32,128]{2,1,0:T(8,128)(2,1)S(1)}, bf16[4,32,128]{2,1,0:T(8,128)(2,1)}, u32[]{:S(2)}) copy-start(bf16[4,32,128]{2,1,0:T(8,128)(2,1)} %param.21) | copy-start | bytes 98308
  13.8 9.8 %copy-start.4 = (bf16[128,384]{1,0:T(8,128)(2,1)S(1)}, bf16[128,384]{1,0:T(8,128)(2,1)}, u32[]{:S(2)}) copy-start(bf16[128,384]{1,0:T(8,128)(2,1)} %edges_ref.1) | copy-start | bytes 294916
  13.8 9.8 %copy-start.6 = (bf16[128,128]{1,0:T(8,128)(2,1)S(1)}, bf16[128,128]{1,0:T(8,128)(2,1)}, u32[]{:S(2)}) copy-start(bf16[128,128]{1,0:T(8,128)(2,1)} %cycle_ref.1) | copy-start | bytes 98308

commit v11 on v8

--- a/solution.py
+++ b/solution.py
@@ -274,13 +274,14 @@
     width,
     heads,
     hidden,
-    family_ref,
+    family_hbm,
     project_hbm,
     covariance_hbm,
     logits_ref,
     value_ref,
     gating_ref,
     cov_ref,
+    family_ref,
     project_ref,
     covariance_ref,
     sems,
@@ -291,6 +292,7 @@
     cov_s,
 ):
     copies = [
+        pltpu.make_async_copy(family_hbm, family_ref, sems.at[2]),
         pltpu.make_async_copy(project_hbm, project_ref, sems.at[0]),
         pltpu.make_async_copy(covariance_hbm, covariance_ref, sems.at[1]),
     ]
@@ -299,8 +301,9 @@
     rows, depth = family_ref.shape
     seqs = rows // width
     group = 128 // width
+    copies[0].wait()
     normed = standardize_features(family_ref[...].astype(F32)).astype(BF16)
-    copies[0].wait()
+    copies[1].wait()
     query_s[...] = dot(normed, project_ref[:, :depth]).astype(BF16)
     key_s[...] = dot(normed, project_ref[:, depth : 2 * depth]).astype(BF16)
     value_s[...] = dot(normed, project_ref[:, 2 * depth : 3 * depth]).astype(BF16)
@@ -318,7 +321,7 @@
         for k in range(rows // 128):
             span = slice(128 * k, 128 * (k + 1))
             logits_ref[span, cols] = logits_s[span, :].T
-    copies[1].wait()
+    copies[2].wait()
     cov_s[...] = covariance_ref[...].astype(F32)
     for b in range(hidden):
         rows_b = cov_s[pl.ds(b, hidden, stride=hidden), :].astype(BF16)
@@ -724,12 +727,13 @@
             jax.ShapeDtypeStruct((seqs * width, depth), F32),
             jax.ShapeDtypeStruct((2, hidden * hidden, chans), BF16),
         ),
-        in_specs=[vmem, hbm, hbm],
+        in_specs=[hbm, hbm, hbm],
         out_specs=(vmem,) * 4,
         scratch_shapes=[
+            pltpu.VMEM((seqs * width, depth), BF16),
             pltpu.VMEM(query_key_value_gate_matrix.shape, BF16),
             pltpu.VMEM(covariance_merge_matrix.shape, BF16),
-            pltpu.SemaphoreType.DMA((2,)),
+            pltpu.SemaphoreType.DMA((3,)),
         ]
         + [pltpu.VMEM((seqs * width, depth), BF16)] * 3
         + [pltpu.VMEM((seqs * width, 128), F32)]
@@ -742,7 +746,7 @@
         ),
         name="project_family",
     )(
-        family,
+        pltpu.with_memory_space_constraint(family, pltpu.HBM),
         pltpu.with_memory_space_constraint(query_key_value_gate_matrix, pltpu.HBM),
         pltpu.with_memory_space_constraint(covariance_merge_matrix, pltpu.HBM),
     )

time: 27.7 us -> 27.7 us (level)
  transfers between devices with their start and end apart: 1 -> 1, of which waited for: 1 -> 1; matrix products, arithmetic and copies ran while one was open for 0% -> 0% of each run, Pallas kernels for 9% -> 10%
where the time goes in v11:
time: 27.7 us; the launch traced here: 27.4 us
  Pallas kernels  9.87 us (36%)
  blocking collectives  9.77 us (35%)
  starting transfers between devices  5.29 us (19%)
  waiting for transfers between devices  1.76 us (6%)
  between operations  0.71 us (3%)
    all_gather x1, blocking collectives, body_resident(): gathered = lax.all_gather(send, 'dap', axis=0, tiled=False)  9.77 us
    all_to_all x1, starting transfers between devices, body_resident(): lax.all_to_all(packed, 'dap', split_axis=0, concat_axis=0, axis_index_gro...  5.29 us
    pallas_call x1, Pallas kernels, body_resident(): pl.pallas_call(functools.partial(pair_kernel, 'dap', width, own, hidden,...  3.72 us
    pallas_call x1, Pallas kernels, body_resident(): pl.pallas_call(functools.partial(project_kernel, width, heads, hidden), o...  2.7 us
    pallas_call x1, Pallas kernels, body_resident(): pl.pallas_call(functools.partial(pack_kernel, width), out_shape=jax.Shape...  1.84 us
    all_to_all x1, waiting for transfers between devices, body_resident(): lax.all_to_all(packed, 'dap', split_axis=0, concat_axis=0, axis_index_gro...  1.76 us
    pallas_call x1, Pallas kernels, body_resident(): pl.pallas_call(functools.partial(attention_kernel, width, own), out_shape...  1.6 us
  transfers between devices with their start and end apart: 1, of which 1 were waited for; matrix products, arithmetic and copies ran while one was open for 0% of the time, Pallas kernels for 10%

profile of v11, /device:TPU:0, one launch (start us, length us, event | category | flops | bytes accessed | tf_op | source)
XLA Modules:
  0.0 27.4 jit_solution(5911956297602182105)
XLA Ops:
  0.6 1.8 %pack_pairs.1 = bf16[256,128]{1,0:T(8,128)(2,1)} custom-call(bf16[128,128]{1,0:T(8,128)(2,1)} %bitcast.13, bf16[8,128]{1,0:T(8,128)(2,1)} %bitcast.19, bf16[128,128]{1,0:T(8,128)(2,1)} %bitcast.15, s32[4,32]{1,0:T(4,128)} %mask_ref.1), custom_call_target="tpu_custom_call" | custom-call | tf_op jit(solution)/shard_map/pack_pairs/pallas_call | solution.py:703
  2.5 5.3 %all-to-all-start = ((bf16[8,32,128]{2,1,0:T(8,128)(2,1)}), bf16[8,32,128]{2,1,0:T(8,128)(2,1)S(1)}, u32[]{:S(2)}, u32[]{:S(2)}) async-start(bf16[8,32,128]{2,1,0:T(8,128)(2,1)} %bitcast.18), calls=%async_computation | async-start | bytes 131072 | tf_op jit(solution)/shard_map/all_to_all | solution.py:718
  7.8 0.0 copy-start
  7.8 0.0 copy-start.1
  7.8 0.0 copy-start.2
  7.8 0.0 copy-start.5
  7.8 2.7 %project_family.1 = (f32[512,256]{1,0:T(8,128)S(1)}, bf16[2048,256]{1,0:T(8,128)(2,1)S(1)}, f32[512,256]{1,0:T(8,128)S(1)}, bf16[2,1024,128]{2,1,0:T(8,128)(2,1)S(1)}) custom-call(bf16[512,256]{1,0:T(8,128)(2,1)} %bitcast.11, bf16[256,1024]{1,0:T(8,128)(2,1)} %project_hbm.1, bf16[1024,128]{1,0:T(8,128)(2,1)} %covariance_hbm.1), custom_call_target="tpu_custom_call" | custom-call | flops 536870912 | bytes 4194304 | tf_op jit(solution)/shard_map/project_family/pallas_call | solution.py:722
  10.5 1.8 %all-to-all-done.got_ref = bf16[8,32,128]{2,1,0:T(8,128)(2,1)S(1)} async-done(((bf16[8,32,128]{2,1,0:T(8,128)(2,1)}), bf16[8,32,128]{2,1,0:T(8,128)(2,1)S(1)}, u32[]{:S(2)}, u32[]{:S(2)}) %all-to-all-start) | async-done | bytes 65568 | tf_op jit(solution)/shard_map/all_to_all | solution.py:718
  12.3 0.0 copy-done
  12.3 0.0 copy-done.1
  12.3 0.0 copy-done.2
  12.3 0.0 copy-done.5
  12.3 1.6 %row_attention.1 = (bf16[512,256]{1,0:T(8,128)(2,1)}, bf16[384,128]{1,0:T(8,128)(2,1)S(1)}) custom-call(bf16[512,256]{1,0:T(8,128)(2,1)S(1)} %bitcast.12, bf16[8,32,128]{2,1,0:T(8,128)(2,1)S(1)} %all-to-all-done.got_ref, f32[512,256]{1,0:T(8,128)S(1)} %get-tuple-element.11.logits_ref, bf16[2048,256]{1,0:T(8,128)(2,1)S(1)} %get-tuple-element.12.value_ref, ...), custom_call_target="tpu_custom_call" | custom-call | tf_op jit(solution)/shard_map/row_attention/pallas_call | solution.py:753
  13.9 0.0 copy-start.3
  13.9 0.0 copy-start.4
  13.9 0.0 copy-start.6
  13.9 9.8 %all-gather = bf16[3072,128]{1,0:T(8,128)(2,1)S(1)} all-gather(bf16[384,128]{1,0:T(8,128)(2,1)S(1)} %get-tuple-element.15), channel_id=2, replica_groups=mesh['dap'=8,'dp'=4] {'dap'}, dimensions={0}, use_global_device_ids=true | all-gather | bytes 884736 | tf_op jit(solution)/shard_map/all_gather | solution.py:772
  23.7 0.0 copy-done.3
  23.7 0.0 copy-done.4
  23.7 0.0 copy-done.6
  23.7 3.7 %pair_update.1 = (bf16[128,128]{1,0:T(8,128)(2,1)}, f32[128,128]{1,0:T(8,128)}) custom-call(bf16[8,384,128]{2,1,0:T(8,128)(2,1)S(1)} %bitcast.10, bf16[8,32,128]{2,1,0:T(8,128)(2,1)S(1)} %all-to-all-done.got_ref, bf16[128,128]{1,0:T(8,128)(2,1)S(1)} %bitcast.16, bf16[2,1024,128]{2,1,0:T(8,128)(2,1)S(1)} %get-tuple-element.16.covariance_ref, ...), custom_call_target="tpu_custom_call" | custom-call | tf_op jit(solution)/shard_map/pair_update/pallas_call | solution.py:773
Async XLA Ops:
  2.5 9.8 %all-to-all-start = ((bf16[8,32,128]{2,1,0:T(8,128)(2,1)}), bf16[8,32,128]{2,1,0:T(8,128)(2,1)S(1)}, u32[]{:S(2)}, u32[]{:S(2)}) async-start(bf16[8,32,128]{2,1,0:T(8,128)(2,1)} %bitcast.18), calls=%async_computation | async-start | bytes 131072 | tf_op jit(solution)/shard_map/all_to_all | solution.py:718
  7.8 4.5 %copy-start = (bf16[16,32,256]{2,1,0:T(8,128)(2,1)S(1)}, bf16[16,32,256]{2,1,0:T(8,128)(2,1)}, u32[]{:S(2)}) copy-start(bf16[16,32,256]{2,1,0:T(8,128)(2,1)} %param.11) | copy-start | bytes 786436
  7.8 4.5 %copy-start.1 = (bf16[4,32,128]{2,1,0:T(8,128)(2,1)S(1)}, bf16[4,32,128]{2,1,0:T(8,128)(2,1)}, u32[]{:S(2)}) copy-start(bf16[4,32,128]{2,1,0:T(8,128)(2,1)} %param.12) | copy-start | bytes 98308
  7.8 4.5 %copy-start.2 = (bf16[256,256]{1,0:T(8,128)(2,1)S(1)}, bf16[256,256]{1,0:T(8,128)(2,1)}, u32[]{:S(2)}) copy-start(bf16[256,256]{1,0:T(8,128)(2,1)} %merge_ref.1) | copy-start | bytes 393220
  7.8 4.5 %copy-start.5 = (bf16[256,64]{0,1:T(8,128)(2,1)S(1)}, bf16[256,64]{0,1:T(8,128)(2,1)}, u32[]{:S(2)}) copy-start(bf16[256,64]{0,1:T(8,128)(2,1)} %param.17) | copy-start | bytes 98308
  13.9 9.8 %copy-start.3 = (bf16[4,32,128]{2,1,0:T(8,128)(2,1)S(1)}, bf16[4,32,128]{2,1,0:T(8,128)(2,1)}, u32[]{:S(2)}) copy-start(bf16[4,32,128]{2,1,0:T(8,128)(2,1)} %param.21) | copy-start | bytes 98308
  13.9 9.8 %copy-start.4 = (bf16[128,384]{1,0:T(8,128)(2,1)S(1)}, bf16[128,384]{1,0:T(8,128)(2,1)}, u32[]{:S(2)}) copy-start(bf16[128,384]{1,0:T(8,128)(2,1)} %edges_ref.1) | copy-start | bytes 294916
  13.9 9.8 %copy-start.6 = (bf16[128,128]{1,0:T(8,128)(2,1)S(1)}, bf16[128,128]{1,0:T(8,128)(2,1)}, u32[]{:S(2)}) copy-start(bf16[128,128]{1,0:T(8,128)(2,1)} %cycle_ref.1) | copy-start | bytes 98308
